TPU v7x, 32 devices: a whole 2x2x4 slice. The times are simulated.
32 devices in a mesh: dp: 8 (over z, x), tensor: 4 (over y, core).
Axes of the slice: x: 2, y: 2, z: 4, core: 2. Of those that a mesh axis runs over, the one named last changes fastest.
Arguments:
- inputs: bfloat16 [2, 8, 1024, 1152], P(None, 'dp', 'tensor'), may hold values from -6 to 6
- lengths: int32 [2, 8], P(None, 'dp'), may hold values from 256 to 1024, as said below
- gain_attn: bfloat16 [1152], P('dp'), may hold values from 0.5 to 1.5
- gain_mlp: bfloat16 [1152], P('dp'), may hold values from 0.5 to 1.5
- w_query: bfloat16 [1152, 1152], P('dp'), may hold values from -0.1875 to 0.1875
- key_weight: bfloat16 [1152, 384], P('dp'), may hold values from -0.1875 to 0.1875
- value_weight: bfloat16 [1152, 384], P('dp'), may hold values from -0.1875 to 0.1875
- w_gate: bfloat16 [1152, 3072], P('dp', 'tensor'), may hold values from -0.1875 to 0.1875
- w_up: bfloat16 [1152, 3072], P('dp', 'tensor'), may hold values from -0.1875 to 0.1875
- w_out: bfloat16 [1152, 1152], P('dp'), may hold values from -0.75 to 0.75
- w_down: bfloat16 [3072, 1152], P('tensor', 'dp'), may hold values from -0.21875 to 0.21875
- cotangent: bfloat16 [2, 8, 1024, 1152], P(None, 'dp', 'tensor'), may hold values from -6 to 6
Outputs:
- out_act: bfloat16 [2, 8, 1024, 1152], P(None, 'dp', 'tensor')
- grad_inputs: bfloat16 [2, 8, 1024, 1152], P(None, 'dp', 'tensor')
- grad_gain_attn: float32 [1152], P('dp')
- grad_gain_mlp: float32 [1152], P('dp')
- grad_w_query: float32 [1152, 1152], P('dp')
- grad_w_key: float32 [1152, 384], P('dp')
- grad_w_value: float32 [1152, 384], P('dp')
- grad_w_gate: float32 [1152, 3072], P('dp', 'tensor')
- grad_w_up: float32 [1152, 3072], P('dp', 'tensor')
- grad_w_out: float32 [1152, 1152], P('dp')
- grad_w_down: float32 [3072, 1152], P('tensor', 'dp')
Inputs may be any that keep to these rules, and one draw needn't show every extreme that they name: `lengths`: each sequence's valid tokens; in every micro-batch one sequence fills all 1024 slots.
All inputs are finite; a program needn't handle non-finite values.
Results may differ from a plain program's by a relative error of at most 0.023.
Values may be sent and summed in bfloat16 or wider, within the bound.
No kernel may reach another device: no remote copies, remote signals or barrier semaphores. Data moves between devices by JAX's collectives and lax.ppermute only.
A program may use at most 192 MiB of HBM per device.

v0:
```python
import jax
import jax.numpy as jnp
from jax import lax
from jax.sharding import PartitionSpec as P

HEAD_SIZE = 64


EPSILON = 1e-05
ROPE_BASE = 10000.0
MASKED = -1e30


def rope_tables(positions, head_dim):
    half_dim = head_dim // 2
    exponent = jnp.arange(half_dim, dtype=jnp.float32) * (2.0 / head_dim)
    frequency = ROPE_BASE ** (-exponent)
    angles = positions[:, None] * frequency[None, :]
    cosine_table = jnp.concatenate([jnp.cos(angles), jnp.cos(angles)], axis=1)
    sine_table = jnp.concatenate([jnp.sin(angles), jnp.sin(angles)], axis=1)
    return (cosine_table, sine_table)


def rotate_half(values):
    half_dim = values.shape[-1] // 2
    return jnp.concatenate([-values[..., half_dim:], values[..., :half_dim]], axis=-1)


def apply_rotary(values, cosine_table, sine_table):
    return values * cosine_table[:, None, :] + rotate_half(values) * sine_table[:, None, :]


def unrope(grads_in, cosine_table, sine_table):
    half_dim = grads_in.shape[-1] // 2
    scaled = grads_in * sine_table[:, None, :]
    turned = jnp.concatenate([scaled[..., half_dim:], -scaled[..., :half_dim]], axis=-1)
    return grads_in * cosine_table[:, None, :] + turned


def contract_rows(left_side, right_side):
    return lax.dot_general(
        left_side, right_side, (((0,), (0,)), ((), ())), preferred_element_type=jnp.float32
    )


def contract_last(left_side, right_side):
    return lax.dot_general(
        left_side, right_side, (((1,), (1,)), ((), ())), preferred_element_type=jnp.float32
    )


def fetch_weights(
    gain_attn, gain_mlp, w_query, key_weight, value_weight, w_gate, w_up, w_out, w_down
):
    return (
        lax.all_gather(gain_attn, "dp", axis=0, tiled=True),
        lax.all_gather(gain_mlp, "dp", axis=0, tiled=True),
        lax.all_gather(w_query, "dp", axis=0, tiled=True),
        lax.all_gather(key_weight, "dp", axis=0, tiled=True),
        lax.all_gather(value_weight, "dp", axis=0, tiled=True),
        lax.all_gather(w_gate, "dp", axis=0, tiled=True),
        lax.all_gather(w_up, "dp", axis=0, tiled=True),
        lax.all_gather(w_out, "dp", axis=0, tiled=True),
        lax.all_gather(w_down, "dp", axis=1, tiled=True),
    )


def project_sum(left_side, right_side):
    return lax.psum_scatter(
        jnp.dot(left_side, right_side, preferred_element_type=jnp.float32).astype(jnp.bfloat16),
        "tensor",
        scatter_dimension=0,
        tiled=True,
    ).astype(jnp.float32)


def back_project_sum(pair_list):
    row_share = pair_list[0][0].shape[0] // lax.axis_size("tensor")
    out_width = pair_list[0][1].shape[0]
    summed = jnp.zeros((lax.axis_size("tensor") * row_share, out_width), jnp.float32)
    for grad_part, weight_part in pair_list:
        summed = summed + contract_last(grad_part, weight_part)
    return lax.psum_scatter(
        summed.astype(jnp.bfloat16), "tensor", scatter_dimension=0, tiled=True
    ).astype(jnp.float32)


def reduce_over_data(grad_list):
    (
        grad_query_w,
        grad_key_w,
        grad_value_w,
        grad_gate_w,
        grad_up_w,
        grad_out_w,
        grad_down_w,
        grad_gain_one,
        grad_gain_two,
    ) = grad_list
    return (
        lax.psum_scatter(grad_query_w, "dp", scatter_dimension=0, tiled=True),
        lax.psum_scatter(grad_key_w, "dp", scatter_dimension=0, tiled=True),
        lax.psum_scatter(grad_value_w, "dp", scatter_dimension=0, tiled=True),
        lax.psum_scatter(grad_gate_w, "dp", scatter_dimension=0, tiled=True),
        lax.psum_scatter(grad_up_w, "dp", scatter_dimension=0, tiled=True),
        lax.psum_scatter(grad_out_w, "dp", scatter_dimension=0, tiled=True),
        lax.psum_scatter(grad_down_w, "dp", scatter_dimension=1, tiled=True),
        lax.psum_scatter(grad_gain_one, "dp", scatter_dimension=0, tiled=True),
        lax.psum_scatter(grad_gain_two, "dp", scatter_dimension=0, tiled=True),
    )


def row_scale_of(values):
    return lax.rsqrt(jnp.mean(values * values, axis=-1, keepdims=True) + EPSILON)


def make_mask(query_pos, position_count, valid_count):
    key_pos = jnp.arange(position_count, dtype=jnp.int32)
    return (key_pos[None, :] <= query_pos[:, None]) & (key_pos[None, :] < valid_count)


def attention_scores(query_rows, keys_all, allowed):
    raw_scores = jnp.einsum(
        "qhgd,shd->hgqs", query_rows, keys_all, preferred_element_type=jnp.float32
    ) * HEAD_SIZE ** (-0.5)
    return jnp.where(allowed, raw_scores, MASKED)


def norm_backward(grad_normed, row_values, row_scale, gain_full):
    gain_grad = jnp.sum(grad_normed * row_values * row_scale, axis=0)
    inner_grad = grad_normed * gain_full
    row_grad = row_scale * inner_grad - row_values * row_scale**3 * jnp.mean(
        inner_grad * row_values, axis=-1, keepdims=True
    )
    return (row_grad, gain_grad)


def forward_pass(rows_in, valid_count, weights, row_start):
    (
        gain_attn,
        gain_mlp,
        full_query,
        full_key,
        full_value,
        full_gate,
        full_up,
        full_out,
        full_down,
    ) = weights
    gain_one = gain_attn.astype(jnp.float32)
    gain_two = gain_mlp.astype(jnp.float32)
    row_count = rows_in.shape[0]
    row_values = rows_in.astype(jnp.float32)
    scale_one = row_scale_of(row_values)
    hidden_one = (row_values * scale_one * gain_one).astype(jnp.bfloat16)
    query_heads = full_query.shape[1] // HEAD_SIZE
    key_heads = full_key.shape[1] // HEAD_SIZE
    group_width = query_heads // key_heads
    query_pos = row_start + jnp.arange(row_count, dtype=jnp.int32)
    cosine_table, sine_table = rope_tables(query_pos.astype(jnp.float32), HEAD_SIZE)
    query_unrotated = jnp.dot(hidden_one, full_query, preferred_element_type=jnp.float32).reshape(
        row_count, query_heads, HEAD_SIZE
    )
    key_unrotated = jnp.dot(hidden_one, full_key, preferred_element_type=jnp.float32).reshape(
        row_count, key_heads, HEAD_SIZE
    )
    values_own = jnp.dot(hidden_one, full_value, preferred_element_type=jnp.float32).astype(
        jnp.bfloat16
    )
    query_rows = (
        apply_rotary(query_unrotated, cosine_table, sine_table)
        .astype(jnp.bfloat16)
        .reshape(row_count, key_heads, group_width, HEAD_SIZE)
    )
    keys_own = (
        apply_rotary(key_unrotated, cosine_table, sine_table)
        .astype(jnp.bfloat16)
        .reshape(row_count, key_heads * HEAD_SIZE)
    )
    keys_flat, values_flat = (
        lax.all_gather(keys_own, "tensor", axis=0, tiled=True),
        lax.all_gather(values_own, "tensor", axis=0, tiled=True),
    )
    position_count = keys_flat.shape[0]
    keys_all = keys_flat.reshape(position_count, key_heads, HEAD_SIZE)
    values_all = values_flat.reshape(position_count, key_heads, HEAD_SIZE)
    allowed = make_mask(query_pos, position_count, valid_count)
    scores = attention_scores(query_rows, keys_all, allowed)
    maxima = jnp.max(scores, axis=-1, keepdims=True)
    log_total = maxima + jnp.log(jnp.sum(jnp.exp(scores - maxima), axis=-1, keepdims=True))
    soft_low = jnp.exp(scores - log_total).astype(jnp.bfloat16)
    attended = jnp.einsum(
        "hgqs,shd->qhgd", soft_low, values_all, preferred_element_type=jnp.float32
    )
    attended = attended.reshape(row_count, query_heads * HEAD_SIZE).astype(jnp.bfloat16)
    middle = row_values + jnp.dot(attended, full_out, preferred_element_type=jnp.float32)
    scale_two = row_scale_of(middle)
    hidden_two = lax.all_gather(
        (middle * scale_two * gain_two).astype(jnp.bfloat16), "tensor", axis=0, tiled=True
    )
    gate_proj = jnp.dot(hidden_two, full_gate, preferred_element_type=jnp.float32)
    up_proj = jnp.dot(hidden_two, full_up, preferred_element_type=jnp.float32)
    activated = (jax.nn.silu(gate_proj) * up_proj).astype(jnp.bfloat16)
    ffn_out = project_sum(activated, full_down)
    valid = (query_pos < valid_count).astype(jnp.float32)[:, None]
    output = (valid * (middle + ffn_out)).astype(jnp.bfloat16)
    kept = (
        row_values,
        scale_one,
        hidden_one,
        query_rows,
        keys_all,
        values_all,
        allowed,
        log_total,
        attended,
        middle,
        scale_two,
        hidden_two,
        gate_proj,
        up_proj,
        activated,
        valid,
        cosine_table,
        sine_table,
    )
    return (output, kept)


def backward_pass(cot_rows, weights, kept):
    (
        gain_attn,
        gain_mlp,
        full_query,
        full_key,
        full_value,
        full_gate,
        full_up,
        full_out,
        full_down,
    ) = weights
    (
        row_values,
        scale_one,
        hidden_one,
        query_rows,
        keys_all,
        values_all,
        allowed,
        log_total,
        attended,
        middle,
        scale_two,
        hidden_two,
        gate_proj,
        up_proj,
        activated,
        valid,
        cosine_table,
        sine_table,
    ) = kept
    gain_one = gain_attn.astype(jnp.float32)
    gain_two = gain_mlp.astype(jnp.float32)
    row_count = row_values.shape[0]
    position_count = keys_all.shape[0]
    query_heads = full_query.shape[1] // HEAD_SIZE
    key_heads = full_key.shape[1] // HEAD_SIZE
    group_width = query_heads // key_heads
    grad_rows = cot_rows.astype(jnp.float32) * valid
    grad_ffn = lax.all_gather(grad_rows.astype(jnp.bfloat16), "tensor", axis=0, tiled=True)
    grad_down_w = contract_rows(activated, grad_ffn)
    grad_act = contract_last(grad_ffn, full_down)
    sigmoid_gate = jax.nn.sigmoid(gate_proj)
    grad_gate = (
        grad_act * up_proj * sigmoid_gate * (1.0 + gate_proj * (1.0 - sigmoid_gate))
    ).astype(jnp.bfloat16)
    grad_up = (grad_act * gate_proj * sigmoid_gate).astype(jnp.bfloat16)
    grad_gate_w = contract_rows(hidden_two, grad_gate)
    grad_up_w = contract_rows(hidden_two, grad_up)
    grad_normed_two = back_project_sum(((grad_gate, full_gate), (grad_up, full_up)))
    row_grad_two, grad_gain_two = norm_backward(grad_normed_two, middle, scale_two, gain_two)
    grad_middle = grad_rows + row_grad_two
    grad_branch = grad_middle.astype(jnp.bfloat16)
    grad_out_w = contract_rows(attended, grad_branch)
    grad_att = (
        contract_last(grad_branch, full_out)
        .astype(jnp.bfloat16)
        .reshape(row_count, key_heads, group_width, HEAD_SIZE)
    )
    soft_float = jnp.exp(attention_scores(query_rows, keys_all, allowed) - log_total)
    grad_soft = jnp.einsum(
        "qhgd,shd->hgqs", grad_att, values_all, preferred_element_type=jnp.float32
    )
    grad_scores = (
        soft_float * (grad_soft - jnp.sum(soft_float * grad_soft, axis=-1, keepdims=True))
    ).astype(jnp.bfloat16)
    value_part = jnp.einsum(
        "hgqs,qhgd->shd",
        soft_float.astype(jnp.bfloat16),
        grad_att,
        preferred_element_type=jnp.float32,
    )
    score_scale = HEAD_SIZE ** (-0.5)
    key_part = (
        jnp.einsum("hgqs,qhgd->shd", grad_scores, query_rows, preferred_element_type=jnp.float32)
        * score_scale
    )
    grad_queries = (
        jnp.einsum("hgqs,shd->qhgd", grad_scores, keys_all, preferred_element_type=jnp.float32)
        * score_scale
    )
    grad_queries = (
        unrope(grad_queries.reshape(row_count, query_heads, HEAD_SIZE), cosine_table, sine_table)
        .astype(jnp.bfloat16)
        .reshape(row_count, query_heads * HEAD_SIZE)
    )
    key_own, value_own = (
        lax.psum_scatter(
            key_part.reshape(position_count, key_heads * HEAD_SIZE).astype(jnp.bfloat16),
            "tensor",
            scatter_dimension=0,
            tiled=True,
        ).astype(jnp.float32),
        lax.psum_scatter(
            value_part.reshape(position_count, key_heads * HEAD_SIZE).astype(jnp.bfloat16),
            "tensor",
            scatter_dimension=0,
            tiled=True,
        ).astype(jnp.float32),
    )
    grad_keys = (
        unrope(key_own.reshape(row_count, key_heads, HEAD_SIZE), cosine_table, sine_table)
        .astype(jnp.bfloat16)
        .reshape(row_count, key_heads * HEAD_SIZE)
    )
    grad_values = value_own.astype(jnp.bfloat16)
    grad_query_w = contract_rows(hidden_one, grad_queries)
    grad_key_w = contract_rows(hidden_one, grad_keys)
    grad_value_w = contract_rows(hidden_one, grad_values)
    grad_normed_one = (
        contract_last(grad_queries, full_query)
        + contract_last(grad_keys, full_key)
        + contract_last(grad_values, full_value)
    )
    row_grad_one, grad_gain_one = norm_backward(grad_normed_one, row_values, scale_one, gain_one)
    grad_input = (grad_middle + row_grad_one).astype(jnp.bfloat16)
    return (
        grad_input,
        (
            grad_query_w,
            grad_key_w,
            grad_value_w,
            grad_gate_w,
            grad_up_w,
            grad_out_w,
            grad_down_w,
            grad_gain_one,
            grad_gain_two,
        ),
    )


def shards(
    inputs,
    lengths,
    gain_attn,
    gain_mlp,
    w_query,
    key_weight,
    value_weight,
    w_gate,
    w_up,
    w_out,
    w_down,
    cotangent,
):
    micro_count = inputs.shape[0]
    row_share = inputs.shape[2]
    row_start = lax.axis_index("tensor") * row_share
    outputs = []
    input_grads = []
    grad_totals = None
    for batch_index in range(micro_count):
        current = fetch_weights(
            gain_attn, gain_mlp, w_query, key_weight, value_weight, w_gate, w_up, w_out, w_down
        )
        output, kept = forward_pass(
            inputs[batch_index, 0], lengths[batch_index, 0], current, row_start
        )
        grad_input, batch_grads = backward_pass(cotangent[batch_index, 0], current, kept)
        if batch_index == 0:
            grad_totals = batch_grads
        else:
            grad_totals = jax.tree.map(jnp.add, grad_totals, batch_grads)
        outputs.append(output)
        input_grads.append(grad_input)
    grad_totals = reduce_over_data(grad_totals)
    (
        grad_query_w,
        grad_key_w,
        grad_value_w,
        grad_gate_w,
        grad_up_w,
        grad_out_w,
        grad_down_w,
        grad_gain_one,
        grad_gain_two,
    ) = grad_totals
    grad_query_w, grad_key_w, grad_value_w, grad_out_w, grad_gain_one, grad_gain_two = (
        lax.psum(grad_query_w.astype(jnp.bfloat16), "tensor").astype(jnp.float32),
        lax.psum(grad_key_w.astype(jnp.bfloat16), "tensor").astype(jnp.float32),
        lax.psum(grad_value_w.astype(jnp.bfloat16), "tensor").astype(jnp.float32),
        lax.psum(grad_out_w.astype(jnp.bfloat16), "tensor").astype(jnp.float32),
        lax.psum(grad_gain_one.astype(jnp.bfloat16), "tensor").astype(jnp.float32),
        lax.psum(grad_gain_two.astype(jnp.bfloat16), "tensor").astype(jnp.float32),
    )
    out_stack = jnp.stack(outputs)[:, None]
    grad_stack = jnp.stack(input_grads)[:, None]
    return (
        out_stack,
        grad_stack,
        grad_gain_one,
        grad_gain_two,
        grad_query_w,
        grad_key_w,
        grad_value_w,
        grad_gate_w,
        grad_up_w,
        grad_out_w,
        grad_down_w,
    )


def solution(mesh):
    in_specs = (
        P(None, "dp", "tensor", None),
        P(None, "dp"),
        P("dp"),
        P("dp"),
        P("dp", None),
        P("dp", None),
        P("dp", None),
        P("dp", "tensor"),
        P("dp", "tensor"),
        P("dp", None),
        P("tensor", "dp"),
        P(None, "dp", "tensor", None),
    )
    out_specs = (
        P(None, "dp", "tensor", None),
        P(None, "dp", "tensor", None),
        P("dp"),
        P("dp"),
        P("dp", None),
        P("dp", None),
        P("dp", None),
        P("dp", "tensor"),
        P("dp", "tensor"),
        P("dp", None),
        P("tensor", "dp"),
    )
    return jax.shard_map(shards, mesh=mesh, in_specs=in_specs, out_specs=out_specs, check_vma=False)
```

profile of v0, /device:TPU:0, one launch (start us, length us, event | category | flops | bytes accessed | tf_op | source)
XLA Modules:
  0.0 1363.0 jit_solution(11270381272452233820)
XLA Ops:
  14.7 23.7 %all-reduce.5 = (bf16[1152]{0:T(1024)(128)(2,1)S(1)}, bf16[1152]{0:T(1024)(128)(2,1)S(1)}) all-reduce(bf16[1152]{0:T(1024)(128)(2,1)S(1)} %dynamic-update-slice, bf16[1152]{0:T(1024)(128)(2,1)S(1)} %dynamic-update-slice.1), channel_id=1, replica_groups=mesh['dp'=8,'tensor'=4] {'dp'}, use_global_device_ids=true, to_apply=%add | all-reduce | flops 2304 | bytes 9216
  38.8 34.3 %all_gather.61 = bf16[1152,384]{1,0:T(8,128)(2,1)S(1)} all-gather(bf16[144,384]{1,0:T(8,128)(2,1)S(1)} %copy-done.50), channel_id=1, replica_groups=mesh['dp'=8,'tensor'=4] {'dp'}, dimensions={0}, use_global_device_ids=true | all-gather | bytes 995328 | tf_op jit(solution)/shard_map/all_gather | solution.py:60
  84.6 34.1 %all_gather.63 = bf16[1152,384]{1,0:T(8,128)(2,1)S(1)} all-gather(bf16[144,384]{1,0:T(8,128)(2,1)S(1)} %copy-done.51), channel_id=1, replica_groups=mesh['dp'=8,'tensor'=4] {'dp'}, dimensions={0}, use_global_device_ids=true | all-gather | bytes 995328 | tf_op jit(solution)/shard_map/all_gather | solution.py:59
  149.7 10.3 exponential_reduce_fusion.1
  160.1 9.5 convolution_convert_fusion.5
  188.5 25.1 %all-gather.14.cloned.1.call-done = bf16[1024,1152]{1,0:T(8,128)(2,1)} async-done(((bf16[256,1152]{1,0:T(8,128)(2,1)}), bf16[1024,1152]{1,0:T(8,128)(2,1)}) %all-gather.14.cloned.1.call-update) | async-done | bytes 2359312 | tf_op jit(solution)/shard_map/all_gather | solution.py:198
  219.7 41.9 %all-gather.16.cloned.1.call-done = bf16[1152,768]{1,0:T(8,128)(2,1)} async-done(((bf16[144,768]{1,0:T(8,128)(2,1)}), bf16[1152,768]{1,0:T(8,128)(2,1)}) %all-gather.16.cloned.1.call-update) | async-done | bytes 1769488 | tf_op jit(solution)/shard_map/all_gather | solution.py:61
  267.6 41.0 %all-gather.20.cloned.1.call-done = bf16[768,1152]{0,1:T(8,128)(2,1)} async-done(((bf16[768,144]{0,1:T(8,128)(2,1)}), bf16[768,1152]{0,1:T(8,128)(2,1)}) %all-gather.20.cloned.1.call-update) | async-done | bytes 1769488 | tf_op jit(solution)/shard_map/all_gather | solution.py:64
  308.6 25.3 %all-gather.24.cloned.1.call-done = bf16[1024,1152]{1,0:T(8,128)(2,1)} async-done(((bf16[256,1152]{1,0:T(8,128)(2,1)}), bf16[1024,1152]{1,0:T(8,128)(2,1)}) %all-gather.24.cloned.1.call-update) | async-done | bytes 2359312 | tf_op jit(solution)/shard_map/all_gather | solution.py:270
  361.6 11.6 all_gather.73
  381.3 10.8 exponential_reduce_fusion
  392.8 11.0 convolution_convert_fusion.4
  410.4 23.2 %all-gather.22.cloned.1.call-done = bf16[1024,1152]{1,0:T(8,128)(2,1)} async-done(((bf16[256,1152]{1,0:T(8,128)(2,1)}), bf16[1024,1152]{1,0:T(8,128)(2,1)}) %all-gather.22.cloned.1.call-update) | async-done | bytes 2359312 | tf_op jit(solution)/shard_map/all_gather | solution.py:198
  443.7 15.5 %all-gather.26.cloned.1.call-done = bf16[1024,1152]{1,0:T(8,128)(2,1)} async-done(((bf16[256,1152]{1,0:T(8,128)(2,1)}), bf16[1024,1152]{1,0:T(8,128)(2,1)}) %all-gather.26.cloned.1.call-update) | async-done | bytes 2359312 | tf_op jit(solution)/shard_map/all_gather | solution.py:270
  486.9 20.2 %reduce-scatter.26.cloned.1.call-done = bf16[256,1152]{1,0:T(8,128)(2,1)} async-done(((bf16[1024,1152]{1,0:T(8,128)(2,1)}), bf16[256,1152]{1,0:T(8,128)(2,1)}) %reduce-scatter.26.cloned.1.call-update) | async-done | bytes 589840 | tf_op jit(solution)/shard_map/reduce_scatter | solution.py:83
  509.6 32.9 %reduce-scatter.16.cloned.1.call-done = bf16[256,1152]{1,0:T(8,128)(2,1)} async-done(((bf16[1024,1152]{1,0:T(8,128)(2,1)}), bf16[256,1152]{1,0:T(8,128)(2,1)}) %reduce-scatter.16.cloned.1.call-update) | async-done | bytes 589840 | tf_op jit(solution)/shard_map/reduce_scatter | solution.py:69
  542.5 35.8 %reduce-scatter.18.cloned.1.call-done = bf16[256,1152]{1,0:T(8,128)(2,1)} async-done(((bf16[1024,1152]{1,0:T(8,128)(2,1)}), bf16[256,1152]{1,0:T(8,128)(2,1)}) %reduce-scatter.18.cloned.1.call-update) | async-done | bytes 589840 | tf_op jit(solution)/shard_map/reduce_scatter | solution.py:69
  593.5 12.0 bitcast_convert_fusion.1
  605.6 12.2 bitcast_convert_fusion
  617.8 12.7 fusion
  631.0 13.6 fusion.2
  652.1 12.9 fusion.3
  665.0 13.6 fusion.5
  689.0 25.8 %reduce-scatter.22.cloned.1.call-done = bf16[256,384]{0,1:T(8,128)(2,1)} async-done(((bf16[1024,384]{0,1:T(8,128)(2,1)}), bf16[256,384]{0,1:T(8,128)(2,1)}) %reduce-scatter.22.cloned.1.call-update) | async-done | bytes 196624 | tf_op jit(solution)/shard_map/reduce_scatter | solution.py:318
  751.1 33.4 %reduce-scatter.36.cloned.1.call-done = f32[144,384]{1,0:T(8,128)} async-done(((f32[1152,384]{1,0:T(8,128)}), f32[144,384]{1,0:T(8,128)}) %reduce-scatter.36.cloned.1.call-update) | async-done | bytes 221200 | tf_op jit(solution)/shard_map/reduce_scatter | solution.py:103
  786.1 67.7 %reduce-scatter.34.cloned.1.call-done = f32[144,384]{1,0:T(8,128)} async-done(((f32[1152,384]{1,0:T(8,128)}), f32[144,384]{1,0:T(8,128)}) %reduce-scatter.34.cloned.1.call-update) | async-done | bytes 221200 | tf_op jit(solution)/shard_map/reduce_scatter | solution.py:102
  855.3 105.0 %reduce-scatter.42.cloned.1.call-done = f32[144,1152]{1,0:T(8,128)} async-done(((f32[1152,1152]{1,0:T(8,128)}), f32[144,1152]{1,0:T(8,128)}) %reduce-scatter.42.cloned.1.call-update) | async-done | bytes 663568 | tf_op jit(solution)/shard_map/reduce_scatter | solution.py:106
  962.2 106.1 %reduce-scatter.32.cloned.1.call-done = f32[144,1152]{1,0:T(8,128)} async-done(((f32[1152,1152]{1,0:T(8,128)}), f32[144,1152]{1,0:T(8,128)}) %reduce-scatter.32.cloned.1.call-update) | async-done | bytes 663568 | tf_op jit(solution)/shard_map/reduce_scatter | solution.py:101
  1107.7 37.7 %all-reduce.4 = (bf16[1152]{0:T(1024)(128)(2,1)}, bf16[1152]{0:T(1024)(128)(2,1)}) all-reduce(f32[1152]{0:T(1024)} %add.291, f32[1152]{0:T(1024)} %add.292), channel_id=10, replica_groups=mesh['dp'=8,'tensor'=4] {'dp'}, use_global_device_ids=true, to_apply=%region_24.25.clone | all-reduce | flops 2304 | bytes 13824
  1167.9 22.6 %reduce-scatter.38.cloned.1.call-done = f32[144,768]{1,0:T(8,128)} async-done(((f32[1152,768]{1,0:T(8,128)}), f32[144,768]{1,0:T(8,128)}) %reduce-scatter.38.cloned.1.call-update) | async-done | bytes 442384 | tf_op jit(solution)/shard_map/reduce_scatter | solution.py:104
  1190.5 82.8 %reduce-scatter.40.cloned.1.call-done = f32[144,768]{1,0:T(8,128)} async-done(((f32[1152,768]{1,0:T(8,128)}), f32[144,768]{1,0:T(8,128)}) %reduce-scatter.40.cloned.1.call-update) | async-done | bytes 442384 | tf_op jit(solution)/shard_map/reduce_scatter | solution.py:105
  1273.3 83.0 %reduce-scatter.44.cloned.1.call-done = f32[768,144]{0,1:T(8,128)} async-done(((f32[768,1152]{0,1:T(8,128)}), f32[768,144]{0,1:T(8,128)}) %reduce-scatter.44.cloned.1.call-update) | async-done | bytes 442384 | tf_op jit(solution)/shard_map/reduce_scatter | solution.py:107
  (347 shorter events, 299.4 us)
Async XLA Ops:
  7.2 124.3 %all-gather.10.cloned.1.call-start = ((), (), s32[]{:S(2)}) async-start(), calls=%async_computation.15 | async-start | bytes 2985984 | tf_op jit(solution)/shard_map/all_gather | solution.py:58
  8.0 161.6 %all-gather.12.cloned.1.call-start = ((), (), s32[]{:S(2)}) async-start(), calls=%async_computation.16 | async-start | bytes 2985984 | tf_op jit(solution)/shard_map/all_gather | solution.py:63
  8.7 179.8 %all-gather.18.cloned.1.call-start = ((), (), s32[]{:S(2)}) async-start(), calls=%async_computation.19 | async-start | bytes 1990656 | tf_op jit(solution)/shard_map/all_gather | solution.py:62
  9.5 204.1 %all-gather.14.cloned.1.call-start = ((), (), s32[]{:S(2)}) async-start(), calls=%async_computation.17 | async-start | bytes 2949120 | tf_op jit(solution)/shard_map/all_gather | solution.py:198
  38.5 310.0 %copy-start.46 = (f32[1152]{0:T(1024)}, f32[1152]{0:T(1024)S(1)}, u32[]{:S(2)}) copy-start(f32[1152]{0:T(1024)S(1)} %convert_element_type.339) | copy-start | bytes 13828
  38.7 102.4 %copy-start.28 = (f32[256,64]{0,1:T(8,128)}, f32[256,64]{0,1:T(8,128)S(1)}, u32[]{:S(2)}) copy-start(f32[256,64]{0,1:T(8,128)S(1)} %pad_maximum_fusion.4) | copy-start | bytes 196612
  38.8 102.3 %copy-start.37 = (f32[256,64]{0,1:T(8,128)}, f32[256,64]{0,1:T(8,128)S(1)}, u32[]{:S(2)}) copy-start(f32[256,64]{0,1:T(8,128)S(1)} %pad_maximum_fusion.5) | copy-start | bytes 196612
  73.7 274.8 %copy-start.54 = (f32[256]{0:T(256)}, f32[256]{0:T(256)S(1)}, u32[]{:S(2)}) copy-start(f32[256]{0:T(256)S(1)} %get-tuple-element.120) | copy-start | bytes 3076
  172.6 233.3 %copy-start.10 = (f32[256,1152]{1,0:T(8,128)}, f32[256,1152]{1,0:T(8,128)S(1)}, u32[]{:S(2)}) copy-start(f32[256,1152]{1,0:T(8,128)S(1)} %get-tuple-element.134) | copy-start | bytes 3538948
  174.3 87.3 %all-gather.16.cloned.1.call-start = ((), (), s32[]{:S(2)}) async-start(), calls=%async_computation.18 | async-start | bytes 1990656 | tf_op jit(solution)/shard_map/all_gather | solution.py:61
  174.8 133.7 %all-gather.20.cloned.1.call-start = ((), (), s32[]{:S(2)}) async-start(), calls=%async_computation.20 | async-start | bytes 1990656 | tf_op jit(solution)/shard_map/all_gather | solution.py:64
  175.4 158.4 %all-gather.24.cloned.1.call-start = ((), (), s32[]{:S(2)}) async-start(), calls=%async_computation.24 | async-start | bytes 2949120 | tf_op jit(solution)/shard_map/all_gather | solution.py:270
  179.5 226.4 %reduce-scatter.20.cloned.1.call-start = ((), (), s32[]{:S(2)}) async-start(), calls=%async_computation.25 | async-start | bytes 2949120 | tf_op jit(solution)/shard_map/reduce_scatter | solution.py:83
  348.5 85.1 %all-gather.22.cloned.1.call-start = ((), (), s32[]{:S(2)}) async-start(), calls=%async_computation.22 | async-start | bytes 2949120 | tf_op jit(solution)/shard_map/all_gather | solution.py:198
  409.3 49.9 %all-gather.26.cloned.1.call-start = ((), (), s32[]{:S(2)}) async-start(), calls=%async_computation.28 | async-start | bytes 2949120 | tf_op jit(solution)/shard_map/all_gather | solution.py:270
  409.9 97.2 %reduce-scatter.26.cloned.1.call-start = ((), (), s32[]{:S(2)}) async-start(), calls=%async_computation.29 | async-start | bytes 2949120 | tf_op jit(solution)/shard_map/reduce_scatter | solution.py:83
  473.8 68.7 %reduce-scatter.16.cloned.1.call-start = ((), (), s32[]{:S(2)}) async-start(), calls=%async_computation.21 | async-start | bytes 2949120 | tf_op jit(solution)/shard_map/reduce_scatter | solution.py:69
  479.5 98.8 %reduce-scatter.18.cloned.1.call-start = ((), (), s32[]{:S(2)}) async-start(), calls=%async_computation.23 | async-start | bytes 2949120 | tf_op jit(solution)/shard_map/reduce_scatter | solution.py:69
  485.5 92.9 %copy-start.62 = (f32[256]{0:T(256)S(1)}, f32[256]{0:T(256)}, u32[]{:S(2)}) copy-start(f32[256]{0:T(256)} %get-tuple-element.121) | copy-start | bytes 3076
  485.5 197.2 %reduce-scatter.24.cloned.1.call-start = ((), (), s32[]{:S(2)}) async-start(), calls=%async_computation.27 | async-start | bytes 983040 | tf_op jit(solution)/shard_map/reduce_scatter | solution.py:324
  582.6 136.9 %copy-start.5 = (f32[256,1152]{1,0:T(8,128)}, f32[256,1152]{1,0:T(8,128)S(1)}, u32[]{:S(2)}) copy-start(f32[256,1152]{1,0:T(8,128)S(1)} %get-tuple-element.74) | copy-start | bytes 3538948
  605.5 80.0 %reduce-scatter.30.cloned.1.call-start = ((), (), s32[]{:S(2)}) async-start(), calls=%async_computation.31 | async-start | bytes 983040 | tf_op jit(solution)/shard_map/reduce_scatter | solution.py:324
  630.6 58.4 %reduce-scatter.28.cloned.1.call-start = ((), (), s32[]{:S(2)}) async-start(), calls=%async_computation.30 | async-start | bytes 983040 | tf_op jit(solution)/shard_map/reduce_scatter | solution.py:318
  665.0 49.8 %reduce-scatter.22.cloned.1.call-start = ((), (), s32[]{:S(2)}) async-start(), calls=%async_computation.26 | async-start | bytes 983040 | tf_op jit(solution)/shard_map/reduce_scatter | solution.py:318
  682.6 101.8 %reduce-scatter.36.cloned.1.call-start = ((), (), s32[]{:S(2)}) async-start(), calls=%async_computation.34 | async-start | bytes 1990656 | tf_op jit(solution)/shard_map/reduce_scatter | solution.py:103
  688.9 164.8 %reduce-scatter.34.cloned.1.call-start = ((), (), s32[]{:S(2)}) async-start(), calls=%async_computation.33 | async-start | bytes 1990656 | tf_op jit(solution)/shard_map/reduce_scatter | solution.py:102
  719.5 240.8 %reduce-scatter.42.cloned.1.call-start = ((), (), s32[]{:S(2)}) async-start(), calls=%async_computation.37 | async-start | bytes 5971968 | tf_op jit(solution)/shard_map/reduce_scatter | solution.py:106
  725.2 343.0 %reduce-scatter.32.cloned.1.call-start = ((), (), s32[]{:S(2)}) async-start(), calls=%async_computation.32 | async-start | bytes 5971968 | tf_op jit(solution)/shard_map/reduce_scatter | solution.py:101
  745.1 416.8 %all-reduce.10.cloned.1.call-start = ((), (), s32[]{:S(2)}) async-start(), calls=%async_computation.39 | async-start | bytes 1769472 | tf_op jit(solution)/shard_map/psum | solution.py:410
  1070.2 120.3 %reduce-scatter.38.cloned.1.call-start = ((), (), s32[]{:S(2)}) async-start(), calls=%async_computation.35 | async-start | bytes 3981312 | tf_op jit(solution)/shard_map/reduce_scatter | solution.py:104
  1077.3 196.0 %reduce-scatter.40.cloned.1.call-start = ((), (), s32[]{:S(2)}) async-start(), calls=%async_computation.36 | async-start | bytes 3981312 | tf_op jit(solution)/shard_map/reduce_scatter | solution.py:105
  1085.7 270.5 %reduce-scatter.44.cloned.1.call-start = ((), (), s32[]{:S(2)}) async-start(), calls=%async_computation.38 | async-start | bytes 3981312 | tf_op jit(solution)/shard_map/reduce_scatter | solution.py:107
  (76 other events, 873.1 us)
Sparse Core Ops, SparseCore 0:
  10.2 70.2 all-gather.9
  82.7 58.9 all-gather.11
  143.9 44.5 all-gather.17
  190.5 23.0 all-gather.13
  215.6 45.9 all-gather.15
  263.6 44.9 all-gather.19
  310.7 23.0 all-gather.23
  348.6 35.0 reduce-scatter.19
  409.4 24.1 all-gather.21
  435.1 24.0 all-gather.25
  473.9 33.0 reduce-scatter.25
  509.4 33.0 reduce-scatter.15
  545.2 33.0 reduce-scatter.17
  605.6 23.2 reduce-scatter.23
  631.5 23.2 reduce-scatter.29
  665.1 23.2 reduce-scatter.27
  691.5 23.2 reduce-scatter.21
  718.1 66.3 reduce-scatter.35
  788.3 65.3 reduce-scatter.33
  857.2 103.0 reduce-scatter.41
  964.3 103.8 reduce-scatter.31
  1071.4 35.1 all-reduce.9
  1110.8 79.6 reduce-scatter.37
  1194.5 78.7 reduce-scatter.39
  1277.5 78.7 reduce-scatter.43
where the time goes:
time: 1370 us; the launch traced here: 1360 us
  waiting for transfers between devices  800 us (58%)
  matrix products  238 us (17%)
  blocking collectives  173 us (13%)
  other arithmetic  102 us (7%)
  local copies, waits for them, and re-layouts  30.3 us (2%)
  between operations  16.6 us (1%)
    reduce_scatter x1, waiting for transfers between devices, reduce_over_data(): lax.psum_scatter(grad_query_w, 'dp', scatter_dimension=0, tiled=True)  106 us
    reduce_scatter x1, waiting for transfers between devices, reduce_over_data(): lax.psum_scatter(grad_out_w, 'dp', scatter_dimension=0, tiled=True)  105 us
    reduce_scatter x1, waiting for transfers between devices, reduce_over_data(): lax.psum_scatter(grad_down_w, 'dp', scatter_dimension=1, tiled=True)  83 us
    reduce_scatter x1, waiting for transfers between devices, reduce_over_data(): lax.psum_scatter(grad_up_w, 'dp', scatter_dimension=0, tiled=True)  82.8 us
    reduce_scatter x2, waiting for transfers between devices, project_sum(): lax.psum_scatter(jnp.dot(left_side, right_side, preferred_element_type=jn...  68.7 us
    reduce_scatter x1, waiting for transfers between devices, reduce_over_data(): lax.psum_scatter(grad_key_w, 'dp', scatter_dimension=0, tiled=True)  67.7 us
    unnamed x2, blocking collectives  61.5 us
    all_gather x2, waiting for transfers between devices, forward_pass(): lax.all_gather((middle * scale_two * gain_two).astype(jnp.bfloat16), 'ten...  48.3 us
  transfers between devices with their start and end apart: 25, of which 18 were waited for; matrix products, arithmetic and copies ran while one was open for 22% of the time, Pallas kernels for 0%

commit v1 on v0

v1 whole, which is shorter than its diff:
```python
import jax
import jax.numpy as jnp
from jax import lax
from jax.sharding import PartitionSpec as P

HEAD_SIZE = 64
EPSILON = 1e-05
ROPE_BASE = 10000.0
MASKED = -1e30
BF16 = jnp.bfloat16
F32 = jnp.float32

BLOCK_XOR = (0, 2, 1, 3)


def near(value):
    count = lax.axis_size("tensor")
    return lax.ppermute(value, "tensor", [(i, i ^ 1) for i in range(count)])


def far(value):
    count = lax.axis_size("tensor")
    return lax.ppermute(value, "tensor", [(i, i ^ 2) for i in range(count)])


def gather_rows(own):
    pair = jnp.concatenate([own, far(own)], axis=0)
    return jnp.concatenate([pair, near(pair)], axis=0)


def scatter_rows(partial):
    half = partial.shape[0] // 2
    quarter = half // 2
    kept = partial[:half].astype(F32) + near(partial[half:].astype(BF16)).astype(F32)
    return kept[:quarter] + far(kept[quarter:].astype(BF16)).astype(F32)


def dot(left_side, right_side):
    return jnp.dot(left_side, right_side, preferred_element_type=F32)


def contract_rows(left_side, right_side):
    return lax.dot_general(
        left_side, right_side, (((0,), (0,)), ((), ())), preferred_element_type=F32
    )


def contract_last(left_side, right_side):
    return lax.dot_general(
        left_side, right_side, (((1,), (1,)), ((), ())), preferred_element_type=F32
    )


def rope_tables(positions, head_dim):
    half_dim = head_dim // 2
    exponent = jnp.arange(half_dim, dtype=F32) * (2.0 / head_dim)
    frequency = ROPE_BASE ** (-exponent)
    angles = positions[:, None] * frequency[None, :]
    cosine_table = jnp.concatenate([jnp.cos(angles), jnp.cos(angles)], axis=1)
    sine_table = jnp.concatenate([jnp.sin(angles), jnp.sin(angles)], axis=1)
    return (cosine_table, sine_table)


def rotate_half(values):
    half_dim = values.shape[-1] // 2
    return jnp.concatenate([-values[..., half_dim:], values[..., :half_dim]], axis=-1)


def apply_rotary(values, cosine_table, sine_table):
    return values * cosine_table[:, None, :] + rotate_half(values) * sine_table[:, None, :]


def unrope(grads_in, cosine_table, sine_table):
    half_dim = grads_in.shape[-1] // 2
    scaled = grads_in * sine_table[:, None, :]
    turned = jnp.concatenate([scaled[..., half_dim:], -scaled[..., :half_dim]], axis=-1)
    return grads_in * cosine_table[:, None, :] + turned


def row_scale_of(values):
    return lax.rsqrt(jnp.mean(values * values, axis=-1, keepdims=True) + EPSILON)


def norm_backward(grad_normed, row_values, row_scale, gain_full):
    gain_grad = jnp.sum(grad_normed * row_values * row_scale, axis=0)
    inner_grad = grad_normed * gain_full
    row_grad = row_scale * inner_grad - row_values * row_scale**3 * jnp.mean(
        inner_grad * row_values, axis=-1, keepdims=True
    )
    return (row_grad, gain_grad)


def attention_scores(query_rows, keys_all, allowed):
    raw_scores = jnp.einsum(
        "qhgd,shd->hgqs", query_rows, keys_all, preferred_element_type=F32
    ) * HEAD_SIZE ** (-0.5)
    return jnp.where(allowed, raw_scores, MASKED)


def attend(query_rows, keys_all, values_all, allowed):
    row_count = query_rows.shape[0]
    scores = attention_scores(query_rows, keys_all, allowed)
    maxima = jnp.max(scores, axis=-1, keepdims=True)
    log_total = maxima + jnp.log(jnp.sum(jnp.exp(scores - maxima), axis=-1, keepdims=True))
    soft_low = jnp.exp(scores - log_total).astype(BF16)
    attended = jnp.einsum("hgqs,shd->qhgd", soft_low, values_all, preferred_element_type=F32)
    return attended.reshape(row_count, -1).astype(BF16), log_total


def attend_backward(grad_att, query_rows, keys_all, values_all, allowed, log_total):
    row_count, position_count = query_rows.shape[0], keys_all.shape[0]
    soft_float = jnp.exp(attention_scores(query_rows, keys_all, allowed) - log_total)
    grad_soft = jnp.einsum("qhgd,shd->hgqs", grad_att, values_all, preferred_element_type=F32)
    grad_scores = (
        soft_float * (grad_soft - jnp.sum(soft_float * grad_soft, axis=-1, keepdims=True))
    ).astype(BF16)
    value_part = jnp.einsum(
        "hgqs,qhgd->shd", soft_float.astype(BF16), grad_att, preferred_element_type=F32
    )
    score_scale = HEAD_SIZE ** (-0.5)
    key_part = (
        jnp.einsum("hgqs,qhgd->shd", grad_scores, query_rows, preferred_element_type=F32)
        * score_scale
    )
    grad_queries = (
        jnp.einsum("hgqs,shd->qhgd", grad_scores, keys_all, preferred_element_type=F32)
        * score_scale
    )
    return (
        grad_queries.reshape(row_count, -1),
        jnp.concatenate(
            [key_part.reshape(position_count, -1), value_part.reshape(position_count, -1)], axis=1
        ),
    )


def shards(
    inputs,
    lengths,
    gain_attn,
    gain_mlp,
    w_query,
    key_weight,
    value_weight,
    w_gate,
    w_up,
    w_out,
    w_down,
    cotangent,
):
    micro = inputs.shape[0]
    row_share = inputs.shape[2]
    model_width = inputs.shape[3]
    tensor_count = lax.axis_size("tensor")
    tensor_index = lax.axis_index("tensor")
    query_width = w_query.shape[1]
    key_width = key_weight.shape[1]
    hidden_share = w_gate.shape[1]
    query_heads = query_width // HEAD_SIZE
    key_heads = key_width // HEAD_SIZE
    group_width = query_heads // key_heads

    attn_local = jnp.concatenate([w_query, key_weight, value_weight, w_out], axis=1)
    attn_width = attn_local.shape[1]
    block_width = attn_width // tensor_count
    attn_quarter = lax.dynamic_slice_in_dim(attn_local, tensor_index * block_width, block_width, 1)
    attn_blocks = lax.all_gather(attn_quarter, ("tensor", "dp"), axis=0, tiled=True)
    attn_full = jnp.concatenate(
        [attn_blocks[b * model_width : (b + 1) * model_width] for b in range(tensor_count)], axis=1
    )
    mlp_local = jnp.concatenate([w_gate, w_up, w_down.T], axis=1)
    mlp_full = lax.all_gather(mlp_local, "dp", axis=0, tiled=True)
    gains = lax.all_gather(jnp.stack([gain_attn, gain_mlp]), "dp", axis=1, tiled=True).astype(F32)
    gain_one, gain_two = gains[0:1], gains[1:2]
    full_query = attn_full[:, :query_width]
    full_key = attn_full[:, query_width : query_width + key_width]
    full_value = attn_full[:, query_width + key_width : query_width + 2 * key_width]
    full_out = attn_full[:, query_width + 2 * key_width :]
    full_gate = mlp_full[:, :hidden_share]
    full_up = mlp_full[:, hidden_share : 2 * hidden_share]
    full_down_t = mlp_full[:, 2 * hidden_share :]

    row_start = tensor_index * row_share
    query_pos = row_start + jnp.arange(row_share, dtype=jnp.int32)
    block_start = jnp.stack([(tensor_index ^ x) * row_share for x in BLOCK_XOR])
    key_pos = (block_start[:, None] + jnp.arange(row_share, dtype=jnp.int32)[None, :]).reshape(-1)
    cosine_table, sine_table = rope_tables(query_pos.astype(F32), HEAD_SIZE)

    valids = [
        (query_pos < lengths[b, 0]).astype(F32)[:, None] for b in range(micro)
    ]
    grad_rows = [cotangent[b, 0].astype(F32) * valids[b] for b in range(micro)]
    grad_own = [g.astype(BF16) for g in grad_rows]
    grad_far = far(jnp.stack(grad_own))
    grad_near = near(jnp.stack([jnp.stack(grad_own), grad_far]))
    grad_ffn = [
        jnp.concatenate([grad_own[b], grad_far[b], grad_near[0, b], grad_near[1, b]], axis=0)
        for b in range(micro)
    ]

    kept = []
    for b in range(micro):
        row_values = inputs[b, 0].astype(F32)
        scale_one = row_scale_of(row_values)
        hidden_one = (row_values * scale_one * gain_one).astype(BF16)
        key_unrotated = dot(hidden_one, full_key).reshape(row_share, key_heads, HEAD_SIZE)
        values_own = dot(hidden_one, full_value).astype(BF16)
        keys_own = (
            apply_rotary(key_unrotated, cosine_table, sine_table)
            .astype(BF16)
            .reshape(row_share, key_width)
        )
        pairs_all = gather_rows(jnp.concatenate([keys_own, values_own], axis=1))
        query_unrotated = dot(hidden_one, full_query).reshape(row_share, query_heads, HEAD_SIZE)
        query_rows = (
            apply_rotary(query_unrotated, cosine_table, sine_table)
            .astype(BF16)
            .reshape(row_share, key_heads, group_width, HEAD_SIZE)
        )
        keys_all = pairs_all[:, :key_width].reshape(-1, key_heads, HEAD_SIZE)
        values_all = pairs_all[:, key_width:].reshape(-1, key_heads, HEAD_SIZE)
        allowed = (key_pos[None, :] <= query_pos[:, None]) & (key_pos[None, :] < lengths[b, 0])
        attended, log_total = attend(query_rows, keys_all, values_all, allowed)
        middle = row_values + dot(attended, full_out)
        scale_two = row_scale_of(middle)
        hidden_two = gather_rows((middle * scale_two * gain_two).astype(BF16))
        kept.append(
            dict(
                row_values=row_values,
                scale_one=scale_one,
                hidden_one=hidden_one,
                query_rows=query_rows,
                keys_all=keys_all,
                values_all=values_all,
                allowed=allowed,
                log_total=log_total,
                attended=attended,
                middle=middle,
                scale_two=scale_two,
                hidden_two=hidden_two,
            )
        )

    for b in range(micro):
        k = kept[b]
        gate_proj = dot(k["hidden_two"], full_gate)
        up_proj = dot(k["hidden_two"], full_up)
        grad_act = dot(grad_ffn[b], full_down_t)
        sigmoid_gate = jax.nn.sigmoid(gate_proj)
        k["activated"] = (gate_proj * sigmoid_gate * up_proj).astype(BF16)
        k["grad_gate"] = (
            grad_act * up_proj * sigmoid_gate * (1.0 + gate_proj * (1.0 - sigmoid_gate))
        ).astype(BF16)
        k["grad_up"] = (grad_act * gate_proj * sigmoid_gate).astype(BF16)
        grad_partial = contract_last(k["grad_gate"], full_gate) + contract_last(
            k["grad_up"], full_up
        )
        k["grad_normed_two"] = scatter_rows(grad_partial)
    def total(left_side, right_side):
        parts = [contract_rows(left_side(b), right_side(b)) for b in range(micro)]
        return sum(parts[1:], parts[0])

    grad_mlp_w = jnp.concatenate(
        [
            total(lambda b: kept[b]["hidden_two"], lambda b: kept[b]["grad_gate"]).astype(BF16),
            total(lambda b: kept[b]["hidden_two"], lambda b: kept[b]["grad_up"]).astype(BF16),
            total(lambda b: grad_ffn[b], lambda b: kept[b]["activated"]).astype(BF16),
        ],
        axis=1,
    )
    grad_mlp_w = lax.psum_scatter(grad_mlp_w, "dp", scatter_dimension=0, tiled=True).astype(F32)
    grad_gate_w = grad_mlp_w[:, :hidden_share]
    grad_up_w = grad_mlp_w[:, hidden_share : 2 * hidden_share]
    grad_down_w = grad_mlp_w[:, 2 * hidden_share :].T

    gain_two_grads = []
    for b in range(micro):
        k = kept[b]
        row_grad_two, gain_two_grad = norm_backward(
            k["grad_normed_two"], k["middle"], k["scale_two"], gain_two
        )
        gain_two_grads.append(gain_two_grad)
        k["grad_middle"] = grad_rows[b] + row_grad_two
        k["grad_branch"] = k["grad_middle"].astype(BF16)
        grad_att = (
            contract_last(k["grad_branch"], full_out)
            .astype(BF16)
            .reshape(row_share, key_heads, group_width, HEAD_SIZE)
        )
        grad_queries, pair_partial = attend_backward(
            grad_att, k["query_rows"], k["keys_all"], k["values_all"], k["allowed"], k["log_total"]
        )
        pair_own = scatter_rows(pair_partial)
        k["grad_queries"] = (
            unrope(grad_queries.reshape(row_share, query_heads, HEAD_SIZE), cosine_table, sine_table)
            .astype(BF16)
            .reshape(row_share, query_width)
        )
        grad_keys = (
            unrope(
                pair_own[:, :key_width].reshape(row_share, key_heads, HEAD_SIZE),
                cosine_table,
                sine_table,
            )
            .astype(BF16)
            .reshape(row_share, key_width)
        )
        k["grad_pairs"] = jnp.concatenate(
            [k["grad_queries"], grad_keys, pair_own[:, key_width:].astype(BF16)], axis=1
        )

    outputs, input_grads, gain_one_grads = [], [], []
    full_qkv = attn_full[:, : query_width + 2 * key_width]
    for b in range(micro):
        k = kept[b]
        grad_normed_one = contract_last(k["grad_pairs"], full_qkv)
        row_grad_one, gain_one_grad = norm_backward(
            grad_normed_one, k["row_values"], k["scale_one"], gain_one
        )
        gain_one_grads.append(gain_one_grad)
        input_grads.append((k["grad_middle"] + row_grad_one).astype(BF16))
        ffn_out = scatter_rows(contract_last(k["activated"], full_down_t))
        outputs.append((valids[b] * (k["middle"] + ffn_out)).astype(BF16))

    grad_gains = jnp.stack(
        [sum(gain_one_grads[1:], gain_one_grads[0]), sum(gain_two_grads[1:], gain_two_grads[0])]
    )
    grad_attn_w = jnp.concatenate(
        [
            total(lambda b: kept[b]["hidden_one"], lambda b: kept[b]["grad_pairs"]),
            total(lambda b: kept[b]["attended"], lambda b: kept[b]["grad_branch"]),
        ],
        axis=1,
    )
    blocks = [grad_attn_w[:, b * block_width : (b + 1) * block_width] for b in range(tensor_count)]
    odd = (tensor_index & 1) == 1
    high = (tensor_index & 2) == 2
    sent = [jnp.where(odd, blocks[0], blocks[1]), jnp.where(odd, blocks[2], blocks[3])]
    mine = [jnp.where(odd, blocks[1], blocks[0]), jnp.where(odd, blocks[3], blocks[2])]
    came = near(jnp.stack(sent).astype(BF16)).astype(F32)
    low_sum, high_sum = mine[0] + came[0], mine[1] + came[1]
    came = far(jnp.where(high, low_sum, high_sum).astype(BF16)).astype(F32)
    quarter = (jnp.where(high, high_sum, low_sum) + came).astype(BF16)
    quarter = lax.psum_scatter(quarter, "dp", scatter_dimension=0, tiled=True)
    other = far(quarter)
    pair = jnp.stack([jnp.where(high, other, quarter), jnp.where(high, quarter, other)])
    other = near(pair)
    even_pair, odd_pair = jnp.where(odd, other, pair), jnp.where(odd, pair, other)
    grad_attn = jnp.concatenate(
        [even_pair[0], odd_pair[0], even_pair[1], odd_pair[1]], axis=1
    ).astype(F32)
    gains_own = lax.psum_scatter(
        lax.psum(grad_gains, "tensor"), "dp", scatter_dimension=1, tiled=True
    )
    return (
        jnp.stack(outputs)[:, None],
        jnp.stack(input_grads)[:, None],
        gains_own[0],
        gains_own[1],
        grad_attn[:, :query_width],
        grad_attn[:, query_width : query_width + key_width],
        grad_attn[:, query_width + key_width : query_width + 2 * key_width],
        grad_gate_w,
        grad_up_w,
        grad_attn[:, query_width + 2 * key_width :],
        grad_down_w,
    )


def solution(mesh):
    in_specs = (
        P(None, "dp", "tensor", None),
        P(None, "dp"),
        P("dp"),
        P("dp"),
        P("dp", None),
        P("dp", None),
        P("dp", None),
        P("dp", "tensor"),
        P("dp", "tensor"),
        P("dp", None),
        P("tensor", "dp"),
        P(None, "dp", "tensor", None),
    )
    out_specs = (
        P(None, "dp", "tensor", None),
        P(None, "dp", "tensor", None),
        P("dp"),
        P("dp"),
        P("dp", None),
        P("dp", None),
        P("dp", None),
        P("dp", "tensor"),
        P("dp", "tensor"),
        P("dp", None),
        P("tensor", "dp"),
    )
    return jax.shard_map(shards, mesh=mesh, in_specs=in_specs, out_specs=out_specs, check_vma=False)
```

time: 1370 us -> 762 us (0.56)
  waiting for transfers between devices: 800 us -> 309 us
  blocking collectives: 173 us -> 26.6 us
  matrix products: 238 us -> 169 us
  local copies, waits for them, and re-layouts: 30.3 us -> 91.5 us
  starting transfers between devices: 2.62 us -> 21.1 us
  other arithmetic: 102 us -> 117 us
    reduce_scatter x15 -> x0, waiting for transfers between devices: 615 us -> none  [the longest x1 106 us: reduce_over_data(): lax.psum_scatter(grad_query_w, 'dp', scatter_dimension=0, tiled=True)]
    unnamed x25 -> x8, waiting for transfers between devices: 3.96 us -> 154 us
    all_gather x9 -> x2, waiting for transfers between devices: 181 us -> 38.5 us  [the longest x1 38.5 us: shards(): lax.all_gather(attn_quarter, ('tensor', 'dp'), axis=0, tiled=True)]
    ppermute x0 -> x26, waiting for transfers between devices: none -> 116 us  [the longest x13 107 us: far(): return lax.ppermute(value, 'tensor', [(i, i ^ 2) for i in range(count)])]
    all_gather x6 -> x1, blocking collectives: 105 us -> 20.8 us  [shards(): lax.all_gather(jnp.stack([gain_attn, gain_mlp]), 'dp', axis=1, tiled=True)]
    unnamed x2 -> x0, blocking collectives: 61.5 us -> none
    unnamed x173 -> x340, local copies, waits for them, and re-layouts: 15.1 us -> 49.8 us
    dot_general x24, matrix products: 135 us -> 103 us  [the longest x14 30.9 us: dot(): return jnp.dot(left_side, right_side, preferred_element_type=F32)]
  transfers between devices with their start and end apart: 25 -> 31, of which waited for: 18 -> 16; matrix products, arithmetic and copies ran while one was open for 22% -> 27% of each run, Pallas kernels for 0% -> 0%
where the time goes in v1:
time: 762 us; the launch traced here: 751 us
  waiting for transfers between devices  309 us (41%)
  matrix products  169 us (22%)
  other arithmetic  117 us (15%)
  local copies, waits for them, and re-layouts  91.5 us (12%)
  blocking collectives  26.6 us (3%)
  starting transfers between devices  21.1 us (3%)
  between operations  16.7 us (2%)
    unnamed x8, waiting for transfers between devices  154 us
    ppermute x13, waiting for transfers between devices, far(): return lax.ppermute(value, 'tensor', [(i, i ^ 2) for i in range(count)])  107 us
    unnamed x340, local copies, waits for them, and re-layouts  49.8 us
    all_gather x1, waiting for transfers between devices, shards(): lax.all_gather(attn_quarter, ('tensor', 'dp'), axis=0, tiled=True)  38.5 us
    dot_general x14, matrix products, dot(): return jnp.dot(left_side, right_side, preferred_element_type=F32)  30.9 us
    dot_general x10, matrix products, contract_rows(): lax.dot_general(left_side, right_side, (((0,), (0,)), ((), ())), preferre...  28.3 us
    convert_element_type x2, other arithmetic, attend_backward(): grad_scores = (soft_float * (grad_soft - jnp.sum(soft_float * grad_soft,...  27.1 us
    dot_general x2, matrix products, attend_backward(): jnp.einsum('qhgd,shd->hgqs', grad_att, values_all, preferred_element_type...  26 us
  transfers between devices with their start and end apart: 31, of which 16 were waited for; matrix products, arithmetic and copies ran while one was open for 27% of the time, Pallas kernels for 0%

profile of v1, /device:TPU:0, one launch (start us, length us, event | category | flops | bytes accessed | tf_op | source)
XLA Modules:
  0.0 751.4 jit_solution(13870508765482715038)
XLA Ops:
  19.3 20.8 %all-gather = bf16[8,144,2]{1,2,0:T(2,128)(2,1)S(1)} all-gather(bf16[1,144,2]{1,2,0:T(2,128)(2,1)S(1)} %maximum_bitcast_fusion.2), channel_id=1, replica_groups=mesh['dp'=8,'tensor'=4] {'dp'}, dimensions={0}, use_global_device_ids=true | all-gather | bytes 5184 | tf_op jit(solution)/shard_map/all_gather | solution.py:173
  50.0 38.5 %all-gather.4.cloned.1.call-done = bf16[4608,768]{1,0:T(8,128)(2,1)} async-done(((bf16[144,768]{1,0:T(8,128)(2,1)}), bf16[4608,768]{1,0:T(8,128)(2,1)}) %all-gather.4.cloned.1.call-update) | async-done | bytes 7077904 | tf_op jit(solution)/shard_map/all_gather | solution.py:167
  101.4 5.3 fusion.172
  110.3 5.3 copy.155
  129.7 8.1 %fusion.8 = (f32[6,3,256]{2,1,0:T(4,128)S(1)}, f32[6,1024,256,3]{2,1,3,0:T(8,128)}) fusion(pred[256,1024]{0,1:T(8,128)(4,1)S(1)} %get-tuple-element.159, bf16[1024,6,64,1]{0,2,3,1:T(8,128)(2,1)S(1)} %bitcast.398, bf16[256,6,3,64]{0,3,2,1:T(8,128)(2,1)S(1)} %bitcast.402), kind=kOutput, calls=%fused_computation.19 | convolution fusion | flops 618130944 | bytes 20531200 | tf_op jit(solution)/shard_map/qhgd,shd->hgqs/dot_general | solution.py:94
  137.8 10.3 %exponential_reduce_fusion.1 = f32[6,3,256]{2,1,0:T(4,128)S(1)} fusion(f32[6,1024,256,3]{2,1,3,0:T(8,128)} %get-tuple-element.178, f32[6,3,256]{2,1,0:T(4,128)S(1)} %get-tuple-element.177, pred[256,1024]{0,1:T(8,128)(4,1)S(1)} %get-tuple-element.159), kind=kLoop, calls=%fused_computation.15 | loop fusion | flops 18869760 | bytes 19173376 | tf_op jit(solution)/shard_map/reduce_sum | solution.py:104
  148.2 8.9 %convolution_convert_fusion.3 = bf16[6,64,3,256]{3,1,2,0:T(8,128)(2,1)S(1)} fusion(bf16[1024,6,64,1]{0,2,3,1:T(8,128)(2,1)S(1)} %bitcast.410, f32[6,1024,256,3]{2,1,3,0:T(8,128)} %get-tuple-element.178, f32[6,3,256]{2,1,0:T(4,128)S(1)} %log_add_fusion.1, pred[256,1024]{0,1:T(8,128)(4,1)S(1)} %get-tuple-element.159), kind=kOutput, calls=%fused_computation.115 | convolution fusion | flops 623149056 | bytes 20531200 | tf_op jit(solution)/shard_map/hgqs,shd->qhgd/dot_general | solution.py:106
  163.4 10.3 %collective-permute-done.2 = bf16[256,1152]{1,0:T(8,128)(2,1)S(1)} collective-permute-done((bf16[256,1152]{1,0:T(8,128)(2,1)S(1)}, bf16[256,1152]{1,0:T(8,128)(2,1)S(1)}, u32[]{:S(2)}, u32[]{:S(2)}) %collective-permute-start.2) | collective-permute-done | bytes 589856 | tf_op jit(solution)/shard_map/ppermute | solution.py:23
  180.3 8.2 %fusion.9 = (f32[6,3,256]{2,1,0:T(4,128)S(1)}, f32[6,1024,256,3]{2,1,3,0:T(8,128)}) fusion(pred[256,1024]{0,1:T(8,128)(4,1)S(1)} %get-tuple-element.160, bf16[1024,6,64,1]{0,2,3,1:T(8,128)(2,1)S(1)} %bitcast.400, bf16[256,6,3,64]{0,3,2,1:T(8,128)(2,1)S(1)} %bitcast.404), kind=kOutput, calls=%fused_computation.20 | convolution fusion | flops 618130944 | bytes 20531200 | tf_op jit(solution)/shard_map/qhgd,shd->hgqs/dot_general | solution.py:94
  188.6 4.4 fusion.96
  210.8 10.4 %exponential_reduce_fusion = f32[6,3,256]{2,1,0:T(4,128)S(1)} fusion(f32[6,1024,256,3]{2,1,3,0:T(8,128)} %get-tuple-element.182, f32[6,3,256]{2,1,0:T(4,128)S(1)} %get-tuple-element.181, pred[256,1024]{0,1:T(8,128)(4,1)S(1)} %get-tuple-element.160), kind=kLoop, calls=%fused_computation.13 | loop fusion | flops 18869760 | bytes 19173376 | tf_op jit(solution)/shard_map/reduce_sum | solution.py:104
  228.9 8.8 %convolution_convert_fusion.2 = bf16[6,64,3,256]{3,1,2,0:T(8,128)(2,1)S(1)} fusion(bf16[1024,6,64,1]{0,2,3,1:T(8,128)(2,1)S(1)} %bitcast.412, f32[6,1024,256,3]{2,1,3,0:T(8,128)} %get-tuple-element.182, f32[6,3,256]{2,1,0:T(4,128)S(1)} %log_add_fusion, pred[256,1024]{0,1:T(8,128)(4,1)S(1)} %get-tuple-element.160), kind=kOutput, calls=%fused_computation.114 | convolution fusion | flops 623149056 | bytes 20531200 | tf_op jit(solution)/shard_map/hgqs,shd->qhgd/dot_general | solution.py:106
  241.0 12.2 %collective-permute-done.15 = bf16[256,1152]{1,0:T(8,128)(2,1)S(1)} collective-permute-done((bf16[256,1152]{1,0:T(8,128)(2,1)S(1)}, bf16[256,1152]{1,0:T(8,128)(2,1)S(1)}, u32[]{:S(2)}, u32[]{:S(2)}) %collective-permute-start.15) | collective-permute-done | bytes 589856 | tf_op jit(solution)/shard_map/ppermute | solution.py:23
  256.8 13.5 %collective-permute-done.8 = bf16[256,1152]{1,0:T(8,128)(2,1)S(1)} collective-permute-done((bf16[256,1152]{1,0:T(8,128)(2,1)S(1)}, bf16[256,1152]{1,0:T(8,128)(2,1)S(1)}, u32[]{:S(2)}, u32[]{:S(2)}) %collective-permute-start.8) | collective-permute-done | bytes 589856 | tf_op jit(solution)/shard_map/ppermute | solution.py:23
  300.0 12.0 %collective-permute-done.19 = bf16[256,1152]{1,0:T(8,128)(2,1)S(1)} collective-permute-done((bf16[256,1152]{1,0:T(8,128)(2,1)S(1)}, bf16[256,1152]{1,0:T(8,128)(2,1)S(1)}, u32[]{:S(2)}, u32[]{:S(2)}) %collective-permute-start.19) | collective-permute-done | bytes 589856 | tf_op jit(solution)/shard_map/ppermute | solution.py:23
  313.1 10.7 %collective-permute-done.11 = bf16[256,1152]{1,0:T(8,128)(2,1)S(1)} collective-permute-done((bf16[256,1152]{1,0:T(8,128)(2,1)S(1)}, bf16[256,1152]{1,0:T(8,128)(2,1)S(1)}, u32[]{:S(2)}, u32[]{:S(2)}) %collective-permute-start.11) | collective-permute-done | bytes 589856 | tf_op jit(solution)/shard_map/ppermute | solution.py:23
  332.5 10.0 %fusion.132 = f32[6,64,1024,1]{2,1,3,0:T(8,128)} fusion(bf16[256,6,3,64]{0,3,2,1:T(8,128)(2,1)S(1)} %bitcast.414, f32[6,1024,256,3]{2,1,3,0:T(8,128)} %get-tuple-element.182, f32[6,3,256]{2,1,0:T(4,128)S(1)} %log_add_fusion, pred[256,1024]{0,1:T(8,128)(4,1)S(1)} %get-tuple-element.160), kind=kOutput, calls=%fused_computation.296 | convolution fusion | flops 622854144 | bytes 21317632 | tf_op jit(solution)/shard_map/hgqs,qhgd->shd/dot_general | solution.py:117
  342.6 12.7 %fusion = (f32[6,3,256]{2,1,0:T(4,128)S(1)}, f32[6,1024,256,3]{2,1,3,0:T(8,128)}) fusion(f32[6,1024,256,3]{2,1,3,0:T(8,128)} %get-tuple-element.182, f32[6,3,256]{2,1,0:T(4,128)S(1)} %log_add_fusion, pred[256,1024]{0,1:T(8,128)(4,1)S(1)} %get-tuple-element.160, bf16[1024,6,64,1]{0,2,3,1:T(8,128)(2,1)S(1)} %bitcast.413, bf16[256,6,3,64]{0,3,2,1:T(8,128)(2,1)S(1)} %bitcast.415), kind=kOutput, calls=%fused_computation.2 | convolution fusion | flops 627568128 | bytes 39424000 | tf_op jit(solution)/shard_map/qhgd,shd->hgqs/dot_general | solution.py:113
  355.3 13.5 %fusion.2 = bf16[6,3,256,1024]{2,3,1,0:T(8,128)(2,1)S(1)} fusion(f32[6,1024,256,3]{2,1,3,0:T(8,128)} %get-tuple-element.188, f32[6,1024,256,3]{2,1,3,0:T(8,128)} %get-tuple-element.182, f32[6,3,256]{2,1,0:T(4,128)S(1)} %get-tuple-element.187, f32[6,3,256]{2,1,0:T(4,128)S(1)} %log_add_fusion, pred[256,1024]{0,1:T(8,128)(4,1)S(1)} %get-tuple-element.160), kind=kLoop, calls=%fused_computation.4 | loop fusion | flops 28311552 | bytes 47484928 | tf_op jit(solution)/shard_map/convert_element_type | solution.py:116
  375.6 9.0 %fusion.135 = f32[6,64,1024,1]{2,1,3,0:T(8,128)S(1)} fusion(bf16[256,6,3,64]{0,3,2,1:T(8,128)(2,1)} %bitcast.416, f32[6,1024,256,3]{2,1,3,0:T(8,128)} %get-tuple-element.178, f32[6,3,256]{2,1,0:T(4,128)S(1)} %copy-done.124, pred[256,1024]{0,1:T(8,128)(4,1)S(1)} %copy-done.4), kind=kOutput, calls=%fused_computation.297 | convolution fusion | flops 622854144 | bytes 21317632 | tf_op jit(solution)/shard_map/hgqs,qhgd->shd/dot_general | solution.py:117
  384.6 13.3 %fusion.3 = (f32[6,3,256]{2,1,0:T(4,128)S(1)}, f32[6,1024,256,3]{2,1,3,0:T(8,128)}) fusion(f32[6,1024,256,3]{2,1,3,0:T(8,128)} %get-tuple-element.178, f32[6,3,256]{2,1,0:T(4,128)S(1)} %copy-done.124, pred[256,1024]{0,1:T(8,128)(4,1)S(1)} %copy-done.4, bf16[1024,6,64,1]{0,2,3,1:T(8,128)(2,1)S(1)} %bitcast.411, bf16[256,6,3,64]{0,3,2,1:T(8,128)(2,1)S(1)} %bitcast.417), kind=kOutput, calls=%fused_computation.7 | convolution fusion | flops 627568128 | bytes 39424000 | tf_op jit(solution)/shard_map/qhgd,shd->hgqs/dot_general | solution.py:113
  397.9 13.6 %fusion.5 = bf16[6,3,256,1024]{2,3,1,0:T(8,128)(2,1)S(1)} fusion(f32[6,1024,256,3]{2,1,3,0:T(8,128)} %get-tuple-element.186, f32[6,1024,256,3]{2,1,3,0:T(8,128)} %get-tuple-element.178, f32[6,3,256]{2,1,0:T(4,128)S(1)} %get-tuple-element.185, f32[6,3,256]{2,1,0:T(4,128)S(1)} %copy-done.124, pred[256,1024]{0,1:T(8,128)(4,1)S(1)} %copy-done.4), kind=kLoop, calls=%fused_computation.9 | loop fusion | flops 28311552 | bytes 47484928 | tf_op jit(solution)/shard_map/convert_element_type | solution.py:116
  425.6 7.5 collective-permute-done.21
  433.3 7.8 %collective-permute-done.17 = bf16[256,768]{0,1:T(8,128)(2,1)S(1)} collective-permute-done((bf16[256,768]{0,1:T(8,128)(2,1)S(1)}, bf16[256,768]{0,1:T(8,128)(2,1)S(1)}, u32[]{:S(2)}, u32[]{:S(2)}) %collective-permute-start.17) | collective-permute-done | bytes 393248 | tf_op jit(solution)/shard_map/ppermute | solution.py:23
  451.0 6.3 collective-permute-done.22
  461.9 5.6 select_convert_fusion
  480.7 27.2 %collective-permute-done.23 = bf16[1152,768]{0,1:T(8,128)(2,1)} collective-permute-done((bf16[1152,768]{0,1:T(8,128)(2,1)}, bf16[1152,768]{0,1:T(8,128)(2,1)}, u32[]{:S(2)}, u32[]{:S(2)}) %collective-permute-start.23) | collective-permute-done | bytes 1769504 | tf_op jit(solution)/shard_map/ppermute | solution.py:23
  516.4 4.3 fusion.169
  537.0 8.6 %copy.203 = bf16[1152,2304]{1,0:T(8,128)(2,1)} copy(bf16[1152,2304]{0,1:T(8,128)(2,1)} %pad_maximum_fusion) | data formatting | bytes 10616832
  552.8 5.8 psum.8
  558.5 51.6 %reduce-scatter.10.cloned.1.call-done = bf16[144,768]{1,0:T(8,128)(2,1)} async-done(((bf16[1152,768]{1,0:T(8,128)(2,1)}), bf16[144,768]{1,0:T(8,128)(2,1)}) %reduce-scatter.10.cloned.1.call-update) | async-done | bytes 221200
  614.0 102.6 %reduce-scatter.12.cloned.1.call-done = bf16[144,2304]{1,0:T(8,128)(2,1)} async-done(((bf16[1152,2304]{1,0:T(8,128)(2,1)}), bf16[144,2304]{1,0:T(8,128)(2,1)}) %reduce-scatter.12.cloned.1.call-update) | async-done | bytes 663568
  (562 shorter events, 247.6 us)
Async XLA Ops:
  7.2 81.3 %all-gather.4.cloned.1.call-start = ((), (), s32[]{:S(2)}) async-start(), calls=%async_computation.3 | async-start | bytes 7299072 | tf_op jit(solution)/shard_map/all_gather | solution.py:167
  9.2 179.4 %all-gather.6.cloned.1.call-start = ((), (), s32[]{:S(2)}) async-start(), calls=%async_computation.4 | async-start | bytes 5971968 | tf_op jit(solution)/shard_map/all_gather | solution.py:172
  13.8 33.2 %collective-permute-start.12 = (bf16[2,256,1152]{2,1,0:T(8,128)(2,1)}, bf16[2,256,1152]{2,1,0:T(8,128)(2,1)}, u32[]{:S(2)}, u32[]{:S(2)}) collective-permute-start(bf16[2,256,1152]{2,1,0:T(8,128)(2,1)} %get-tuple-element.125), channel_id=1, source_target_pairs={{0,2},{1,3},{2,0},{3,1},{4,6},{5,7},{6,4},{7,5},{8,10},{9,11},{10,... | collective-permute-start | bytes 3538952 | tf_op jit(solution)/shard_map/ppermute | solution.py:23
  17.7 534.1 %reduce-scatter.14.cloned.1.call-start = ((), (), s32[]{:S(2)}) async-start(), calls=%async_computation.7 | async-start | bytes 663552
  42.3 105.9 %copy-start.3 = (pred[256,1024]{0,1:T(8,128)(4,1)}, pred[256,1024]{0,1:T(8,128)(4,1)S(1)}, u32[]{:S(2)}) copy-start(pred[256,1024]{0,1:T(8,128)(4,1)S(1)} %get-tuple-element.159) | copy-start | bytes 786436
  50.0 125.0 %collective-permute-start.13 = (bf16[2,2,256,1152]{3,2,1,0:T(8,128)(2,1)}, bf16[2,2,256,1152]{3,2,1,0:T(8,128)(2,1)}, u32[]{:S(2)}, u32[]{:S(2)}) collective-permute-start(bf16[2,2,256,1152]{3,2,1,0:T(8,128)(2,1)} %pad_maximum_fusion.9), channel_id=1, source_target_pairs={{0,1},{1,0},{2,3},{3,2},{4,5},{5,4},{6,7},{7,6},{8,9},{9,8},{10,11... | collective-permute-start | bytes 7077896 | tf_op jit(solution)/shard_map/ppermute | solution.py:18
  96.8 22.9 %collective-permute-start = (bf16[256,768]{1,0:T(8,128)(2,1)}, bf16[256,768]{1,0:T(8,128)(2,1)}, u32[]{:S(2)}, u32[]{:S(2)}) collective-permute-start(bf16[256,768]{1,0:T(8,128)(2,1)} %pad_maximum_fusion.37), channel_id=1, source_target_pairs={{0,2},{1,3},{2,0},{3,1},{4,6},{5,7},{6,4},{7,5},{8,10},{9,11},{10,... | collective-permute-start | bytes 1179656 | tf_op jit(solution)/shard_map/ppermute | solution.py:23
  100.8 61.5 %collective-permute-start.6 = (bf16[256,768]{1,0:T(8,128)(2,1)}, bf16[256,768]{1,0:T(8,128)(2,1)}, u32[]{:S(2)}, u32[]{:S(2)}) collective-permute-start(bf16[256,768]{1,0:T(8,128)(2,1)} %pad_maximum_fusion.38), channel_id=1, source_target_pairs={{0,2},{1,3},{2,0},{3,1},{4,6},{5,7},{6,4},{7,5},{8,10},{9,11},{10,... | collective-permute-start | bytes 1179656 | tf_op jit(solution)/shard_map/ppermute | solution.py:23
  120.7 2.4 collective-permute-start.1
  158.5 15.2 %collective-permute-start.2 = (bf16[256,1152]{1,0:T(8,128)(2,1)S(1)}, bf16[256,1152]{1,0:T(8,128)(2,1)S(1)}, u32[]{:S(2)}, u32[]{:S(2)}) collective-permute-start(bf16[256,1152]{1,0:T(8,128)(2,1)S(1)} %multiply_convert_fusion.7), channel_id=1, source_target_pairs={{0,2},{1,3},{2,0},{3,1},{4,6},{5,7},{6,4},{7,5},{8,10},{9,11},{10,... | collective-permute-start | bytes 1769480 | tf_op jit(solution)/shard_map/ppermute | solution.py:23
  163.3 14.7 %collective-permute-start.7 = (bf16[512,768]{1,0:T(8,128)(2,1)S(1)}, bf16[512,768]{1,0:T(8,128)(2,1)S(1)}, u32[]{:S(2)}, u32[]{:S(2)}) collective-permute-start(bf16[512,768]{1,0:T(8,128)(2,1)S(1)} %pad_maximum_fusion.26), channel_id=1, source_target_pairs={{0,1},{1,0},{2,3},{3,2},{4,5},{5,4},{6,7},{7,6},{8,9},{9,8},{10,11... | collective-permute-start | bytes 2359304 | tf_op jit(solution)/shard_map/ppermute | solution.py:18
  175.0 13.6 %collective-permute-start.3 = (bf16[512,1152]{1,0:T(8,128)(2,1)}, bf16[512,1152]{1,0:T(8,128)(2,1)}, u32[]{:S(2)}, u32[]{:S(2)}) collective-permute-start(bf16[512,1152]{1,0:T(8,128)(2,1)} %pad_maximum_fusion.18), channel_id=1, source_target_pairs={{0,1},{1,0},{2,3},{3,2},{4,5},{5,4},{6,7},{7,6},{8,9},{9,8},{10,11... | collective-permute-start | bytes 3538952 | tf_op jit(solution)/shard_map/ppermute | solution.py:18
  203.4 19.0 %collective-permute-start.4 = (bf16[512,1152]{1,0:T(8,128)(2,1)}, bf16[512,1152]{1,0:T(8,128)(2,1)}, u32[]{:S(2)}, u32[]{:S(2)}) collective-permute-start(bf16[512,1152]{1,0:T(8,128)(2,1)} %slice.640), channel_id=1, source_target_pairs={{0,1},{1,0},{2,3},{3,2},{4,5},{5,4},{6,7},{7,6},{8,9},{9,8},{10,11... | collective-permute-start | bytes 3538952 | tf_op jit(solution)/shard_map/ppermute | solution.py:18
  210.7 15.5 %collective-permute-start.14 = (bf16[512,1152]{1,0:T(8,128)(2,1)S(1)}, bf16[512,1152]{1,0:T(8,128)(2,1)}, u32[]{:S(2)}, u32[]{:S(2)}) collective-permute-start(bf16[512,1152]{1,0:T(8,128)(2,1)S(1)} %slice.638), channel_id=1, source_target_pairs={{0,1},{1,0},{2,3},{3,2},{4,5},{5,4},{6,7},{7,6},{8,9},{9,8},{10,11... | collective-permute-start | bytes 3538952 | tf_op jit(solution)/shard_map/ppermute | solution.py:18
  224.8 16.2 %collective-permute-start.5 = (bf16[256,1152]{1,0:T(8,128)(2,1)S(1)}, bf16[256,1152]{1,0:T(8,128)(2,1)S(1)}, u32[]{:S(2)}, u32[]{:S(2)}) collective-permute-start(bf16[256,1152]{1,0:T(8,128)(2,1)S(1)} %slice.644), channel_id=1, source_target_pairs={{0,2},{1,3},{2,0},{3,1},{4,6},{5,7},{6,4},{7,5},{8,10},{9,11},{10,... | collective-permute-start | bytes 1769480 | tf_op jit(solution)/shard_map/ppermute | solution.py:23
  227.9 25.3 %collective-permute-start.15 = (bf16[256,1152]{1,0:T(8,128)(2,1)S(1)}, bf16[256,1152]{1,0:T(8,128)(2,1)S(1)}, u32[]{:S(2)}, u32[]{:S(2)}) collective-permute-start(bf16[256,1152]{1,0:T(8,128)(2,1)S(1)} %slice.642), channel_id=1, source_target_pairs={{0,2},{1,3},{2,0},{3,1},{4,6},{5,7},{6,4},{7,5},{8,10},{9,11},{10,... | collective-permute-start | bytes 1769480 | tf_op jit(solution)/shard_map/ppermute | solution.py:23
  255.4 14.9 %collective-permute-start.8 = (bf16[256,1152]{1,0:T(8,128)(2,1)S(1)}, bf16[256,1152]{1,0:T(8,128)(2,1)S(1)}, u32[]{:S(2)}, u32[]{:S(2)}) collective-permute-start(bf16[256,1152]{1,0:T(8,128)(2,1)S(1)} %get-tuple-element.158), channel_id=1, source_target_pairs={{0,2},{1,3},{2,0},{3,1},{4,6},{5,7},{6,4},{7,5},{8,10},{9,11},{10,... | collective-permute-start | bytes 1769480 | tf_op jit(solution)/shard_map/ppermute | solution.py:23
  270.4 2.9 collective-permute-start.9
  286.9 6.4 collective-permute-start.18
  292.9 4.3 collective-permute-start.10
  295.7 16.2 %collective-permute-start.19 = (bf16[256,1152]{1,0:T(8,128)(2,1)S(1)}, bf16[256,1152]{1,0:T(8,128)(2,1)S(1)}, u32[]{:S(2)}, u32[]{:S(2)}) collective-permute-start(bf16[256,1152]{1,0:T(8,128)(2,1)S(1)} %slice.641), channel_id=1, source_target_pairs={{0,2},{1,3},{2,0},{3,1},{4,6},{5,7},{6,4},{7,5},{8,10},{9,11},{10,... | collective-permute-start | bytes 1769480 | tf_op jit(solution)/shard_map/ppermute | solution.py:23
  299.0 24.8 %collective-permute-start.11 = (bf16[256,1152]{1,0:T(8,128)(2,1)S(1)}, bf16[256,1152]{1,0:T(8,128)(2,1)S(1)}, u32[]{:S(2)}, u32[]{:S(2)}) collective-permute-start(bf16[256,1152]{1,0:T(8,128)(2,1)S(1)} %slice.643), channel_id=1, source_target_pairs={{0,2},{1,3},{2,0},{3,1},{4,6},{5,7},{6,4},{7,5},{8,10},{9,11},{10,... | collective-permute-start | bytes 1769480 | tf_op jit(solution)/shard_map/ppermute | solution.py:23
  416.3 4.4 collective-permute-start.20
  416.6 6.0 collective-permute-start.16
  421.1 12.0 %collective-permute-start.21 = (bf16[256,768]{0,1:T(8,128)(2,1)S(1)}, bf16[256,768]{0,1:T(8,128)(2,1)S(1)}, u32[]{:S(2)}, u32[]{:S(2)}) collective-permute-start(bf16[256,768]{0,1:T(8,128)(2,1)S(1)} %slice.645), channel_id=1, source_target_pairs={{0,2},{1,3},{2,0},{3,1},{4,6},{5,7},{6,4},{7,5},{8,10},{9,11},{10,... | collective-permute-start | bytes 1179656 | tf_op jit(solution)/shard_map/ppermute | solution.py:23
  423.6 17.4 %collective-permute-start.17 = (bf16[256,768]{0,1:T(8,128)(2,1)S(1)}, bf16[256,768]{0,1:T(8,128)(2,1)S(1)}, u32[]{:S(2)}, u32[]{:S(2)}) collective-permute-start(bf16[256,768]{0,1:T(8,128)(2,1)S(1)} %slice.646), channel_id=1, source_target_pairs={{0,2},{1,3},{2,0},{3,1},{4,6},{5,7},{6,4},{7,5},{8,10},{9,11},{10,... | collective-permute-start | bytes 1179656 | tf_op jit(solution)/shard_map/ppermute | solution.py:23
  450.9 6.4 collective-permute-start.22
  467.6 40.3 %collective-permute-start.23 = (bf16[1152,768]{0,1:T(8,128)(2,1)}, bf16[1152,768]{0,1:T(8,128)(2,1)}, u32[]{:S(2)}, u32[]{:S(2)}) collective-permute-start(bf16[1152,768]{0,1:T(8,128)(2,1)} %get-tuple-element.80), channel_id=1, source_target_pairs={{0,2},{1,3},{2,0},{3,1},{4,6},{5,7},{6,4},{7,5},{8,10},{9,11},{10,... | collective-permute-start | bytes 5308424 | tf_op jit(solution)/shard_map/ppermute | solution.py:23
  480.7 129.5 %reduce-scatter.10.cloned.1.call-start = ((), (), s32[]{:S(2)}) async-start(), calls=%async_computation.5 | async-start | bytes 1990656
  516.2 200.5 %reduce-scatter.12.cloned.1.call-start = ((), (), s32[]{:S(2)}) async-start(), calls=%async_computation.6 | async-start | bytes 5971968
  612.0 106.4 %collective-permute-start.24 = (bf16[144,768]{0,1:T(8,128)(2,1)}, bf16[144,768]{0,1:T(8,128)(2,1)}, u32[]{:S(2)}, u32[]{:S(2)}) collective-permute-start(bf16[144,768]{0,1:T(8,128)(2,1)} %copy.202), channel_id=1, source_target_pairs={{0,2},{1,3},{2,0},{3,1},{4,6},{5,7},{6,4},{7,5},{8,10},{9,11},{10,... | collective-permute-start | bytes 663560 | tf_op jit(solution)/shard_map/ppermute | solution.py:23
  723.6 8.6 %collective-permute-start.25 = (bf16[2,144,768]{2,1,0:T(8,128)(2,1)}, bf16[2,144,768]{2,1,0:T(8,128)(2,1)}, u32[]{:S(2)}, u32[]{:S(2)}) collective-permute-start(bf16[2,144,768]{2,1,0:T(8,128)(2,1)} %copy.171), channel_id=1, source_target_pairs={{0,1},{1,0},{2,3},{3,2},{4,5},{5,4},{6,7},{7,6},{8,9},{9,8},{10,11... | collective-permute-start | bytes 1327112 | tf_op jit(solution)/shard_map/ppermute | solution.py:18
  (162 other events, 1353.8 us)
Sparse Core Ops, SparseCore 0:
  11.6 76.8 all-gather.3
  91.2 85.6 all-gather.5
  480.8 60.5 reduce-scatter.13
  545.1 64.9 reduce-scatter.9
  613.6 103.0 reduce-scatter.11

commit v2 on v1

v2 whole, which is shorter than its diff:
```python
import functools

import jax
import jax.numpy as jnp
from jax import lax
from jax.experimental import pallas as pl
from jax.experimental.pallas import tpu as pltpu
from jax.sharding import PartitionSpec as P

HEAD_SIZE = 64
EPSILON = 1e-05
ROPE_BASE = 10000.0
MASKED = -1e30
BF16 = jnp.bfloat16
F32 = jnp.float32

BLOCK_XOR = (0, 2, 1, 3)


def near(value):
    count = lax.axis_size("tensor")
    return lax.ppermute(value, "tensor", [(i, i ^ 1) for i in range(count)])


def far(value):
    count = lax.axis_size("tensor")
    return lax.ppermute(value, "tensor", [(i, i ^ 2) for i in range(count)])


def gather_rows(own):
    pair = jnp.concatenate([own, far(own)], axis=0)
    return jnp.concatenate([pair, near(pair)], axis=0)


def scatter_rows(partial):
    half = partial.shape[0] // 2
    quarter = half // 2
    kept = partial[:half].astype(F32) + near(partial[half:].astype(BF16)).astype(F32)
    return kept[:quarter] + far(kept[quarter:].astype(BF16)).astype(F32)


def dot(left_side, right_side):
    return jnp.dot(left_side, right_side, preferred_element_type=F32)


def contract_rows(left_side, right_side):
    return lax.dot_general(
        left_side, right_side, (((0,), (0,)), ((), ())), preferred_element_type=F32
    )


def contract_last(left_side, right_side):
    return lax.dot_general(
        left_side, right_side, (((1,), (1,)), ((), ())), preferred_element_type=F32
    )


def dot_nt(left_side, right_side):
    return lax.dot_general(
        left_side, right_side, (((1,), (1,)), ((), ())), preferred_element_type=F32
    )


def dot_nn(left_side, right_side):
    return lax.dot_general(
        left_side, right_side, (((1,), (0,)), ((), ())), preferred_element_type=F32
    )


def head_of(ref, index):
    return ref[:, index * HEAD_SIZE : (index + 1) * HEAD_SIZE]


def row_scale_of(values):
    return lax.rsqrt(jnp.mean(values * values, axis=-1, keepdims=True) + EPSILON)


def turn(values, cosine, sine):
    lane = lax.broadcasted_iota(jnp.int32, (values.shape[0], 128), 1)
    first_half = lane % HEAD_SIZE < HEAD_SIZE // 2
    parts = []
    for start in range(0, values.shape[1], 128):
        part = values[:, start : start + 128]
        later = pltpu.roll(part, 128 - HEAD_SIZE // 2, 1)
        earlier = pltpu.roll(part, HEAD_SIZE // 2, 1)
        parts.append(part * cosine + jnp.where(first_half, later, earlier) * sine)
    return jnp.concatenate(parts, axis=1)


def project_pairs_kernel(x_ref, gain_ref, cosine_ref, sine_ref, weight_ref, pair_ref, normed_ref):
    @pl.when(pl.program_id(0) == 0)
    def _():
        values = x_ref[...].astype(F32)
        normed_ref[...] = (values * row_scale_of(values) * gain_ref[...]).astype(BF16)

    product = dot_nn(normed_ref[...], weight_ref[...])

    @pl.when(pl.program_id(0) == 0)
    def _():
        pair_ref[...] = turn(product, cosine_ref[...], sine_ref[...]).astype(BF16)

    @pl.when(pl.program_id(0) == 1)
    def _():
        pair_ref[...] = product.astype(BF16)


def project_queries_kernel(normed_ref, cosine_ref, sine_ref, weight_ref, query_ref):
    product = dot_nn(normed_ref[...], weight_ref[...])
    turned = turn(product, cosine_ref[...], sine_ref[...])
    query_ref[...] = (turned * HEAD_SIZE ** (-0.5)).astype(BF16)


def chunk_spec(width, first):
    return pl.BlockSpec(
        (width, width // 3), lambda i: ((first + i) // 2, (first + i) % 2)
    )


def whole(shape):
    return pl.BlockSpec(shape, lambda i: (0,) * len(shape))


def cost(flops, *arrays):
    moved = sum(a.size * a.dtype.itemsize for a in arrays)
    return pl.CostEstimate(flops=int(flops), transcendentals=0, bytes_accessed=int(moved))


def project_pairs(x_rows, gain, cosine, sine, weights):
    rows, width = x_rows.shape
    third = width // 3
    return pl.pallas_call(
        project_pairs_kernel,
        grid=(2,),
        in_specs=[
            whole((rows, width)),
            whole((1, width)),
            whole((rows, 128)),
            whole((rows, 128)),
            chunk_spec(width, 3),
        ],
        out_specs=[pl.BlockSpec((rows, third), lambda i: (0, i)), whole((rows, width))],
        out_shape=[
            jax.ShapeDtypeStruct((rows, 2 * third), BF16),
            jax.ShapeDtypeStruct((rows, width), BF16),
        ],
        compiler_params=pltpu.CompilerParams(vmem_limit_bytes=40 << 20),
        cost_estimate=cost(4 * rows * width * third, x_rows, x_rows),
        name="project_pairs",
    )(x_rows, gain, cosine, sine, weights)


def project_queries(normed, cosine, sine, weights):
    rows, width = normed.shape
    third = width // 3
    return pl.pallas_call(
        project_queries_kernel,
        grid=(3,),
        in_specs=[
            whole((rows, width)),
            whole((rows, 128)),
            whole((rows, 128)),
            chunk_spec(width, 0),
        ],
        out_specs=pl.BlockSpec((rows, third), lambda i: (0, i)),
        out_shape=jax.ShapeDtypeStruct((rows, width), BF16),
        compiler_params=pltpu.CompilerParams(vmem_limit_bytes=40 << 20),
        cost_estimate=cost(6 * rows * width * third, normed, normed, normed),
        name="project_queries",
    )(normed, cosine, sine, weights)


def attend_kernel(group, counts, q_ref, k0, k1, k2, k3, v0, v1, v2, v3, o_ref):
    rows = q_ref.shape[0]
    k_refs, v_refs = (k0, k1, k2, k3), (v0, v1, v2, v3)
    row = lax.broadcasted_iota(jnp.int32, (rows, rows), 0)
    col = lax.broadcasted_iota(jnp.int32, (rows, rows), 1)
    allowed = [jnp.logical_and(col <= row, col < counts[0])]
    allowed += [col < counts[j] for j in range(1, 4)]
    allowed = [jnp.concatenate([a] * group, axis=0) for a in allowed]
    for pair in range(2):
        queries = jnp.concatenate([head_of(q_ref, pair * group + i) for i in range(group)], axis=0)
        scores = [
            jnp.where(allowed[j], dot_nt(queries, head_of(k_refs[j], pair)), MASKED)
            for j in range(4)
        ]
        top = functools.reduce(
            jnp.maximum, [jnp.max(s, axis=1, keepdims=True) for s in scores]
        )
        soft = [jnp.exp(s - top) for s in scores]
        total = functools.reduce(jnp.add, [jnp.sum(s, axis=1, keepdims=True) for s in soft])
        out = functools.reduce(
            jnp.add, [dot_nn(soft[j].astype(BF16), head_of(v_refs[j], pair)) for j in range(4)]
        )
        out = (out / total).astype(BF16)
        for i in range(group):
            start = (pair * group + i) * HEAD_SIZE
            o_ref[:, start : start + HEAD_SIZE] = out[i * rows : (i + 1) * rows]


def attend(counts, queries, pairs):
    rows, width = queries.shape
    key_heads = pairs[0].shape[1] // (2 * HEAD_SIZE)
    group = width // HEAD_SIZE // key_heads
    steps = key_heads // 2
    query_spec = pl.BlockSpec((rows, 2 * group * HEAD_SIZE), lambda i, c: (0, i))
    key_spec = pl.BlockSpec((rows, 2 * HEAD_SIZE), lambda i, c: (0, i))
    value_spec = pl.BlockSpec((rows, 2 * HEAD_SIZE), lambda i, c: (0, steps + i))
    return pl.pallas_call(
        functools.partial(attend_kernel, group),
        grid_spec=pltpu.PrefetchScalarGridSpec(
            num_scalar_prefetch=1,
            grid=(steps,),
            in_specs=[query_spec] + [key_spec] * 4 + [value_spec] * 4,
            out_specs=query_spec,
        ),
        out_shape=jax.ShapeDtypeStruct((rows, width), BF16),
        compiler_params=pltpu.CompilerParams(vmem_limit_bytes=48 << 20),
        cost_estimate=cost(4 * rows * 4 * rows * width, queries, queries, *pairs),
        name="attend",
    )(counts, queries, *pairs, *pairs)


def attend_back_kernel(
    group, counts, q_ref, g_ref, cos_ref, sin_ref,
    k0, k1, k2, k3, v0, v1, v2, v3, dq_ref, dk_ref, dv_ref, turned_ref,
):
    rows = q_ref.shape[0]
    half = HEAD_SIZE // 2
    keys = jnp.concatenate([k0[...], k1[...], k2[...], k3[...]], axis=0)
    values = jnp.concatenate([v0[...], v1[...], v2[...], v3[...]], axis=0)
    keys_t = keys.T
    row = lax.broadcasted_iota(jnp.int32, (rows, rows), 0)
    col = lax.broadcasted_iota(jnp.int32, (rows, rows), 1)
    allowed = [jnp.logical_and(row <= col, row < counts[0])]
    allowed += [row < counts[j] for j in range(1, 4)]
    allowed = jnp.concatenate([jnp.concatenate([a] * group, axis=1) for a in allowed], axis=0)
    key_grads, value_grads = [], []
    for pair in range(2):
        lanes = slice(pair * HEAD_SIZE, (pair + 1) * HEAD_SIZE)
        key, value = keys[:, lanes], values[:, lanes]
        queries = jnp.concatenate([head_of(q_ref, pair * group + i) for i in range(group)], axis=0)
        grads = jnp.concatenate([head_of(g_ref, pair * group + i) for i in range(group)], axis=0)
        scores = jnp.where(allowed, dot_nt(key, queries), MASKED)
        soft = jnp.exp(scores - jnp.max(scores, axis=0, keepdims=True))
        soft = soft * (1.0 / jnp.sum(soft, axis=0, keepdims=True))
        grad_soft = dot_nt(value, grads)
        both = soft * grad_soft
        grad_scores = (both - soft * jnp.sum(both, axis=0, keepdims=True)).astype(BF16)
        value_grads.append(dot_nn(soft.astype(BF16), grads))
        key_grads.append(dot_nn(grad_scores, queries))
        query_grad = dot_nn(keys_t[lanes, :], grad_scores) * HEAD_SIZE ** (-0.5)
        for i in range(group):
            part = query_grad[:, i * rows : (i + 1) * rows]
            first, second = part[:half], part[half:]
            start = (pair * group + i) * HEAD_SIZE
            turned_ref[start : start + half, :] = first * cos_ref[...] + second * sin_ref[...]
            turned_ref[start + half : start + HEAD_SIZE, :] = (
                second * cos_ref[...] - first * sin_ref[...]
            )
    dk_ref[...] = jnp.concatenate(key_grads, axis=1).astype(BF16)
    dv_ref[...] = jnp.concatenate(value_grads, axis=1).astype(BF16)
    dq_ref[...] = turned_ref[...].T.astype(BF16)


def attend_back(counts, queries, grads, cosine_t, sine_t, pairs):
    rows, width = queries.shape
    key_width = pairs[0].shape[1] // 2
    key_heads = key_width // HEAD_SIZE
    group = width // HEAD_SIZE // key_heads
    steps = key_heads // 2
    query_spec = pl.BlockSpec((rows, 2 * group * HEAD_SIZE), lambda i, c: (0, i))
    key_spec = pl.BlockSpec((rows, 2 * HEAD_SIZE), lambda i, c: (0, i))
    value_spec = pl.BlockSpec((rows, 2 * HEAD_SIZE), lambda i, c: (0, steps + i))
    table_spec = pl.BlockSpec(cosine_t.shape, lambda i, c: (0, 0))
    out_spec = pl.BlockSpec((4 * rows, 2 * HEAD_SIZE), lambda i, c: (0, i))
    return pl.pallas_call(
        functools.partial(attend_back_kernel, group),
        grid_spec=pltpu.PrefetchScalarGridSpec(
            num_scalar_prefetch=1,
            grid=(steps,),
            in_specs=[query_spec, query_spec, table_spec, table_spec]
            + [key_spec] * 4
            + [value_spec] * 4,
            out_specs=[query_spec, out_spec, out_spec],
            scratch_shapes=[pltpu.VMEM((2 * group * HEAD_SIZE, rows), F32)],
        ),
        out_shape=[
            jax.ShapeDtypeStruct((rows, width), BF16),
            jax.ShapeDtypeStruct((4 * rows, key_width), BF16),
            jax.ShapeDtypeStruct((4 * rows, key_width), BF16),
        ],
        compiler_params=pltpu.CompilerParams(vmem_limit_bytes=56 << 20),
        cost_estimate=cost(10 * rows * 4 * rows * width, queries, grads, queries, *pairs),
        name="attend_back",
    )(counts, queries, grads, cosine_t, sine_t, *pairs, *pairs)


def leave_kernel(x_ref, o_ref, gain_ref, w0, w1, w2, middle_ref, normed_ref):
    out = o_ref[...]
    added = jnp.concatenate([dot_nn(out, w[...]) for w in (w0, w1, w2)], axis=1)
    middle = x_ref[...].astype(F32) + added
    middle_ref[...] = middle
    normed_ref[...] = (middle * row_scale_of(middle) * gain_ref[...]).astype(BF16)


def out_specs_of(width):
    return [
        pl.BlockSpec((width, width // 3), lambda i, c=c: (c // 2, c % 2)) for c in (5, 6, 7)
    ]


def leave(x_rows, attended, gain, weights):
    rows, width = x_rows.shape
    return pl.pallas_call(
        leave_kernel,
        grid=(1,),
        in_specs=[whole((rows, width)), whole((rows, width)), whole((1, width))]
        + out_specs_of(width),
        out_specs=[whole((rows, width)), whole((rows, width))],
        out_shape=[
            jax.ShapeDtypeStruct((rows, width), F32),
            jax.ShapeDtypeStruct((rows, width), BF16),
        ],
        compiler_params=pltpu.CompilerParams(vmem_limit_bytes=40 << 20),
        cost_estimate=cost(2 * rows * width * width, x_rows, x_rows, x_rows),
        name="leave",
    )(x_rows, attended, gain, weights, weights, weights)


def enter_kernel(
    count, kept_ref, came_ref, middle_ref, cot_ref, gain_ref, w0, w1, w2,
    grad_middle_ref, branch_ref, out_ref, gain_grad_ref,
):
    rows, width = middle_ref.shape
    third = width // 3
    middle = middle_ref[...]
    grad_normed = kept_ref[...] + came_ref[...].astype(F32)
    scale = row_scale_of(middle)
    row = lax.broadcasted_iota(jnp.int32, (rows, width), 0)
    grad_row = jnp.where(row < count[0], cot_ref[...].astype(F32), 0.0)
    gain_grad = jnp.sum(grad_normed * middle * scale, axis=0, keepdims=True)
    gain_grad_ref[...] = jnp.broadcast_to(gain_grad, gain_grad_ref.shape)
    inner = grad_normed * gain_ref[...]
    grad_middle = grad_row + (
        scale * inner - middle * scale**3 * jnp.mean(inner * middle, axis=-1, keepdims=True)
    )
    grad_middle_ref[...] = grad_middle
    branch = grad_middle.astype(BF16)
    branch_ref[...] = branch
    weights = (w0, w1, w2)
    out = dot_nt(branch[:, :third], w0[...])
    for c in range(1, 3):
        out = out + dot_nt(branch[:, c * third : (c + 1) * third], weights[c][...])
    out_ref[...] = out.astype(BF16)


def enter(count, kept, came, middle, cot_rows, gain, weights):
    rows, width = middle.shape

    def spec(shape, block=(0, 0)):
        return pl.BlockSpec(shape, lambda i, c: block)

    full = spec((rows, width))
    weight_specs = [spec((width, width // 3), (c // 2, c % 2)) for c in (5, 6, 7)]
    return pl.pallas_call(
        enter_kernel,
        grid_spec=pltpu.PrefetchScalarGridSpec(
            num_scalar_prefetch=1,
            grid=(1,),
            in_specs=[full] * 4 + [spec((1, width))] + weight_specs,
            out_specs=[full, full, full, spec((8, width))],
        ),
        out_shape=[
            jax.ShapeDtypeStruct((rows, width), F32),
            jax.ShapeDtypeStruct((rows, width), BF16),
            jax.ShapeDtypeStruct((rows, width), BF16),
            jax.ShapeDtypeStruct((8, width), F32),
        ],
        compiler_params=pltpu.CompilerParams(vmem_limit_bytes=48 << 20),
        cost_estimate=cost(2 * rows * width * width, kept, middle, middle, cot_rows),
        name="enter",
    )(count, kept, came, middle, cot_rows, gain, weights, weights, weights)


def pairs_back_kernel(kept_ref, came_ref, cosine_ref, sine_ref, pair_ref):
    width = kept_ref.shape[1] // 2
    total = kept_ref[...].astype(F32) + came_ref[...].astype(F32)
    pair_ref[:, :width] = turn(total[:, :width], cosine_ref[...], -sine_ref[...]).astype(BF16)
    pair_ref[:, width:] = total[:, width:].astype(BF16)


def pairs_back(kept, came, cosine, sine):
    rows, width = kept.shape
    return pl.pallas_call(
        pairs_back_kernel,
        grid=(1,),
        in_specs=[whole((rows, width))] * 2 + [whole((rows, 128))] * 2,
        out_specs=whole((rows, width)),
        out_shape=jax.ShapeDtypeStruct((rows, width), BF16),
        cost_estimate=cost(0, kept, came, came),
        name="pairs_back",
    )(kept, came, cosine, sine)


def finish_kernel(
    x_ref, query_ref, pair_ref, middle_ref, gain_ref, w0, w1, w2, w3, w4, grad_ref, gain_grad_ref
):
    rows, width = x_ref.shape
    third = width // 3
    weights = (w0, w1, w2, w3, w4)
    grads = [query_ref[:, c * third : (c + 1) * third] for c in range(3)]
    grads += [pair_ref[:, :third], pair_ref[:, third:]]
    grad_normed = dot_nt(grads[0], w0[...])
    for c in range(1, 5):
        grad_normed = grad_normed + dot_nt(grads[c], weights[c][...])
    values = x_ref[...].astype(F32)
    scale = row_scale_of(values)
    gain_grad = jnp.sum(grad_normed * values * scale, axis=0, keepdims=True)
    gain_grad_ref[...] = jnp.broadcast_to(gain_grad, gain_grad_ref.shape)
    inner = grad_normed * gain_ref[...]
    grad_ref[...] = (
        middle_ref[...]
        + scale * inner
        - values * scale**3 * jnp.mean(inner * values, axis=-1, keepdims=True)
    ).astype(BF16)


def finish(x_rows, query_grads, pair_grads, grad_middle, gain, weights):
    rows, width = x_rows.shape
    weight_specs = [
        pl.BlockSpec((width, width // 3), lambda i, c=c: (c // 2, c % 2)) for c in range(5)
    ]
    return pl.pallas_call(
        finish_kernel,
        grid=(1,),
        in_specs=[
            whole((rows, width)),
            whole((rows, width)),
            whole(pair_grads.shape),
            whole((rows, width)),
            whole((1, width)),
        ]
        + weight_specs,
        out_specs=[whole((rows, width)), whole((8, width))],
        out_shape=[
            jax.ShapeDtypeStruct((rows, width), BF16),
            jax.ShapeDtypeStruct((8, width), F32),
        ],
        compiler_params=pltpu.CompilerParams(vmem_limit_bytes=48 << 20),
        cost_estimate=cost(10 * rows * width * width // 3, x_rows, query_grads, grad_middle),
        name="finish",
    )(x_rows, query_grads, pair_grads, grad_middle, gain, *([weights] * 5))


def shards(
    inputs,
    lengths,
    gain_attn,
    gain_mlp,
    w_query,
    key_weight,
    value_weight,
    w_gate,
    w_up,
    w_out,
    w_down,
    cotangent,
):
    micro = inputs.shape[0]
    row_share = inputs.shape[2]
    width = inputs.shape[3]
    tensor_count = lax.axis_size("tensor")
    tensor_index = lax.axis_index("tensor")
    query_width = w_query.shape[1]
    key_width = key_weight.shape[1]
    hidden_share = w_gate.shape[1]

    attn_local = jnp.concatenate([w_query, key_weight, value_weight, w_out], axis=1)
    attn_width = attn_local.shape[1]
    block_width = attn_width // tensor_count
    attn_quarter = lax.dynamic_slice_in_dim(attn_local, tensor_index * block_width, block_width, 1)
    attn_w = lax.all_gather(attn_quarter, ("tensor", "dp"), axis=0, tiled=True)
    mlp_local = jnp.concatenate([w_gate, w_up, w_down.T], axis=1)
    mlp_full = lax.all_gather(mlp_local, "dp", axis=0, tiled=True)
    gains = lax.all_gather(jnp.stack([gain_attn, gain_mlp]), "dp", axis=1, tiled=True).astype(F32)
    gain_one, gain_two = gains[0:1], gains[1:2]
    full_gate = mlp_full[:, :hidden_share]
    full_up = mlp_full[:, hidden_share : 2 * hidden_share]
    full_down_t = mlp_full[:, 2 * hidden_share :]

    query_pos = tensor_index * row_share + jnp.arange(row_share, dtype=jnp.int32)
    exponent = jnp.arange(HEAD_SIZE // 2, dtype=F32) * (2.0 / HEAD_SIZE)
    angles = query_pos.astype(F32)[:, None] * (ROPE_BASE ** (-exponent))[None, :]
    cosine, sine = jnp.cos(angles), jnp.sin(angles)
    cosine_t, sine_t = cosine.T, sine.T
    cosine = jnp.concatenate([cosine] * 4, axis=1)
    sine = jnp.concatenate([-sine, sine, -sine, sine], axis=1)

    def counts_of(b):
        counts = []
        for x in BLOCK_XOR:
            block = tensor_index ^ x
            count = jnp.clip(lengths[b, 0] - block * row_share, 0, row_share)
            counts.append(jnp.where(block <= tensor_index, count, 0))
        return jnp.stack(counts).astype(jnp.int32)

    counts = [counts_of(b) for b in range(micro)]
    valid_rows = [
        jnp.clip(lengths[b, 0] - tensor_index * row_share, 0, row_share).astype(jnp.int32)
        for b in range(micro)
    ]
    valids = [
        (jnp.arange(row_share, dtype=jnp.int32) < valid_rows[b])[:, None] for b in range(micro)
    ]

    grad_own = jnp.stack(
        [jnp.where(valids[b], cotangent[b, 0], jnp.zeros((), BF16)) for b in range(micro)]
    )
    grad_far = far(grad_own)
    grad_near = near(jnp.stack([grad_own, grad_far]))
    grad_ffn = [
        jnp.concatenate([grad_own[b], grad_far[b], grad_near[0, b], grad_near[1, b]], axis=0)
        for b in range(micro)
    ]

    x_rows = inputs[:, 0].reshape(micro * row_share, width)
    cosine_all = jnp.concatenate([cosine] * micro, axis=0)
    sine_all = jnp.concatenate([sine] * micro, axis=0)
    pairs_own, normed = project_pairs(x_rows, gain_one, cosine_all, sine_all, attn_w)
    queries = project_queries(normed, cosine_all, sine_all, attn_w)
    kept = []
    for b in range(micro):
        rows = slice(b * row_share, (b + 1) * row_share)
        own = pairs_own[rows]
        across = far(own)
        pairs = [own, across, near(own), near(across)]
        attended = attend(counts[b], queries[rows], pairs)
        middle, hidden_own = leave(x_rows[rows], attended, gain_two, attn_w)
        kept.append(
            dict(
                x_rows=x_rows[rows],
                normed=normed[rows],
                queries=queries[rows],
                pairs=pairs,
                attended=attended,
                middle=middle,
                hidden=gather_rows(hidden_own),
            )
        )

    for b in range(micro):
        k = kept[b]
        gate_proj = dot(k["hidden"], full_gate)
        up_proj = dot(k["hidden"], full_up)
        grad_act = dot(grad_ffn[b], full_down_t)
        sigmoid_gate = jax.nn.sigmoid(gate_proj)
        k["activated"] = (gate_proj * sigmoid_gate * up_proj).astype(BF16)
        k["grad_gate"] = (
            grad_act * up_proj * sigmoid_gate * (1.0 + gate_proj * (1.0 - sigmoid_gate))
        ).astype(BF16)
        k["grad_up"] = (grad_act * gate_proj * sigmoid_gate).astype(BF16)
        grad_partial = contract_last(k["grad_gate"], full_gate) + contract_last(
            k["grad_up"], full_up
        )
        half = 2 * row_share
        summed = grad_partial[:half] + near(grad_partial[half:].astype(BF16)).astype(F32)
        k["normed_kept"] = summed[:row_share]
        k["normed_came"] = far(summed[row_share:].astype(BF16))

    def total(left_side, right_side):
        parts = [contract_rows(left_side(b), right_side(b)) for b in range(micro)]
        return sum(parts[1:], parts[0])

    grad_mlp_w = jnp.concatenate(
        [
            total(lambda b: kept[b]["hidden"], lambda b: kept[b]["grad_gate"]).astype(BF16),
            total(lambda b: kept[b]["hidden"], lambda b: kept[b]["grad_up"]).astype(BF16),
            total(lambda b: grad_ffn[b], lambda b: kept[b]["activated"]).astype(BF16),
        ],
        axis=1,
    )
    grad_mlp_w, kept[0]["middle"] = lax.optimization_barrier((grad_mlp_w, kept[0]["middle"]))
    grad_mlp_w = lax.psum_scatter(grad_mlp_w, "dp", scatter_dimension=0, tiled=True)

    gain_two_grads = []
    for b in range(micro):
        k = kept[b]
        k["grad_middle"], k["grad_branch"], grad_att, gain_two_grad = enter(
            valid_rows[b][None],
            k["normed_kept"],
            k["normed_came"],
            k["middle"],
            cotangent[b, 0],
            gain_two,
            attn_w,
        )
        gain_two_grads.append(gain_two_grad[0:1])
        k["grad_queries"], key_part, value_part = attend_back(
            counts[b], k["queries"], grad_att, cosine_t, sine_t, k["pairs"]
        )
        half = 2 * row_share
        came = near(jnp.concatenate([key_part[half:], value_part[half:]], axis=1))
        summed = jnp.concatenate([key_part[:half], value_part[:half]], axis=1).astype(
            F32
        ) + came.astype(F32)
        k["grad_pairs"] = pairs_back(
            summed[:row_share], far(summed[row_share:].astype(BF16)), cosine, sine
        )

    outputs, input_grads, gain_one_grads = [], [], []
    for b in range(micro):
        k = kept[b]
        input_grad, gain_one_grad = finish(
            k["x_rows"], k["grad_queries"], k["grad_pairs"], k["grad_middle"], gain_one, attn_w
        )
        gain_one_grads.append(gain_one_grad[0:1])
        input_grads.append(input_grad)
        ffn_out = scatter_rows(contract_last(k["activated"], full_down_t))
        outputs.append(jnp.where(valids[b], k["middle"] + ffn_out, 0.0).astype(BF16))

    gain_part = jnp.concatenate(
        [sum(gain_one_grads[1:], gain_one_grads[0]), sum(gain_two_grads[1:], gain_two_grads[0])],
        axis=0,
    )
    gain_part = jnp.pad(gain_part.T, ((0, 0), (0, 126))).astype(BF16)
    third = key_width

    def pick(flag, first, second):
        return jnp.where(flag, first, second)

    odd = (tensor_index & 1) == 1
    high = (tensor_index & 2) == 2

    def halves(flag):
        low_block, left, right = [], [], []
        for b in range(micro):
            k = kept[b]
            grads = jnp.concatenate([k["grad_queries"], k["grad_pairs"]], axis=1)
            low_block.append(
                contract_rows(
                    k["normed"],
                    pick(flag, grads[:, block_width : 2 * block_width], grads[:, :block_width]),
                )
            )
            left.append(
                contract_rows(
                    pick(flag, k["attended"], k["normed"]),
                    pick(flag, k["grad_branch"][:, third : 2 * third], k["grad_pairs"][:, third:]),
                )
            )
            right.append(
                contract_rows(
                    k["attended"],
                    pick(flag, k["grad_branch"][:, 2 * third :], k["grad_branch"][:, :third]),
                )
            )
        left, right = sum(left[1:], left[0]), sum(right[1:], right[0])
        return jnp.stack(
            [
                sum(low_block[1:], low_block[0]).astype(BF16),
                jnp.concatenate([left, right], axis=1).astype(BF16),
            ]
        )

    summed = halves(odd).astype(F32) + near(halves(jnp.logical_not(odd))).astype(F32)
    came = far(pick(high, summed[0], summed[1]).astype(BF16)).astype(F32)
    quarter = (pick(high, summed[1], summed[0]) + came).astype(BF16)
    quarter = jnp.concatenate([quarter, gain_part], axis=1)
    quarter, grad_mlp_w = lax.optimization_barrier((quarter, grad_mlp_w))
    quarter = lax.psum_scatter(quarter, "dp", scatter_dimension=0, tiled=True)
    other = far(quarter)
    pair = jnp.stack([pick(high, other, quarter), pick(high, quarter, other)])
    other = near(pair)
    even_pair, odd_pair = pick(odd, other, pair), pick(odd, pair, other)
    blocks = [even_pair[0], odd_pair[0], even_pair[1], odd_pair[1]]
    grad_attn = jnp.concatenate([p[:, :block_width] for p in blocks], axis=1).astype(F32)
    gain_sum = sum(p[:, block_width : block_width + 2].astype(F32) for p in blocks)
    grad_mlp_w = grad_mlp_w.astype(F32)
    return (
        jnp.stack(outputs)[:, None],
        jnp.stack(input_grads)[:, None],
        gain_sum[:, 0],
        gain_sum[:, 1],
        grad_attn[:, :query_width],
        grad_attn[:, query_width : query_width + key_width],
        grad_attn[:, query_width + key_width : query_width + 2 * key_width],
        grad_mlp_w[:, :hidden_share],
        grad_mlp_w[:, hidden_share : 2 * hidden_share],
        grad_attn[:, query_width + 2 * key_width :],
        grad_mlp_w[:, 2 * hidden_share :].T,
    )


def solution(mesh):
    in_specs = (
        P(None, "dp", "tensor", None),
        P(None, "dp"),
        P("dp"),
        P("dp"),
        P("dp", None),
        P("dp", None),
        P("dp", None),
        P("dp", "tensor"),
        P("dp", "tensor"),
        P("dp", None),
        P("tensor", "dp"),
        P(None, "dp", "tensor", None),
    )
    out_specs = (
        P(None, "dp", "tensor", None),
        P(None, "dp", "tensor", None),
        P("dp"),
        P("dp"),
        P("dp", None),
        P("dp", None),
        P("dp", None),
        P("dp", "tensor"),
        P("dp", "tensor"),
        P("dp", None),
        P("tensor", "dp"),
    )
    return jax.shard_map(shards, mesh=mesh, in_specs=in_specs, out_specs=out_specs, check_vma=False)
```

time: 762 us -> 593 us (0.78)
  Pallas kernels: 0 us -> 92.5 us
  matrix products: 169 us -> 77.1 us
  other arithmetic: 117 us -> 38.6 us
  waiting for transfers between devices: 309 us -> 262 us
  local copies, waits for them, and re-layouts: 91.5 us -> 56.5 us
    unnamed x8 -> x6, waiting for transfers between devices: 154 us -> 42.1 us
    pallas_call x0 -> x14, Pallas kernels: none -> 92.5 us  [the longest x2 38.1 us: attend_back(): pl.pallas_call(functools.partial(attend_back_kernel, group), grid_spec=pl...]
    dot_general x12 -> x0, matrix products: 88.2 us -> none  [the longest x2 26 us: attend_backward(): jnp.einsum('qhgd,shd->hgqs', grad_att, values_all, preferred_element_type...]
    all_gather x1, waiting for transfers between devices: 0.02 us -> 80.5 us  [shards(): mlp_full = lax.all_gather(mlp_local, 'dp', axis=0, tiled=True)]
    convert_element_type x15 -> x5, other arithmetic: 45 us -> 4.09 us  [the longest x1 1.94 us: shards(): quarter = (pick(high, summed[1], summed[0]) + came).astype(BF16)]
    reduce_sum x5 -> x0, other arithmetic: 24.2 us -> none  [the longest x2 20.7 us: attend(): jnp.sum(jnp.exp(scores - maxima), axis=-1, keepdims=True)]
    unnamed x340 -> x186, local copies, waits for them, and re-layouts: 49.8 us -> 32.3 us
    ppermute x13 -> x15, waiting for transfers between devices: 9.34 us -> 0.87 us  [near(): return lax.ppermute(value, 'tensor', [(i, i ^ 1) for i in range(count)])]
  transfers between devices with their start and end apart: 31 -> 32, of which waited for: 16 -> 16; matrix products, arithmetic and copies ran while one was open for 27% -> 25% of each run, Pallas kernels for 0% -> 16%
where the time goes in v2:
time: 593 us; the launch traced here: 589 us
  waiting for transfers between devices  262 us (44%)
  Pallas kernels  92.5 us (16%)
  matrix products  77.1 us (13%)
  local copies, waits for them, and re-layouts  56.5 us (10%)
  other arithmetic  38.6 us (7%)
  between operations  20.9 us (4%)
  blocking collectives  20.8 us (4%)
  starting transfers between devices  20.4 us (3%)
    ppermute x13, waiting for transfers between devices, far(): return lax.ppermute(value, 'tensor', [(i, i ^ 2) for i in range(count)])  107 us
    all_gather x1, waiting for transfers between devices, shards(): mlp_full = lax.all_gather(mlp_local, 'dp', axis=0, tiled=True)  80.5 us
    unnamed x6, waiting for transfers between devices  42.1 us
    pallas_call x2, Pallas kernels, attend_back(): pl.pallas_call(functools.partial(attend_back_kernel, group), grid_spec=pl...  38.1 us
    unnamed x186, local copies, waits for them, and re-layouts  32.3 us
    dot_general x18, matrix products, contract_rows(): lax.dot_general(left_side, right_side, (((0,), (0,)), ((), ())), preferre...  31.7 us
    all_gather x1, waiting for transfers between devices, shards(): attn_w = lax.all_gather(attn_quarter, ('tensor', 'dp'), axis=0, tiled=True)  31.3 us
    dot_general x6, matrix products, dot(): return jnp.dot(left_side, right_side, preferred_element_type=F32)  28.2 us
  transfers between devices with their start and end apart: 32, of which 16 were waited for; matrix products, arithmetic and copies ran while one was open for 25% of the time, Pallas kernels for 16%

profile of v2, /device:TPU:0, one launch (start us, length us, event | category | flops | bytes accessed | tf_op | source)
XLA Modules:
  0.0 588.8 jit_solution(9922136107876681030)
XLA Ops:
  17.7 20.8 %all-gather = bf16[8,144,2]{1,2,0:T(2,128)(2,1)S(1)} all-gather(bf16[1,144,2]{1,2,0:T(2,128)(2,1)S(1)} %maximum_bitcast_fusion.3), channel_id=1, replica_groups=mesh['dp'=8,'tensor'=4] {'dp'}, dimensions={0}, use_global_device_ids=true | all-gather | bytes 5184 | tf_op jit(solution)/shard_map/all_gather | solution.py:485
  43.8 4.2 collective-permute-done.5
  57.7 31.3 %all-gather.4.cloned.1.call-done.weight_ref.w0.w1.w2.w3.w4 = bf16[4608,768]{1,0:T(8,128)(2,1)} async-done(((bf16[144,768]{1,0:T(8,128)(2,1)}), bf16[4608,768]{1,0:T(8,128)(2,1)}) %all-gather.4.cloned.1.call-update) | async-done | bytes 7077904 | tf_op jit(solution)/shard_map/all_gather | solution.py:482
  96.9 80.5 %all-gather.6.cloned.1.call-done = bf16[1152,2304]{1,0:T(8,128)(2,1)} async-done(((bf16[144,2304]{1,0:T(8,128)(2,1)}), bf16[1152,2304]{1,0:T(8,128)(2,1)}) %all-gather.6.cloned.1.call-update) | async-done | bytes 5308432 | tf_op jit(solution)/shard_map/all_gather | solution.py:484
  177.4 6.2 %fusion.43 = f32[1024,768]{1,0:T(8,128)} fusion(bf16[1152,2304]{1,0:T(8,128)(2,1)} %all-gather.6.cloned.1.call-done, bf16[256,1152]{1,0:T(8,128)(2,1)} %get-tuple-element.118, bf16[256,1152]{1,0:T(8,128)(2,1)} %get-tuple-element.119, bf16[256,1152]{1,0:T(8,128)(2,1)} %get-tuple-element.132, bf16[256,1152]{1,0:T(8,128)(2,1)} %get-tuple-element.130), kind=kOutput, calls=%fused_computation.93 | convolution fusion | flops 1821376512 | bytes 7274496 | tf_op jit(solution)/shard_map/dot_general | solution.py:43
  185.3 3.9 project_queries.1
  189.7 5.4 collective-permute-done.k1.v1
  195.1 12.1 %attend.3.o_ref = bf16[256,1152]{1,0:T(8,128)(2,1)S(1)} custom-call(s32[4]{0:T(128)S(1)} %pad_add_fusion.1.counts, bf16[256,1152]{1,0:T(8,128)(2,1)S(1)} %get-tuple-element.134.q_ref, bf16[256,768]{1,0:T(8,128)(2,1)S(1)} %get-tuple-element.156.k0.v0, bf16[256,768]{1,0:T(8,128)(2,1)} %collective-permute-done.7.k1.v1, ...), custom_call_target="tpu_custom_call" | custom-call | flops 1207959552 | bytes 2752512 | tf_op jit(solution)/shard_map/attend/pallas_call | solution.py:208
  210.2 5.3 fusion.45
  215.6 11.9 %attend.2.o_ref = bf16[256,1152]{1,0:T(8,128)(2,1)S(1)} custom-call(s32[4]{0:T(128)S(1)} %pad_add_fusion.counts, bf16[256,1152]{1,0:T(8,128)(2,1)S(1)} %get-tuple-element.133.q_ref, bf16[256,768]{1,0:T(8,128)(2,1)S(1)} %get-tuple-element.155.k0.v0, bf16[256,768]{1,0:T(8,128)(2,1)S(1)} %collective-permute-done.k1.v1, ...), custom_call_target="tpu_custom_call" | custom-call | flops 1207959552 | bytes 2752512 | tf_op jit(solution)/shard_map/attend/pallas_call | solution.py:208
  229.9 14.5 %collective-permute-done.3 = bf16[256,1152]{1,0:T(8,128)(2,1)S(1)} collective-permute-done((bf16[256,1152]{1,0:T(8,128)(2,1)S(1)}, bf16[256,1152]{1,0:T(8,128)(2,1)S(1)}, u32[]{:S(2)}, u32[]{:S(2)}) %collective-permute-start.3) | collective-permute-done | bytes 589856 | tf_op jit(solution)/shard_map/ppermute | solution.py:27
  248.8 4.6 multiply_convert_fusion.4
  261.2 4.1 fusion.135
  265.3 4.1 fusion.59
  272.0 5.8 multiply_convert_fusion.5
  286.1 4.4 fusion.4
  299.9 13.0 %collective-permute-done.21.came_ref = bf16[256,1152]{1,0:T(8,128)(2,1)S(1)} collective-permute-done((bf16[256,1152]{1,0:T(8,128)(2,1)S(1)}, bf16[256,1152]{1,0:T(8,128)(2,1)S(1)}, u32[]{:S(2)}, u32[]{:S(2)}) %collective-permute-start.21) | collective-permute-done | bytes 589856 | tf_op jit(solution)/shard_map/ppermute | solution.py:27
  318.2 19.0 %attend_back.3 = (bf16[256,1152]{1,0:T(8,128)(2,1)}, bf16[1024,384]{1,0:T(8,128)(2,1)}, bf16[1024,384]{1,0:T(8,128)(2,1)}) custom-call(s32[4]{0:T(128)} %copy-done.43, bf16[256,1152]{1,0:T(8,128)(2,1)} %copy-done.35, bf16[256,1152]{1,0:T(8,128)(2,1)} %copy-done.45, f32[32,256]{1,0:T(8,128)} %get-tuple-element.162.cos_ref, ...), custom_call_target="tpu_custom_call" | custom-call | flops 3019898880 | bytes 3342336 | tf_op jit(solution)/shard_map/attend_back/pallas_call | solution.py:276
  346.1 19.1 %attend_back.2 = (bf16[256,1152]{1,0:T(8,128)(2,1)}, bf16[1024,384]{1,0:T(8,128)(2,1)}, bf16[1024,384]{1,0:T(8,128)(2,1)}) custom-call(s32[4]{0:T(128)} %copy-done.42, bf16[256,1152]{1,0:T(8,128)(2,1)} %copy-done.34, bf16[256,1152]{1,0:T(8,128)(2,1)} %copy-done.44, f32[32,256]{1,0:T(8,128)} %get-tuple-element.162.cos_ref, ...), custom_call_target="tpu_custom_call" | custom-call | flops 3019898880 | bytes 3342336 | tf_op jit(solution)/shard_map/attend_back/pallas_call | solution.py:276
  372.3 8.6 %copy.79 = bf16[1152,2304]{1,0:T(8,128)(2,1)} copy(bf16[1152,2304]{0,1:T(8,128)(2,1)} %pad_maximum_fusion) | data formatting | bytes 10616832
  390.5 4.1 collective-permute-done.23.came_ref
  396.9 5.1 collective-permute-done.19.came_ref
  425.4 4.5 finish.3
  430.0 4.5 finish.2
  434.6 30.4 %collective-permute-done.25 = bf16[1152,768]{0,1:T(8,128)(2,1)} collective-permute-done((bf16[1152,768]{0,1:T(8,128)(2,1)S(1)}, bf16[1152,768]{0,1:T(8,128)(2,1)}, u32[]{:S(2)}, u32[]{:S(2)}) %collective-permute-start.25) | collective-permute-done | bytes 1769504 | tf_op jit(solution)/shard_map/ppermute | solution.py:27
  468.4 14.0 %reduce-scatter.7.cloned.1.call-done = bf16[144,2304]{1,0:T(8,128)(2,1)} async-done(((bf16[1152,2304]{1,0:T(8,128)(2,1)}), bf16[144,2304]{1,0:T(8,128)(2,1)}) %reduce-scatter.7.cloned.1.call-update) | async-done | bytes 663568
  483.9 4.3 copy.81
  488.3 4.3 fusion.39
  501.6 12.2 %collective-permute-done.15 = bf16[256,1152]{1,0:T(8,128)(2,1)S(1)} collective-permute-done((bf16[256,1152]{1,0:T(8,128)(2,1)S(1)}, bf16[256,1152]{1,0:T(8,128)(2,1)S(1)}, u32[]{:S(2)}, u32[]{:S(2)}) %collective-permute-start.15) | collective-permute-done | bytes 589856 | tf_op jit(solution)/shard_map/ppermute | solution.py:27
  514.0 11.5 %collective-permute-done.13 = bf16[256,1152]{1,0:T(8,128)(2,1)S(1)} collective-permute-done((bf16[256,1152]{1,0:T(8,128)(2,1)S(1)}, bf16[256,1152]{1,0:T(8,128)(2,1)S(1)}, u32[]{:S(2)}, u32[]{:S(2)}) %collective-permute-start.13) | collective-permute-done | bytes 589856 | tf_op jit(solution)/shard_map/ppermute | solution.py:27
  526.9 28.1 %reduce-scatter.9.cloned.1.call-done = bf16[144,896]{1,0:T(8,128)(2,1)} async-done(((bf16[1152,896]{1,0:T(8,128)(2,1)}), bf16[144,896]{1,0:T(8,128)(2,1)}) %reduce-scatter.9.cloned.1.call-update) | async-done | bytes 258064
  560.4 6.9 %collective-permute-done.26 = bf16[144,896]{0,1:T(8,128)(2,1)S(1)} collective-permute-done((bf16[144,896]{0,1:T(8,128)(2,1)S(1)}, bf16[144,896]{0,1:T(8,128)(2,1)S(1)}, u32[]{:S(2)}, u32[]{:S(2)}) %collective-permute-start.26) | collective-permute-done | bytes 258080 | tf_op jit(solution)/shard_map/ppermute | solution.py:27
  (361 shorter events, 159.1 us)
Async XLA Ops:
  7.2 81.8 %all-gather.4.cloned.1.call-start = ((), (), s32[]{:S(2)}) async-start(), calls=%async_computation.2 | async-start | bytes 7299072 | tf_op jit(solution)/shard_map/all_gather | solution.py:482
  9.2 168.2 %all-gather.6.cloned.1.call-start = ((), (), s32[]{:S(2)}) async-start(), calls=%async_computation.3 | async-start | bytes 5971968 | tf_op jit(solution)/shard_map/all_gather | solution.py:484
  11.3 471.2 %reduce-scatter.7.cloned.1.call-start = ((), (), s32[]{:S(2)}) async-start(), calls=%async_computation.4 | async-start | bytes 5971968
  14.7 33.3 %collective-permute-start.5 = (bf16[2,256,1152]{2,1,0:T(8,128)(2,1)}, bf16[2,256,1152]{2,1,0:T(8,128)(2,1)}, u32[]{:S(2)}, u32[]{:S(2)}) collective-permute-start(bf16[2,256,1152]{2,1,0:T(8,128)(2,1)} %get-tuple-element.138), channel_id=1, source_target_pairs={{0,2},{1,3},{2,0},{3,1},{4,6},{5,7},{6,4},{7,5},{8,10},{9,11},{10,... | collective-permute-start | bytes 3538952 | tf_op jit(solution)/shard_map/ppermute | solution.py:27
  49.5 6.9 %collective-permute-start.6 = (bf16[2,2,256,1152]{3,2,1,0:T(8,128)(2,1)S(1)}, bf16[2,2,256,1152]{3,2,1,0:T(8,128)(2,1)S(1)}, u32[]{:S(2)}, u32[]{:S(2)}) collective-permute-start(bf16[2,2,256,1152]{3,2,1,0:T(8,128)(2,1)S(1)} %pad_maximum_fusion.1), channel_id=1, source_target_pairs={{0,1},{1,0},{2,3},{3,2},{4,5},{5,4},{6,7},{7,6},{8,9},{9,8},{10,11... | collective-permute-start | bytes 7077896 | tf_op jit(solution)/shard_map/ppermute | solution.py:22
  95.3 93.9 %collective-permute-start.7 = (bf16[256,768]{1,0:T(8,128)(2,1)S(1)}, bf16[256,768]{1,0:T(8,128)(2,1)}, u32[]{:S(2)}, u32[]{:S(2)}) collective-permute-start(bf16[256,768]{1,0:T(8,128)(2,1)S(1)} %get-tuple-element.156.k0.v0), channel_id=1, source_target_pairs={{0,2},{1,3},{2,0},{3,1},{4,6},{5,7},{6,4},{7,5},{8,10},{9,11},{10,... | collective-permute-start | bytes 1179656 | tf_op jit(solution)/shard_map/ppermute | solution.py:27
  183.5 11.5 %collective-permute-start.8 = (bf16[256,768]{1,0:T(8,128)(2,1)S(1)}, bf16[256,768]{1,0:T(8,128)(2,1)S(1)}, u32[]{:S(2)}, u32[]{:S(2)}) collective-permute-start(bf16[256,768]{1,0:T(8,128)(2,1)S(1)} %get-tuple-element.156.k0.v0), channel_id=1, source_target_pairs={{0,1},{1,0},{2,3},{3,2},{4,5},{5,4},{6,7},{7,6},{8,9},{9,8},{10,11... | collective-permute-start | bytes 1179656 | tf_op jit(solution)/shard_map/ppermute | solution.py:22
  183.5 11.5 %collective-permute-start = (bf16[256,768]{1,0:T(8,128)(2,1)S(1)}, bf16[256,768]{1,0:T(8,128)(2,1)S(1)}, u32[]{:S(2)}, u32[]{:S(2)}) collective-permute-start(bf16[256,768]{1,0:T(8,128)(2,1)S(1)} %get-tuple-element.155.k0.v0), channel_id=1, source_target_pairs={{0,2},{1,3},{2,0},{3,1},{4,6},{5,7},{6,4},{7,5},{8,10},{9,11},{10,... | collective-permute-start | bytes 1179656 | tf_op jit(solution)/shard_map/ppermute | solution.py:27
  185.0 30.5 %collective-permute-start.1 = (bf16[256,768]{1,0:T(8,128)(2,1)S(1)}, bf16[256,768]{1,0:T(8,128)(2,1)S(1)}, u32[]{:S(2)}, u32[]{:S(2)}) collective-permute-start(bf16[256,768]{1,0:T(8,128)(2,1)S(1)} %get-tuple-element.155.k0.v0), channel_id=1, source_target_pairs={{0,1},{1,0},{2,3},{3,2},{4,5},{5,4},{6,7},{7,6},{8,9},{9,8},{10,11... | collective-permute-start | bytes 1179656 | tf_op jit(solution)/shard_map/ppermute | solution.py:22
  189.2 5.9 %collective-permute-start.9 = (bf16[256,768]{1,0:T(8,128)(2,1)}, bf16[256,768]{1,0:T(8,128)(2,1)S(1)}, u32[]{:S(2)}, u32[]{:S(2)}) collective-permute-start(bf16[256,768]{1,0:T(8,128)(2,1)} %collective-permute-done.7.k1.v1), channel_id=1, source_target_pairs={{0,1},{1,0},{2,3},{3,2},{4,5},{5,4},{6,7},{7,6},{8,9},{9,8},{10,11... | collective-permute-start | bytes 1179656 | tf_op jit(solution)/shard_map/ppermute | solution.py:22
  195.1 20.5 %collective-permute-start.2 = (bf16[256,768]{1,0:T(8,128)(2,1)S(1)}, bf16[256,768]{1,0:T(8,128)(2,1)S(1)}, u32[]{:S(2)}, u32[]{:S(2)}) collective-permute-start(bf16[256,768]{1,0:T(8,128)(2,1)S(1)} %collective-permute-done.k1.v1), channel_id=1, source_target_pairs={{0,1},{1,0},{2,3},{3,2},{4,5},{5,4},{6,7},{7,6},{8,9},{9,8},{10,11... | collective-permute-start | bytes 1179656 | tf_op jit(solution)/shard_map/ppermute | solution.py:22
  208.6 20.9 %collective-permute-start.10 = (bf16[256,1152]{1,0:T(8,128)(2,1)S(1)}, bf16[256,1152]{1,0:T(8,128)(2,1)S(1)}, u32[]{:S(2)}, u32[]{:S(2)}) collective-permute-start(bf16[256,1152]{1,0:T(8,128)(2,1)S(1)} %get-tuple-element.42), channel_id=1, source_target_pairs={{0,2},{1,3},{2,0},{3,1},{4,6},{5,7},{6,4},{7,5},{8,10},{9,11},{10,... | collective-permute-start | bytes 1769480 | tf_op jit(solution)/shard_map/ppermute | solution.py:27
  228.9 15.5 %collective-permute-start.3 = (bf16[256,1152]{1,0:T(8,128)(2,1)S(1)}, bf16[256,1152]{1,0:T(8,128)(2,1)S(1)}, u32[]{:S(2)}, u32[]{:S(2)}) collective-permute-start(bf16[256,1152]{1,0:T(8,128)(2,1)S(1)} %get-tuple-element.41), channel_id=1, source_target_pairs={{0,2},{1,3},{2,0},{3,1},{4,6},{5,7},{6,4},{7,5},{8,10},{9,11},{10,... | collective-permute-start | bytes 1769480 | tf_op jit(solution)/shard_map/ppermute | solution.py:27
  229.6 15.1 %collective-permute-start.11 = (bf16[512,1152]{1,0:T(8,128)(2,1)S(1)}, bf16[512,1152]{1,0:T(8,128)(2,1)S(1)}, u32[]{:S(2)}, u32[]{:S(2)}) collective-permute-start(bf16[512,1152]{1,0:T(8,128)(2,1)S(1)} %pad_maximum_fusion.6), channel_id=1, source_target_pairs={{0,1},{1,0},{2,3},{3,2},{4,5},{5,4},{6,7},{7,6},{8,9},{9,8},{10,11... | collective-permute-start | bytes 3538952 | tf_op jit(solution)/shard_map/ppermute | solution.py:22
  244.5 24.9 %collective-permute-start.4 = (bf16[512,1152]{1,0:T(8,128)(2,1)S(1)}, bf16[512,1152]{1,0:T(8,128)(2,1)S(1)}, u32[]{:S(2)}, u32[]{:S(2)}) collective-permute-start(bf16[512,1152]{1,0:T(8,128)(2,1)S(1)} %pad_maximum_fusion.4), channel_id=1, source_target_pairs={{0,1},{1,0},{2,3},{3,2},{4,5},{5,4},{6,7},{7,6},{8,9},{9,8},{10,11... | collective-permute-start | bytes 3538952 | tf_op jit(solution)/shard_map/ppermute | solution.py:22
  260.6 35.6 %collective-permute-start.20 = (bf16[512,1152]{1,0:T(8,128)(2,1)S(1)}, bf16[512,1152]{1,0:T(8,128)(2,1)S(1)}, u32[]{:S(2)}, u32[]{:S(2)}) collective-permute-start(bf16[512,1152]{1,0:T(8,128)(2,1)S(1)} %slice.658), channel_id=1, source_target_pairs={{0,1},{1,0},{2,3},{3,2},{4,5},{5,4},{6,7},{7,6},{8,9},{9,8},{10,11... | collective-permute-start | bytes 3538952 | tf_op jit(solution)/shard_map/ppermute | solution.py:22
  285.0 12.4 %collective-permute-start.16 = (bf16[512,1152]{1,0:T(8,128)(2,1)S(1)}, bf16[512,1152]{1,0:T(8,128)(2,1)S(1)}, u32[]{:S(2)}, u32[]{:S(2)}) collective-permute-start(bf16[512,1152]{1,0:T(8,128)(2,1)S(1)} %slice.659), channel_id=1, source_target_pairs={{0,1},{1,0},{2,3},{3,2},{4,5},{5,4},{6,7},{7,6},{8,9},{9,8},{10,11... | collective-permute-start | bytes 3538952 | tf_op jit(solution)/shard_map/ppermute | solution.py:22
  296.6 16.3 %collective-permute-start.21 = (bf16[256,1152]{1,0:T(8,128)(2,1)S(1)}, bf16[256,1152]{1,0:T(8,128)(2,1)S(1)}, u32[]{:S(2)}, u32[]{:S(2)}) collective-permute-start(bf16[256,1152]{1,0:T(8,128)(2,1)S(1)} %slice.662), channel_id=1, source_target_pairs={{0,2},{1,3},{2,0},{3,1},{4,6},{5,7},{6,4},{7,5},{8,10},{9,11},{10,... | collective-permute-start | bytes 1769480 | tf_op jit(solution)/shard_map/ppermute | solution.py:27
  298.5 42.3 %collective-permute-start.17 = (bf16[256,1152]{1,0:T(8,128)(2,1)}, bf16[256,1152]{1,0:T(8,128)(2,1)S(1)}, u32[]{:S(2)}, u32[]{:S(2)}) collective-permute-start(bf16[256,1152]{1,0:T(8,128)(2,1)} %slice.663), channel_id=1, source_target_pairs={{0,2},{1,3},{2,0},{3,1},{4,6},{5,7},{6,4},{7,5},{8,10},{9,11},{10,... | collective-permute-start | bytes 1769480 | tf_op jit(solution)/shard_map/ppermute | solution.py:27
  340.8 40.2 %collective-permute-start.22 = (bf16[512,768]{1,0:T(8,128)(2,1)}, bf16[512,768]{1,0:T(8,128)(2,1)}, u32[]{:S(2)}, u32[]{:S(2)}) collective-permute-start(bf16[512,768]{1,0:T(8,128)(2,1)} %pad_maximum_fusion.9), channel_id=1, source_target_pairs={{0,1},{1,0},{2,3},{3,2},{4,5},{5,4},{6,7},{7,6},{8,9},{9,8},{10,11... | collective-permute-start | bytes 2359304 | tf_op jit(solution)/shard_map/ppermute | solution.py:22
  369.3 13.8 %collective-permute-start.18 = (bf16[512,768]{1,0:T(8,128)(2,1)}, bf16[512,768]{1,0:T(8,128)(2,1)}, u32[]{:S(2)}, u32[]{:S(2)}) collective-permute-start(bf16[512,768]{1,0:T(8,128)(2,1)} %pad_maximum_fusion.8), channel_id=1, source_target_pairs={{0,1},{1,0},{2,3},{3,2},{4,5},{5,4},{6,7},{7,6},{8,9},{9,8},{10,11... | collective-permute-start | bytes 2359304 | tf_op jit(solution)/shard_map/ppermute | solution.py:22
  380.9 174.1 %reduce-scatter.9.cloned.1.call-start = ((), (), s32[]{:S(2)}) async-start(), calls=%async_computation.5 | async-start | bytes 2322432
  382.4 12.2 %collective-permute-start.23 = (bf16[256,768]{1,0:T(8,128)(2,1)S(1)}, bf16[256,768]{1,0:T(8,128)(2,1)}, u32[]{:S(2)}, u32[]{:S(2)}) collective-permute-start(bf16[256,768]{1,0:T(8,128)(2,1)S(1)} %slice.666), channel_id=1, source_target_pairs={{0,2},{1,3},{2,0},{3,1},{4,6},{5,7},{6,4},{7,5},{8,10},{9,11},{10,... | collective-permute-start | bytes 1179656 | tf_op jit(solution)/shard_map/ppermute | solution.py:27
  385.2 16.8 %collective-permute-start.19 = (bf16[256,768]{1,0:T(8,128)(2,1)}, bf16[256,768]{1,0:T(8,128)(2,1)}, u32[]{:S(2)}, u32[]{:S(2)}) collective-permute-start(bf16[256,768]{1,0:T(8,128)(2,1)} %slice.667), channel_id=1, source_target_pairs={{0,2},{1,3},{2,0},{3,1},{4,6},{5,7},{6,4},{7,5},{8,10},{9,11},{10,... | collective-permute-start | bytes 1179656 | tf_op jit(solution)/shard_map/ppermute | solution.py:27
  413.3 6.6 %collective-permute-start.24 = (bf16[2,1152,768]{1,2,0:T(8,128)(2,1)}, bf16[2,1152,768]{1,2,0:T(8,128)(2,1)}, u32[]{:S(2)}, u32[]{:S(2)}) collective-permute-start(bf16[2,1152,768]{1,2,0:T(8,128)(2,1)} %maximum_maximum_fusion), channel_id=1, source_target_pairs={{0,1},{1,0},{2,3},{3,2},{4,5},{5,4},{6,7},{7,6},{8,9},{9,8},{10,11... | collective-permute-start | bytes 10616840 | tf_op jit(solution)/shard_map/ppermute | solution.py:22
  424.0 41.0 %collective-permute-start.25 = (bf16[1152,768]{0,1:T(8,128)(2,1)S(1)}, bf16[1152,768]{0,1:T(8,128)(2,1)}, u32[]{:S(2)}, u32[]{:S(2)}) collective-permute-start(bf16[1152,768]{0,1:T(8,128)(2,1)S(1)} %fusion.18), channel_id=1, source_target_pairs={{0,2},{1,3},{2,0},{3,1},{4,6},{5,7},{6,4},{7,5},{8,10},{9,11},{10,... | collective-permute-start | bytes 5308424 | tf_op jit(solution)/shard_map/ppermute | solution.py:27
  492.8 4.5 collective-permute-start.14
  496.7 3.0 collective-permute-start.12
  497.5 16.3 %collective-permute-start.15 = (bf16[256,1152]{1,0:T(8,128)(2,1)S(1)}, bf16[256,1152]{1,0:T(8,128)(2,1)S(1)}, u32[]{:S(2)}, u32[]{:S(2)}) collective-permute-start(bf16[256,1152]{1,0:T(8,128)(2,1)S(1)} %slice.664), channel_id=1, source_target_pairs={{0,2},{1,3},{2,0},{3,1},{4,6},{5,7},{6,4},{7,5},{8,10},{9,11},{10,... | collective-permute-start | bytes 1769480 | tf_op jit(solution)/shard_map/ppermute | solution.py:27
  500.0 25.5 %collective-permute-start.13 = (bf16[256,1152]{1,0:T(8,128)(2,1)S(1)}, bf16[256,1152]{1,0:T(8,128)(2,1)S(1)}, u32[]{:S(2)}, u32[]{:S(2)}) collective-permute-start(bf16[256,1152]{1,0:T(8,128)(2,1)S(1)} %slice.665), channel_id=1, source_target_pairs={{0,2},{1,3},{2,0},{3,1},{4,6},{5,7},{6,4},{7,5},{8,10},{9,11},{10,... | collective-permute-start | bytes 1769480 | tf_op jit(solution)/shard_map/ppermute | solution.py:27
  556.1 11.2 %collective-permute-start.26 = (bf16[144,896]{0,1:T(8,128)(2,1)S(1)}, bf16[144,896]{0,1:T(8,128)(2,1)S(1)}, u32[]{:S(2)}, u32[]{:S(2)}) collective-permute-start(bf16[144,896]{0,1:T(8,128)(2,1)S(1)} %copy.82), channel_id=1, source_target_pairs={{0,2},{1,3},{2,0},{3,1},{4,6},{5,7},{6,4},{7,5},{8,10},{9,11},{10,... | collective-permute-start | bytes 774152 | tf_op jit(solution)/shard_map/ppermute | solution.py:27
  568.7 6.4 %collective-permute-start.27 = (bf16[2,144,896]{2,1,0:T(8,128)(2,1)}, bf16[2,144,896]{2,1,0:T(8,128)(2,1)}, u32[]{:S(2)}, u32[]{:S(2)}) collective-permute-start(bf16[2,144,896]{2,1,0:T(8,128)(2,1)} %copy.65), channel_id=1, source_target_pairs={{0,1},{1,0},{2,3},{3,2},{4,5},{5,4},{6,7},{7,6},{8,9},{9,8},{10,11... | collective-permute-start | bytes 1548296 | tf_op jit(solution)/shard_map/ppermute | solution.py:22
  (86 other events, 1456.2 us)
Sparse Core Ops, SparseCore 0:
  11.6 77.3 all-gather.3
  91.7 85.5 all-gather.5
  381.0 101.3 reduce-scatter.6
  488.4 66.5 reduce-scatter.8

commit v3 on v2

v3 whole, which is shorter than its diff:
```python
import functools

import jax
import jax.numpy as jnp
from jax import lax
from jax.experimental import pallas as pl
from jax.experimental.layout import Layout, with_layout_constraint
from jax.experimental.pallas import tpu as pltpu
from jax.sharding import PartitionSpec as P

HEAD_SIZE = 64
EPSILON = 1e-05
ROPE_BASE = 10000.0
MASKED = -1e30
BF16 = jnp.bfloat16
F32 = jnp.float32

BLOCK_XOR = (0, 2, 1, 3)


def near(value):
    count = lax.axis_size("tensor")
    return lax.ppermute(value, "tensor", [(i, i ^ 1) for i in range(count)])


def far(value):
    count = lax.axis_size("tensor")
    return lax.ppermute(value, "tensor", [(i, i ^ 2) for i in range(count)])


def scatter_rows(partial):
    half = partial.shape[0] // 2
    quarter = half // 2
    kept = partial[:half].astype(F32) + near(partial[half:].astype(BF16)).astype(F32)
    return kept[:quarter] + far(kept[quarter:].astype(BF16)).astype(F32)


def dot(left_side, right_side):
    return jnp.dot(left_side, right_side, preferred_element_type=F32)


def contract_rows(left_side, right_side):
    return lax.dot_general(
        left_side, right_side, (((0,), (0,)), ((), ())), preferred_element_type=F32
    )


def contract_last(left_side, right_side):
    return lax.dot_general(
        left_side, right_side, (((1,), (1,)), ((), ())), preferred_element_type=F32
    )


def dot_nt(left_side, right_side):
    return lax.dot_general(
        left_side, right_side, (((1,), (1,)), ((), ())), preferred_element_type=F32
    )


def dot_nn(left_side, right_side):
    return lax.dot_general(
        left_side, right_side, (((1,), (0,)), ((), ())), preferred_element_type=F32
    )


def head_of(ref, index):
    return ref[:, index * HEAD_SIZE : (index + 1) * HEAD_SIZE]


def row_scale_of(values):
    return lax.rsqrt(jnp.mean(values * values, axis=-1, keepdims=True) + EPSILON)


def turn(values, cosine, sine):
    lane = lax.broadcasted_iota(jnp.int32, (values.shape[0], 128), 1)
    first_half = lane % HEAD_SIZE < HEAD_SIZE // 2
    parts = []
    for start in range(0, values.shape[1], 128):
        part = values[:, start : start + 128]
        later = pltpu.roll(part, 128 - HEAD_SIZE // 2, 1)
        earlier = pltpu.roll(part, HEAD_SIZE // 2, 1)
        parts.append(part * cosine + jnp.where(first_half, later, earlier) * sine)
    return jnp.concatenate(parts, axis=1)


PAIR_CHUNKS = ((0, 0), (1, 0))
QUERY_CHUNKS = ((0, 1), (1, 1), (2, 1))
OUT_CHUNKS = ((3, 1), (2, 0), (3, 0))


def call(kernel, name, arrays, specs, outs, out_specs, flops=0, scalars=(), aliases=None, **more):
    moved = sum(x.size * x.dtype.itemsize for x in (*arrays, *jax.tree.leaves(outs)))
    return pl.pallas_call(
        kernel,
        grid_spec=pltpu.PrefetchScalarGridSpec(
            num_scalar_prefetch=len(scalars),
            grid=more.get("grid", (1,)),
            in_specs=specs,
            out_specs=out_specs,
            scratch_shapes=more.get("scratch", ()),
        ),
        out_shape=outs,
        input_output_aliases=aliases or {},
        compiler_params=pltpu.CompilerParams(vmem_limit_bytes=52 << 20),
        cost_estimate=pl.CostEstimate(flops=1, transcendentals=0, bytes_accessed=1),
        name=name,
    )(*scalars, *arrays)


def block(shape, at=(0, 0)):
    return pl.BlockSpec(shape, lambda *_: at)


def chunk_specs(width, chunks):
    return [block((width, width // 3), c) for c in chunks]


def array(shape, kind=BF16):
    return jax.ShapeDtypeStruct(shape, kind)


ANY = pl.BlockSpec(memory_space=pl.ANY)


def project_pairs_kernel(x_ref, gain_ref, cosine_ref, sine_ref, wk, wv, pair_ref, normed_ref):
    values = x_ref[...].astype(F32)
    normed = (values * row_scale_of(values) * gain_ref[...]).astype(BF16)
    normed_ref[...] = normed
    keys = turn(dot_nn(normed, wk[...]), cosine_ref[...], sine_ref[...]).astype(BF16)
    values = dot_nn(normed, wv[...]).astype(BF16)
    for i in range(keys.shape[1] // 128):
        pair_ref[:, 256 * i : 256 * i + 128] = keys[:, 128 * i : 128 * (i + 1)]
        pair_ref[:, 256 * i + 128 : 256 * (i + 1)] = values[:, 128 * i : 128 * (i + 1)]


def project_pairs(x_rows, gain, cosine, sine, weights):
    rows, width = x_rows.shape
    pair_width = 2 * (width // 3)
    return call(
        project_pairs_kernel,
        "project_pairs",
        (x_rows, gain, cosine, sine, weights, weights),
        [block(x.shape) for x in (x_rows, gain, cosine, sine)] + chunk_specs(width, PAIR_CHUNKS),
        [array((rows, pair_width)), array((rows, width))],
        [block((rows, pair_width)), block((rows, width))],
        2 * rows * width * pair_width,
    )


def project_queries_kernel(normed_ref, cosine_ref, sine_ref, w0, w1, w2, query_ref):
    third = w0.shape[1]
    for i, w in enumerate((w0, w1, w2)):
        turned = turn(dot_nn(normed_ref[...], w[...]), cosine_ref[...], sine_ref[...])
        query_ref[:, i * third : (i + 1) * third] = (turned * HEAD_SIZE ** (-0.5)).astype(BF16)


def project_queries(normed, cosine, sine, weights):
    rows, width = normed.shape
    return call(
        project_queries_kernel,
        "project_queries",
        (normed, cosine, sine, weights, weights, weights),
        [block(x.shape) for x in (normed, cosine, sine)] + chunk_specs(width, QUERY_CHUNKS),
        array((rows, width)),
        block((rows, width)),
        2 * rows * width * width,
    )


def attend_kernel(group, counts, q_ref, p0, p1, p2, p3, *rest):
    o_ref = rest[-1]
    rows = q_ref.shape[0]
    refs = (p0, p1, p2, p3)
    row = lax.broadcasted_iota(jnp.int32, (rows, rows), 0)
    col = lax.broadcasted_iota(jnp.int32, (rows, rows), 1)
    allowed = [jnp.logical_and(col <= row, col < counts[0])]
    allowed += [col < counts[j] for j in range(1, 4)]
    allowed = [jnp.concatenate([a] * group, axis=0) for a in allowed]
    for pair in range(2):
        queries = jnp.concatenate([head_of(q_ref, pair * group + i) for i in range(group)], axis=0)
        scores = [
            jnp.where(allowed[j], dot_nt(queries, head_of(refs[j], pair)), MASKED)
            for j in range(4)
        ]
        top = functools.reduce(jnp.maximum, [jnp.max(s, axis=1, keepdims=True) for s in scores])
        soft = [jnp.exp(s - top) for s in scores]
        total = functools.reduce(jnp.add, [jnp.sum(s, axis=1, keepdims=True) for s in soft])
        out = functools.reduce(
            jnp.add, [dot_nn(soft[j].astype(BF16), head_of(refs[j], 2 + pair)) for j in range(4)]
        )
        out = (out / total).astype(BF16)
        for i in range(group):
            start = (pair * group + i) * HEAD_SIZE
            o_ref[:, start : start + HEAD_SIZE] = out[i * rows : (i + 1) * rows]


def attention_sizes(queries, pairs_own):
    rows = queries.shape[0] // 2
    steps = pairs_own.shape[1] // (4 * HEAD_SIZE)
    group = queries.shape[1] // (2 * HEAD_SIZE * steps)
    return rows, steps, group


def attend(b, counts, queries, pairs_own, others, earlier):
    rows, steps, group = attention_sizes(queries, pairs_own)
    width = queries.shape[1]
    query_spec = pl.BlockSpec((rows, width // steps), lambda i, c: (b, i))
    own_spec = pl.BlockSpec((rows, 4 * HEAD_SIZE), lambda i, c: (b, i))
    pair_spec = pl.BlockSpec((rows, 4 * HEAD_SIZE), lambda i, c: (0, i))
    more = [] if earlier is None else [earlier]
    return call(
        functools.partial(attend_kernel, group),
        "attend",
        (queries, pairs_own, *others, *more),
        [query_spec, own_spec] + [pair_spec] * 3 + [ANY] * len(more),
        array(queries.shape),
        query_spec,
        16 * rows * rows * width,
        (counts,),
        {6: 0} if more else None,
        grid=(steps,),
    )


def attend_back_kernel(group, counts, q_ref, g_ref, cos_ref, sin_ref, p0, p1, p2, p3, *rest):
    dq_ref, kept_ref, sent_ref, turned_ref = rest[-4:]
    rows = q_ref.shape[0]
    half = HEAD_SIZE // 2
    both = jnp.concatenate([p0[...], p1[...], p2[...], p3[...]], axis=0)
    keys, values = both[:, :128], both[:, 128:]
    keys_t = keys.T
    row = lax.broadcasted_iota(jnp.int32, (rows, rows), 0)
    col = lax.broadcasted_iota(jnp.int32, (rows, rows), 1)
    allowed = [jnp.logical_and(row <= col, row < counts[0])]
    allowed += [row < counts[j] for j in range(1, 4)]
    allowed = jnp.concatenate([jnp.concatenate([a] * group, axis=1) for a in allowed], axis=0)
    key_grads, value_grads = [], []
    for pair in range(2):
        lanes = slice(pair * HEAD_SIZE, (pair + 1) * HEAD_SIZE)
        key, value = keys[:, lanes], values[:, lanes]
        queries = jnp.concatenate([head_of(q_ref, pair * group + i) for i in range(group)], axis=0)
        grads = jnp.concatenate([head_of(g_ref, pair * group + i) for i in range(group)], axis=0)
        scores = jnp.where(allowed, dot_nt(key, queries), MASKED)
        soft = jnp.exp(scores - jnp.max(scores, axis=0, keepdims=True))
        soft = soft * (1.0 / jnp.sum(soft, axis=0, keepdims=True))
        grad_soft = dot_nt(value, grads)
        scaled = soft * grad_soft
        grad_scores = (scaled - soft * jnp.sum(scaled, axis=0, keepdims=True)).astype(BF16)
        value_grads.append(dot_nn(soft.astype(BF16), grads))
        key_grads.append(dot_nn(grad_scores, queries))
        query_grad = dot_nn(keys_t[lanes, :], grad_scores) * HEAD_SIZE ** (-0.5)
        for i in range(group):
            part = query_grad[:, i * rows : (i + 1) * rows]
            first, second = part[:half], part[half:]
            start = (pair * group + i) * HEAD_SIZE
            turned_ref[start : start + half, :] = first * cos_ref[...] + second * sin_ref[...]
            turned_ref[start + half : start + HEAD_SIZE, :] = (
                second * cos_ref[...] - first * sin_ref[...]
            )
    grads = jnp.concatenate(key_grads + value_grads, axis=1).astype(BF16)
    kept_ref[...] = grads[: 2 * rows]
    sent_ref[...] = grads[2 * rows :]
    dq_ref[...] = turned_ref[...].T.astype(BF16)


def attend_back(b, counts, queries, grads, cosine_t, sine_t, pairs_own, others, earlier):
    rows, steps, group = attention_sizes(queries, pairs_own)
    width = queries.shape[1]
    query_spec = pl.BlockSpec((rows, width // steps), lambda i, c: (b, i))
    grad_spec = pl.BlockSpec((rows, width // steps), lambda i, c: (0, i))
    own_spec = pl.BlockSpec((rows, 4 * HEAD_SIZE), lambda i, c: (b, i))
    pair_spec = pl.BlockSpec((rows, 4 * HEAD_SIZE), lambda i, c: (0, i))
    half_spec = pl.BlockSpec((2 * rows, 4 * HEAD_SIZE), lambda i, c: (0, i))
    more = [] if earlier is None else [earlier]
    return call(
        functools.partial(attend_back_kernel, group),
        "attend_back",
        (queries, grads, cosine_t, sine_t, pairs_own, *others, *more),
        [query_spec, grad_spec, block(cosine_t.shape), block(sine_t.shape), own_spec]
        + [pair_spec] * 3
        + [ANY] * len(more),
        [array(queries.shape)] + [array((2 * rows, pairs_own.shape[1]))] * 2,
        [query_spec, half_spec, half_spec],
        40 * rows * rows * width,
        (counts,),
        {9: 0} if more else None,
        grid=(steps,),
        scratch=[pltpu.VMEM((width // steps, rows), F32)],
    )


def leave_kernel(x_ref, o_ref, gain_ref, w0, w1, w2, middle_ref, normed_ref):
    out = o_ref[...]
    added = jnp.concatenate([dot_nn(out, w[...]) for w in (w0, w1, w2)], axis=1)
    middle = x_ref[...].astype(F32) + added
    middle_ref[...] = middle
    normed_ref[...] = (middle * row_scale_of(middle) * gain_ref[...]).astype(BF16)


def leave(b, x_rows, attended, gain, weights):
    rows, width = x_rows.shape[0] // 2, x_rows.shape[1]
    here = block((rows, width), (b, 0))
    return call(
        leave_kernel,
        "leave",
        (x_rows, attended, gain, weights, weights, weights),
        [here, here, block(gain.shape)] + chunk_specs(width, OUT_CHUNKS),
        [array((rows, width), F32), array((rows, width))],
        [block((rows, width))] * 2,
        2 * rows * width * width,
    )


def enter_kernel(
    count, part_ref, near_ref, far_ref, middle_ref, cot_ref, gain_ref, w0, w1, w2, *rest
):
    grad_middle_ref, branch_ref, out_ref, gain_grad_ref = rest[-4:]
    rows, width = middle_ref.shape
    third = width // 3
    middle = middle_ref[...]
    grad_normed = part_ref[...] + near_ref[...].astype(F32) + far_ref[...].astype(F32)
    scale = row_scale_of(middle)
    row = lax.broadcasted_iota(jnp.int32, (rows, width), 0)
    grad_row = jnp.where(row < count[0], cot_ref[...].astype(F32), 0.0)
    gain_grad = jnp.sum(grad_normed * middle * scale, axis=0, keepdims=True)
    gain_grad_ref[...] = jnp.broadcast_to(gain_grad, gain_grad_ref.shape)
    inner = grad_normed * gain_ref[...]
    grad_middle = grad_row + (
        scale * inner - middle * scale**3 * jnp.mean(inner * middle, axis=-1, keepdims=True)
    )
    grad_middle_ref[...] = grad_middle
    branch = grad_middle.astype(BF16)
    branch_ref[...] = branch
    weights = (w0, w1, w2)
    out = dot_nt(branch[:, :third], w0[...])
    for c in range(1, 3):
        out = out + dot_nt(branch[:, c * third : (c + 1) * third], weights[c][...])
    out_ref[...] = out.astype(BF16)


def enter(b, count, part, near_part, far_part, middle, cot_rows, gain, weights, earlier):
    rows, width = middle.shape
    full, here = block((rows, width)), block((rows, width), (b, 0))
    more = [] if earlier is None else [earlier]
    return call(
        enter_kernel,
        "enter",
        (part, near_part, far_part, middle, cot_rows, gain, weights, weights, weights, *more),
        [full, full, full, full, here, block(gain.shape)]
        + chunk_specs(width, OUT_CHUNKS)
        + [ANY] * len(more),
        [
            array((rows, width), F32),
            array((2 * rows, width)),
            array((rows, width)),
            array((8, width), F32),
        ],
        [full, here, full, block((8, width))],
        2 * rows * width * width,
        (count,),
        {10: 1} if more else None,
    )


def pairs_back_kernel(kept_ref, near_ref, far_ref, cosine_ref, sine_ref, *rest):
    pair_ref = rest[-1]
    width = pair_ref.shape[1] // 2
    for i in range(width // 128):
        lanes = slice(256 * i, 256 * (i + 1))
        total = (
            kept_ref[:, lanes].astype(F32)
            + near_ref[:, lanes].astype(F32)
            + far_ref[:, lanes].astype(F32)
        )
        turned = turn(total[:, :128], cosine_ref[...], -sine_ref[...])
        pair_ref[:, 128 * i : 128 * (i + 1)] = turned.astype(BF16)
        pair_ref[:, width + 128 * i : width + 128 * (i + 1)] = total[:, 128:].astype(BF16)


def pairs_back(b, kept, near_part, far_part, cosine, sine, earlier):
    rows, width = far_part.shape
    first = block((rows, width))
    table = block((rows, 128))
    more = [] if earlier is None else [earlier]
    return call(
        pairs_back_kernel,
        "pairs_back",
        (kept, near_part, far_part, cosine, sine, *more),
        [first, first, first, table, table] + [ANY] * len(more),
        array((2 * rows, width)),
        block((rows, width), (b, 0)),
        aliases={5: 0} if more else None,
    )


def finish_kernel(
    x_ref, query_ref, pair_ref, middle_ref, gain_ref, wk, wv, w0, w1, w2, grad_ref, gain_grad_ref
):
    third = x_ref.shape[1] // 3
    grads = [pair_ref[:, :third], pair_ref[:, third:]]
    grads += [query_ref[:, c * third : (c + 1) * third] for c in range(3)]
    grad_normed = dot_nt(grads[0], wk[...])
    for grad, w in zip(grads[1:], (wv, w0, w1, w2)):
        grad_normed = grad_normed + dot_nt(grad, w[...])
    values = x_ref[...].astype(F32)
    scale = row_scale_of(values)
    gain_grad = jnp.sum(grad_normed * values * scale, axis=0, keepdims=True)
    gain_grad_ref[...] = jnp.broadcast_to(gain_grad, gain_grad_ref.shape)
    inner = grad_normed * gain_ref[...]
    grad_ref[...] = (
        middle_ref[...]
        + scale * inner
        - values * scale**3 * jnp.mean(inner * values, axis=-1, keepdims=True)
    ).astype(BF16)


def finish(b, x_rows, query_grads, pair_grads, grad_middle, gain, weights):
    rows, width = grad_middle.shape
    here = block((rows, width), (b, 0))
    return call(
        finish_kernel,
        "finish",
        (x_rows, query_grads, pair_grads, grad_middle, gain, *([weights] * 5)),
        [here, here, block((rows, pair_grads.shape[1]), (b, 0)), block((rows, width))]
        + [block(gain.shape)]
        + chunk_specs(width, PAIR_CHUNKS + QUERY_CHUNKS),
        [array((rows, width)), array((8, width), F32)],
        [block((rows, width)), block((8, width))],
        10 * rows * width * width // 3,
    )


def row_major(value):
    return with_layout_constraint(value, Layout(major_to_minor=tuple(range(value.ndim))))


def pick(flag, first, second):
    return jnp.where(flag, first, second)


def sum_over_data(part_a, part_b, extra):
    data_count = lax.axis_size("dp")
    data_index = lax.axis_index("dp")
    columns = part_a[0].shape[1]

    def split(value):
        return value.reshape(data_count, -1, columns)

    if data_count != 8:
        total = part_a[0] + far(part_a[1].astype(BF16)).astype(F32)
        other = part_b[0] + far(part_b[1].astype(BF16)).astype(F32)
        rows = jnp.concatenate([split(total), split(other), extra], axis=1).astype(BF16)
        rows = lax.psum_scatter(rows, "dp", scatter_dimension=0, tiled=True)[0].astype(F32)
        share = total.shape[0] // data_count
        return rows[:share], rows[share : 2 * share], rows[2 * share :]

    groups = data_count // 2
    odd = (data_index & 1) == 1
    group = data_index // 2

    def beside(value):
        even_rows, odd_rows = value[..., 0, :, :], value[..., 1, :, :]
        sent = pick(odd, even_rows, odd_rows).astype(BF16)
        came = lax.ppermute(sent, "dp", [(i, i ^ 1) for i in range(data_count)])
        return pick(odd, odd_rows, even_rows).astype(F32) + came.astype(F32)

    def along(value):
        low = value.astype(BF16)
        total = lax.dynamic_index_in_dim(value, group, 0, keepdims=False)
        for step in range(1, groups):
            sent = lax.dynamic_index_in_dim(low, (group + step) % groups, 0, keepdims=False)
            moves = [(i, (i + 2 * step) % data_count) for i in range(data_count)]
            total = total + lax.ppermute(sent, "dp", moves).astype(F32)
        return total

    second = jnp.stack([split(p) for p in part_b], axis=0)
    second = beside(second.reshape(2, groups, 2, -1, columns))
    first = split(part_a[0] + far(part_a[1].astype(BF16)).astype(F32))
    first = jnp.concatenate([first, extra], axis=1).reshape(groups, 2, -1, columns)
    first = beside(first)
    second = along(jnp.moveaxis(second, 1, 0))
    first = along(first)
    second = second[0] + far(second[1].astype(BF16)).astype(F32)
    share = second.shape[0]
    return first[:share], second, first[share:]


def shards(
    inputs,
    lengths,
    gain_attn,
    gain_mlp,
    w_query,
    key_weight,
    value_weight,
    w_gate,
    w_up,
    w_out,
    w_down,
    cotangent,
):
    micro = inputs.shape[0]
    row_share = inputs.shape[2]
    width = inputs.shape[3]
    tensor_count = lax.axis_size("tensor")
    tensor_index = lax.axis_index("tensor")
    hidden_share = w_gate.shape[1]

    third = width // 3

    out_parts = [w_out[:, c * third : (c + 1) * third] for c in range(3)]
    query_parts = [w_query[:, c * third : (c + 1) * third] for c in range(3)]
    attn_quarter = lax.select_n(
        tensor_index,
        jnp.concatenate([key_weight, query_parts[0]], axis=1),
        jnp.concatenate([value_weight, query_parts[1]], axis=1),
        jnp.concatenate([out_parts[1], query_parts[2]], axis=1),
        jnp.concatenate([out_parts[2], out_parts[0]], axis=1),
    )
    attn_w = lax.all_gather(attn_quarter, ("tensor", "dp"), axis=0, tiled=True)
    mlp_local = jnp.concatenate([w_gate, w_up, w_down.T], axis=1)
    mlp_full = lax.all_gather(mlp_local, "dp", axis=0, tiled=True)
    gains = lax.all_gather(jnp.stack([gain_attn, gain_mlp]), "dp", axis=1, tiled=True).astype(F32)
    gain_one, gain_two = gains[0:1], gains[1:2]

    query_pos = tensor_index * row_share + jnp.arange(row_share, dtype=jnp.int32)
    exponent = jnp.arange(HEAD_SIZE // 2, dtype=F32) * (2.0 / HEAD_SIZE)
    angles = query_pos.astype(F32)[:, None] * (ROPE_BASE ** (-exponent))[None, :]
    cosine, sine = jnp.cos(angles), jnp.sin(angles)
    cosine_t, sine_t = cosine.T, sine.T
    cosine = jnp.concatenate([cosine] * 4, axis=1)
    sine = jnp.concatenate([-sine, sine, -sine, sine], axis=1)

    def counts_of(b):
        counts = []
        for x in BLOCK_XOR:
            block = tensor_index ^ x
            count = jnp.clip(lengths[b, 0] - block * row_share, 0, row_share)
            counts.append(jnp.where(block <= tensor_index, count, 0))
        return jnp.stack(counts).astype(jnp.int32)

    counts = [counts_of(b) for b in range(micro)]
    valid_rows = [
        jnp.clip(lengths[b, 0] - tensor_index * row_share, 0, row_share).astype(jnp.int32)
        for b in range(micro)
    ]
    valids = [
        (jnp.arange(row_share, dtype=jnp.int32) < valid_rows[b])[:, None] for b in range(micro)
    ]

    grad_own = jnp.stack(
        [jnp.where(valids[b], cotangent[b, 0], jnp.zeros((), BF16)) for b in range(micro)]
    )
    grad_far = far(grad_own)
    grad_near = near(jnp.stack([grad_own, grad_far]))
    grad_ffn = [
        jnp.concatenate([grad_own[b], grad_far[b], grad_near[0, b], grad_near[1, b]], axis=0)
        for b in range(micro)
    ]

    x_rows = inputs[:, 0].reshape(micro * row_share, width)
    cot_rows = cotangent[:, 0].reshape(micro * row_share, width)
    cosine_all = jnp.concatenate([cosine] * micro, axis=0)
    sine_all = jnp.concatenate([sine] * micro, axis=0)
    pairs_own, normed = project_pairs(x_rows, gain_one, cosine_all, sine_all, attn_w)
    queries = project_queries(normed, cosine_all, sine_all, attn_w)
    kept = []
    attended = None
    for b in range(micro):
        own = pairs_own[b * row_share : (b + 1) * row_share]
        across = far(own)
        others = [across, near(own), near(across)]
        attended = attend(b, counts[b], queries, pairs_own, others, attended)
        middle, hidden_own = leave(b, x_rows, attended, gain_two, attn_w)
        across = far(hidden_own)
        half = jnp.concatenate([hidden_own, across], axis=0)
        hidden = jnp.concatenate([half, near(half)], axis=0)
        kept.append(dict(others=others, middle=middle, hidden=hidden))
        if b == micro - 1:
            mlp_full, _ = lax.optimization_barrier((mlp_full, across))

    full_gate = mlp_full[:, :hidden_share]
    full_up = mlp_full[:, hidden_share : 2 * hidden_share]
    full_down_t = mlp_full[:, 2 * hidden_share :]
    for b in range(micro):
        k = kept[b]
        gate_proj = dot(k["hidden"], full_gate)
        up_proj = dot(k["hidden"], full_up)
        grad_act = dot(grad_ffn[b], full_down_t)
        sigmoid_gate = jax.nn.sigmoid(gate_proj)
        k["activated"] = (gate_proj * sigmoid_gate * up_proj).astype(BF16)
        k["grad_gate"] = (
            grad_act * up_proj * sigmoid_gate * (1.0 + gate_proj * (1.0 - sigmoid_gate))
        ).astype(BF16)
        k["grad_up"] = (grad_act * gate_proj * sigmoid_gate).astype(BF16)
        k["part"] = contract_last(k["grad_gate"], full_gate) + contract_last(k["grad_up"], full_up)
        k["near_part"] = near(k["part"][2 * row_share :].astype(BF16))
        k["far_part"] = far(
            (
                k["part"][row_share : 2 * row_share] + k["near_part"][row_share:].astype(F32)
            ).astype(BF16)
        )

    def total(left_side, right_side):
        parts = [contract_rows(left_side(b), right_side(b)) for b in range(micro)]
        return row_major(sum(parts[1:], parts[0]).astype(BF16))

    grad_mlp_w = row_major(
        jnp.concatenate(
            [
                total(lambda b: kept[b]["hidden"], lambda b: kept[b]["grad_gate"]),
                total(lambda b: kept[b]["hidden"], lambda b: kept[b]["grad_up"]),
                total(lambda b: grad_ffn[b], lambda b: kept[b]["activated"]),
            ],
            axis=1,
        )
    )
    grad_mlp_w, kept[0]["middle"] = lax.optimization_barrier((grad_mlp_w, kept[0]["middle"]))

    gain_two_grads = []
    branch = query_grads = pair_grads = None

    def backward(b, branch, query_grads):
        k = kept[b]
        k["grad_middle"], branch, grad_att, gain_two_grad = enter(
            b,
            valid_rows[b][None],
            k["part"],
            k["near_part"],
            k["far_part"],
            k["middle"],
            cot_rows,
            gain_two,
            attn_w,
            branch,
        )
        gain_two_grads.append(gain_two_grad[0:1])
        query_grads, k["pair_kept"], k["pair_sent"] = attend_back(
            b, counts[b], queries, grad_att, cosine_t, sine_t, pairs_own, k["others"], query_grads
        )
        return branch, query_grads

    grad_mlp_w = lax.psum_scatter(grad_mlp_w, "dp", scatter_dimension=0, tiled=True)
    for b in range(micro):
        branch, query_grads = backward(b, branch, query_grads)
    for b in range(micro):
        k = kept[b]
        near_pair = near(k["pair_sent"])
        far_pair = far(
            (k["pair_kept"][row_share:].astype(F32) + near_pair[row_share:].astype(F32)).astype(
                BF16
            )
        )
        pair_grads = pairs_back(b, k["pair_kept"], near_pair, far_pair, cosine, sine, pair_grads)

    outputs, input_grads, gain_one_grads = [], [], []
    for b in range(micro):
        k = kept[b]
        input_grad, gain_one_grad = finish(
            b, x_rows, query_grads, pair_grads, k["grad_middle"], gain_one, attn_w
        )
        gain_one_grads.append(gain_one_grad[0:1])
        input_grads.append(input_grad)
        ffn_out = scatter_rows(contract_last(k["activated"], full_down_t))
        outputs.append(jnp.where(valids[b], k["middle"] + ffn_out, 0.0).astype(BF16))

    odd = (tensor_index & 1) == 1
    high = (tensor_index & 2) == 2
    query_grad = [query_grads[:, c * third : (c + 1) * third] for c in range(3)]
    branch_grad = [branch[:, c * third : (c + 1) * third] for c in range(3)]
    key_grad, value_grad = pair_grads[:, :third], pair_grads[:, third:]

    def traded(left_even, right_even, left_odd, right_odd):
        def product(flag):
            left = left_even if left_even is left_odd else pick(flag, left_odd, left_even)
            return contract_rows(left, pick(flag, right_odd, right_even))

        sent = row_major(product(jnp.logical_not(odd)).astype(BF16))
        return row_major(product(odd)) + near(sent).astype(F32)

    query_low = traded(normed, query_grad[0], normed, query_grad[1])
    query_high = traded(normed, query_grad[2], attended, branch_grad[0])
    pair_low = traded(normed, key_grad, normed, value_grad)
    pair_high = traded(attended, branch_grad[1], attended, branch_grad[2])
    data_count = lax.axis_size("dp")
    gain_part = jnp.stack([sum(gain_one_grads), sum(gain_two_grads)])[:, 0]
    gain_part = jnp.moveaxis(gain_part.reshape(2, data_count, -1), 1, 0)
    gain_share = gain_part.shape[2]
    gain_part = jnp.pad(gain_part, ((0, 0), (0, 14), (0, third - gain_share)))
    first, second, gain_rows = sum_over_data(
        (pick(high, pair_high, pair_low), pick(high, pair_low, pair_high)),
        (pick(high, query_high, query_low), pick(high, query_low, query_high)),
        gain_part,
    )
    quarter = jnp.concatenate([first, second, gain_rows], axis=0).astype(BF16)
    other = far(quarter)
    pair = jnp.stack([pick(high, other, quarter), pick(high, quarter, other)])
    other = near(pair)
    even_pair, odd_pair = pick(odd, other, pair).astype(F32), pick(odd, pair, other).astype(F32)
    share = first.shape[0]
    chunks = [even_pair[0], odd_pair[0], even_pair[1], odd_pair[1]]
    gain_sum = sum(c[2 * share :] for c in chunks)
    first_of = [c[:share] for c in chunks]
    second_of = [c[share : 2 * share] for c in chunks]
    grad_mlp_w = grad_mlp_w.astype(F32)
    return (
        jnp.stack(outputs)[:, None],
        jnp.stack(input_grads)[:, None],
        gain_sum[0, :gain_share],
        gain_sum[1, :gain_share],
        jnp.concatenate(second_of[:3], axis=1),
        first_of[0],
        first_of[1],
        grad_mlp_w[:, :hidden_share],
        grad_mlp_w[:, hidden_share : 2 * hidden_share],
        jnp.concatenate([second_of[3], first_of[2], first_of[3]], axis=1),
        grad_mlp_w[:, 2 * hidden_share :].T,
    )


def solution(mesh):
    in_specs = (
        P(None, "dp", "tensor", None),
        P(None, "dp"),
        P("dp"),
        P("dp"),
        P("dp", None),
        P("dp", None),
        P("dp", None),
        P("dp", "tensor"),
        P("dp", "tensor"),
        P("dp", None),
        P("tensor", "dp"),
        P(None, "dp", "tensor", None),
    )
    out_specs = (
        P(None, "dp", "tensor", None),
        P(None, "dp", "tensor", None),
        P("dp"),
        P("dp"),
        P("dp", None),
        P("dp", None),
        P("dp", None),
        P("dp", "tensor"),
        P("dp", "tensor"),
        P("dp", None),
        P("tensor", "dp"),
    )
    return jax.shard_map(shards, mesh=mesh, in_specs=in_specs, out_specs=out_specs, check_vma=False)
```

time: 593 us -> 439 us (0.74)
  waiting for transfers between devices: 262 us -> 117 us
  local copies, waits for them, and re-layouts: 56.5 us -> 38 us
  starting transfers between devices: 20.4 us -> 29.5 us
  Pallas kernels: 92.5 us -> 101 us
    all_gather x1, waiting for transfers between devices: 80.5 us -> 0.69 us  [shards(): mlp_full = lax.all_gather(mlp_local, 'dp', axis=0, tiled=True)]
    ppermute x13 -> x14, waiting for transfers between devices: 107 us -> 57.2 us  [far(): return lax.ppermute(value, 'tensor', [(i, i ^ 2) for i in range(count)])]
    unnamed x6 -> x3, waiting for transfers between devices: 42.1 us -> 0.05 us
    ppermute x0 -> x8, waiting for transfers between devices: none -> 25 us  [the longest x6 23.4 us: along(): total = total + lax.ppermute(sent, 'dp', moves).astype(F32)]
    unnamed x186 -> x143, local copies, waits for them, and re-layouts: 32.3 us -> 16 us
    ppermute x0 -> x8, starting transfers between devices: none -> 9.53 us  [the longest x6 8 us: along(): total = total + lax.ppermute(sent, 'dp', moves).astype(F32)]
    pallas_call x14, Pallas kernels: 92.5 us -> 101 us  [call(): pl.pallas_call(kernel, grid_spec=pltpu.PrefetchScalarGridSpec(num_scalar_...]
    add x6 -> x5, other arithmetic: 6.86 us -> 0.37 us  [the longest x1 0.22 us: sum_over_data(): first = split(part_a[0] + far(part_a[1].astype(BF16)).astype(F32))]
  transfers between devices with their start and end apart: 32 -> 43, of which waited for: 16 -> 16; matrix products, arithmetic and copies ran while one was open for 25% -> 28% of each run, Pallas kernels for 16% -> 23%
where the time goes in v3:
time: 439 us; the launch traced here: 432 us
  waiting for transfers between devices  117 us (27%)
  Pallas kernels  101 us (23%)
  matrix products  72.3 us (16%)
  local copies, waits for them, and re-layouts  38 us (9%)
  other arithmetic  33.2 us (8%)
  starting transfers between devices  29.5 us (7%)
  blocking collectives  20.8 us (5%)
  between operations  20.7 us (5%)
    pallas_call x14, Pallas kernels, call(): pl.pallas_call(kernel, grid_spec=pltpu.PrefetchScalarGridSpec(num_scalar_...  101 us
    ppermute x14, waiting for transfers between devices, far(): return lax.ppermute(value, 'tensor', [(i, i ^ 2) for i in range(count)])  57.2 us
    all_gather x1, waiting for transfers between devices, shards(): attn_w = lax.all_gather(attn_quarter, ('tensor', 'dp'), axis=0, tiled=True)  33.8 us
    dot_general x14, matrix products, contract_rows(): lax.dot_general(left_side, right_side, (((0,), (0,)), ((), ())), preferre...  30.3 us
    dot_general x6, matrix products, dot(): return jnp.dot(left_side, right_side, preferred_element_type=F32)  24.7 us
    ppermute x6, waiting for transfers between devices, along(): total = total + lax.ppermute(sent, 'dp', moves).astype(F32)  23.4 us
    all_gather x1, blocking collectives, shards(): lax.all_gather(jnp.stack([gain_attn, gain_mlp]), 'dp', axis=1, tiled=True)  20.8 us
    ppermute x14, starting transfers between devices, far(): return lax.ppermute(value, 'tensor', [(i, i ^ 2) for i in range(count)])  17.4 us
  transfers between devices with their start and end apart: 43, of which 16 were waited for; matrix products, arithmetic and copies ran while one was open for 28% of the time, Pallas kernels for 23%

profile of v3, /device:TPU:0, one launch (start us, length us, event | category | flops | bytes accessed | tf_op | source)
XLA Modules:
  0.0 432.4 jit_solution(1979532126128935801)
XLA Ops:
  17.0 20.8 %all-gather = bf16[8,144,2]{1,2,0:T(2,128)(2,1)S(1)} all-gather(bf16[1,144,2]{1,2,0:T(2,128)(2,1)S(1)} %maximum_bitcast_fusion.3), channel_id=1, replica_groups=mesh['dp'=8,'tensor'=4] {'dp'}, dimensions={0}, use_global_device_ids=true | all-gather | bytes 5184 | tf_op jit(solution)/shard_map/all_gather | solution.py:523
  38.4 8.6 %collective-permute-done.5 = bf16[2,256,1152]{2,1,0:T(8,128)(2,1)S(1)} collective-permute-done((bf16[2,256,1152]{2,1,0:T(8,128)(2,1)S(1)}, bf16[2,256,1152]{2,1,0:T(8,128)(2,1)S(1)}, u32[]{:S(2)}, u32[]{:S(2)}) %collective-permute-start.5) | collective-permute-done | bytes 1179680 | tf_op jit(solution)/shard_map/ppermute | solution.py:28
  54.7 33.8 %all-gather.4.cloned.1.call-done.wk.wv.w0.w1.w2 = bf16[4608,768]{1,0:T(8,128)(2,1)} async-done(((bf16[144,768]{1,0:T(8,128)(2,1)}), bf16[4608,768]{1,0:T(8,128)(2,1)}) %all-gather.4.cloned.1.call-update) | async-done | bytes 7077904 | tf_op jit(solution)/shard_map/all_gather | solution.py:520
  88.4 4.1 project_pairs.1
  96.5 8.2 %collective-permute-done.p1 = bf16[256,768]{1,0:T(8,128)(2,1)S(1)} collective-permute-done((bf16[256,768]{1,0:T(8,128)(2,1)S(1)}, bf16[256,768]{1,0:T(8,128)(2,1)S(1)}, u32[]{:S(2)}, u32[]{:S(2)}) %collective-permute-start) | collective-permute-done | bytes 393248 | tf_op jit(solution)/shard_map/ppermute | solution.py:28
  104.7 7.8 %collective-permute-done.7.p1 = bf16[256,768]{1,0:T(8,128)(2,1)S(1)} collective-permute-done((bf16[256,768]{1,0:T(8,128)(2,1)S(1)}, bf16[256,768]{1,0:T(8,128)(2,1)S(1)}, u32[]{:S(2)}, u32[]{:S(2)}) %collective-permute-start.7) | collective-permute-done | bytes 393248 | tf_op jit(solution)/shard_map/ppermute | solution.py:28
  113.5 4.5 %project_queries.1.q_ref = bf16[512,1152]{1,0:T(8,128)(2,1)S(1)} custom-call(bf16[512,1152]{1,0:T(8,128)(2,1)} %get-tuple-element.38.normed_ref, f32[512,128]{1,0:T(8,128)S(1)} %get-tuple-element.174.cosine_ref, f32[512,128]{1,0:T(8,128)S(1)} %get-tuple-element.175.sine_ref, bf16[4608,768]{1,0:T(8,128)(2,1)} %all-gather.4.cloned.1.call-done.wk.wv.w0.w1.w2, ...), custom_call_target="tpu_custom_call" | custom-call | flops 1 | bytes 1 | tf_op jit(solution)/shard_map/project_queries/pallas_call | solution.py:93
  119.1 12.8 %attend.2.o_ref.rest_0_ = bf16[512,1152]{1,0:T(8,128)(2,1)} custom-call(s32[4]{0:T(128)S(1)} %get-tuple-element.181.counts, bf16[512,1152]{1,0:T(8,128)(2,1)} %copy-done, bf16[512,768]{1,0:T(8,128)(2,1)S(1)} %get-tuple-element.39.p0, bf16[256,768]{1,0:T(8,128)(2,1)S(1)} %collective-permute-done.p1, bf16[256,768]{1,0:T(8,128)(2,1)S(1)} %collective-permute-done.1.p2, ...), custom_call_target="tpu_custom_call" | custom-call | flops 1 | bytes 1 | tf_op jit(solution)/shard_map/attend/pallas_call | solution.py:93
  131.9 3.3 leave.2
  137.7 13.0 %attend.3.o_ref = bf16[512,1152]{1,0:T(8,128)(2,1)} custom-call(s32[4]{0:T(128)S(1)} %get-tuple-element.182.counts, bf16[512,1152]{1,0:T(8,128)(2,1)} %copy-done, bf16[512,768]{1,0:T(8,128)(2,1)S(1)} %get-tuple-element.39.p0, bf16[256,768]{1,0:T(8,128)(2,1)S(1)} %collective-permute-done.7.p1, ...), custom_call_target="tpu_custom_call", output_to_operand_aliasing={{}: (6, {})} | custom-call | flops 1 | bytes 1 | tf_op jit(solution)/shard_map/attend/pallas_call | solution.py:93
  158.9 13.8 %collective-permute-done.10 = bf16[256,1152]{1,0:T(8,128)(2,1)S(1)} collective-permute-done((bf16[256,1152]{1,0:T(8,128)(2,1)S(1)}, bf16[256,1152]{1,0:T(8,128)(2,1)S(1)}, u32[]{:S(2)}, u32[]{:S(2)}) %collective-permute-start.10) | collective-permute-done | bytes 589856 | tf_op jit(solution)/shard_map/ppermute | solution.py:28
  176.9 6.2 %fusion.38 = f32[1024,768]{1,0:T(8,128)} fusion(bf16[1152,2304]{1,0:T(8,128)(2,1)} %all-gather.6.cloned.1.call-done, bf16[256,1152]{1,0:T(8,128)(2,1)} %get-tuple-element.124, bf16[256,1152]{1,0:T(8,128)(2,1)} %get-tuple-element.121, bf16[256,1152]{1,0:T(8,128)(2,1)} %get-tuple-element.127, bf16[256,1152]{1,0:T(8,128)(2,1)} %get-tuple-element.125), kind=kOutput, calls=%fused_computation.89 | convolution fusion | flops 1821376512 | bytes 7274496 | tf_op jit(solution)/shard_map/dot_general | solution.py:39
  187.7 3.9 fusion.28
  191.6 4.9 %multiply_convert_fusion.4 = (bf16[1024,768]{1,0:T(8,128)(2,1)S(1)}, bf16[1024,768]{1,0:T(8,128)(2,1)S(1)}, bf16[1024,768]{1,0:T(8,128)(2,1)S(1)}) fusion(f32[1024,768]{1,0:T(8,128)S(1)} %fusion.36, f32[1024,768]{1,0:T(8,128)S(1)} %fusion.28, bf16[1024,1152]{1,0:T(8,128)(2,1)} %constant_dynamic-update-slice_fusion.3, bf16[1152,2304]{1,0:T(8,128)(2,1)S(1)} %copy-done.57), kind=kOutput, calls=%fused_computation.19 | convolution fusion | flops 1824522240 | bytes 15138816 | tf_op jit(solution)/shard_map/dot_general | solution.py:39
  202.4 3.7 fusion.108
  206.2 3.9 fusion.49
  213.7 3.7 fusion.107
  217.5 5.3 %multiply_convert_fusion.5 = (bf16[1024,768]{1,0:T(8,128)(2,1)S(1)}, bf16[1024,768]{1,0:T(8,128)(2,1)S(1)}, bf16[1024,768]{1,0:T(8,128)(2,1)S(1)}) fusion(f32[1024,768]{1,0:T(8,128)} %fusion.38, f32[1024,768]{1,0:T(8,128)S(1)} %fusion.30, bf16[1024,1152]{1,0:T(8,128)(2,1)S(1)} %constant_dynamic-update-slice_fusion, bf16[1152,2304]{1,0:T(8,128)(2,1)S(1)} %copy-done.57), kind=kOutput, calls=%fused_computation.21 | convolution fusion | flops 1824522240 | bytes 15138816 | tf_op jit(solution)/shard_map/dot_general | solution.py:39
  250.6 5.8 %fusion.34 = f32[1024,1152]{1,0:T(8,128)} fusion(bf16[1024,768]{1,0:T(8,128)(2,1)S(1)} %copy-done.61, bf16[1152,2304]{1,0:T(8,128)(2,1)} %all-gather.6.cloned.1.call-done), kind=kOutput, calls=%fused_computation.85 | convolution fusion | flops 1811939328 | bytes 8060928 | tf_op jit(solution)/shard_map/dot_general | solution.py:49
  264.6 5.0 %enter.2 = (f32[256,1152]{1,0:T(8,128)}, bf16[512,1152]{1,0:T(8,128)(2,1)}, bf16[256,1152]{1,0:T(8,128)(2,1)S(1)}, f32[8,1152]{1,0:T(8,128)S(1)}) custom-call(s32[1]{0:T(128)} %bitcast.2.count, f32[1024,1152]{1,0:T(8,128)} %copy-done.20, bf16[512,1152]{1,0:T(8,128)(2,1)} %copy-done.31, bf16[256,1152]{1,0:T(8,128)(2,1)S(1)} %collective-permute-done.19.far_ref, ...), custom_call_target="tpu_custom_call" | custom-call | flops 1 | bytes 1 | tf_op jit(solution)/shard_map/enter/pallas_call | solution.py:93
  269.6 18.5 %attend_back.2 = (bf16[512,1152]{1,0:T(8,128)(2,1)}, bf16[512,768]{1,0:T(8,128)(2,1)}, bf16[512,768]{1,0:T(8,128)(2,1)}) custom-call(s32[4]{0:T(128)S(1)} %get-tuple-element.181.counts, bf16[512,1152]{1,0:T(8,128)(2,1)} %copy-done, bf16[256,1152]{1,0:T(8,128)(2,1)S(1)} %get-tuple-element.48.g_ref, f32[32,256]{1,0:T(8,128)S(1)} %copy-done.9, ...), custom_call_target="tpu_custom_call" | custom-call | flops 1 | bytes 1 | tf_op jit(solution)/shard_map/attend_back/pallas_call | solution.py:93
  291.2 5.0 %enter.3 = (f32[256,1152]{1,0:T(8,128)}, bf16[512,1152]{1,0:T(8,128)(2,1)}, bf16[256,1152]{1,0:T(8,128)(2,1)S(1)}, f32[8,1152]{1,0:T(8,128)S(1)}) custom-call(s32[1]{0:T(128)} %bitcast.19.count, f32[1024,1152]{1,0:T(8,128)} %copy-done.19, bf16[512,1152]{1,0:T(8,128)(2,1)} %collective-permute-done.16.near_ref, ...), custom_call_target="tpu_custom_call", output_to_operand_aliasing={{1}: (10, {})} | custom-call | flops 1 | bytes 1 | tf_op jit(solution)/shard_map/enter/pallas_call | solution.py:93
  296.2 18.6 %attend_back.3 = (bf16[512,1152]{1,0:T(8,128)(2,1)}, bf16[512,768]{1,0:T(8,128)(2,1)}, bf16[512,768]{1,0:T(8,128)(2,1)}) custom-call(s32[4]{0:T(128)S(1)} %get-tuple-element.182.counts, bf16[512,1152]{1,0:T(8,128)(2,1)} %copy-done, bf16[256,1152]{1,0:T(8,128)(2,1)S(1)} %get-tuple-element.47.g_ref, ...), custom_call_target="tpu_custom_call", output_to_operand_aliasing={{0}: (9, {})} | custom-call | flops 1 | bytes 1 | tf_op jit(solution)/shard_map/attend_back/pallas_call | solution.py:93
  325.3 5.9 %collective-permute-done.23.far_ref = bf16[256,768]{1,0:T(8,128)(2,1)S(1)} collective-permute-done((bf16[256,768]{1,0:T(8,128)(2,1)S(1)}, bf16[256,768]{1,0:T(8,128)(2,1)S(1)}, u32[]{:S(2)}, u32[]{:S(2)}) %collective-permute-start.23) | collective-permute-done | bytes 393248 | tf_op jit(solution)/shard_map/ppermute | solution.py:28
  334.5 5.1 %collective-permute-done.21.far_ref = bf16[256,768]{1,0:T(8,128)(2,1)S(1)} collective-permute-done((bf16[256,768]{1,0:T(8,128)(2,1)S(1)}, bf16[256,768]{1,0:T(8,128)(2,1)S(1)}, u32[]{:S(2)}, u32[]{:S(2)}) %collective-permute-start.21) | collective-permute-done | bytes 393248 | tf_op jit(solution)/shard_map/ppermute | solution.py:28
  356.7 5.1 %finish.3 = (bf16[256,1152]{1,0:T(8,128)(2,1)S(1)}, f32[8,1152]{1,0:T(8,128)S(1)}) custom-call(bf16[512,1152]{1,0:T(8,128)(2,1)} %bitcast.200, bf16[512,1152]{1,0:T(8,128)(2,1)} %get-tuple-element.50.query_ref, bf16[512,768]{1,0:T(8,128)(2,1)S(1)} %pairs_back.3.pair_ref, f32[256,1152]{1,0:T(8,128)} %get-tuple-element.57.middle_ref, ...), custom_call_target="tpu_custom_call" | custom-call | flops 1 | bytes 1 | tf_op jit(solution)/shard_map/finish/pallas_call | solution.py:93
  361.8 5.1 %finish.2 = (bf16[256,1152]{1,0:T(8,128)(2,1)S(1)}, f32[8,1152]{1,0:T(8,128)S(1)}) custom-call(bf16[512,1152]{1,0:T(8,128)(2,1)} %bitcast.201, bf16[512,1152]{1,0:T(8,128)(2,1)} %get-tuple-element.50.query_ref, bf16[512,768]{1,0:T(8,128)(2,1)S(1)} %pairs_back.3.pair_ref, f32[256,1152]{1,0:T(8,128)} %get-tuple-element.55.middle_ref, ...), custom_call_target="tpu_custom_call" | custom-call | flops 1 | bytes 1 | tf_op jit(solution)/shard_map/finish/pallas_call | solution.py:93
  384.3 9.4 %collective-permute-done.35 = bf16[2,144,384]{2,1,0:T(8,128)(2,1)S(1)} collective-permute-done((bf16[2,144,384]{2,1,0:T(8,128)(2,1)S(1)}, bf16[2,144,384]{2,1,0:T(8,128)(2,1)S(1)}, u32[]{:S(2)}, u32[]{:S(2)}) %collective-permute-start.35) | collective-permute-done | bytes 221216 | tf_op jit(solution)/shard_map/ppermute | solution.py:473
  395.9 3.8 collective-permute-start.30
  399.7 4.3 collective-permute-done.28
  404.0 4.3 %collective-permute-done.29 = bf16[160,384]{1,0:T(8,128)(2,1)S(1)} collective-permute-done((bf16[160,384]{1,0:T(8,128)(2,1)S(1)}, bf16[160,384]{1,0:T(8,128)(2,1)S(1)}, u32[]{:S(2)}, u32[]{:S(2)}) %collective-permute-start.29) | collective-permute-done | bytes 122912 | tf_op jit(solution)/shard_map/ppermute | solution.py:473
  410.3 5.7 %collective-permute-done.38 = bf16[304,384]{1,0:T(8,128)(2,1)S(1)} collective-permute-done((bf16[304,384]{1,0:T(8,128)(2,1)S(1)}, bf16[304,384]{1,0:T(8,128)(2,1)S(1)}, u32[]{:S(2)}, u32[]{:S(2)}) %collective-permute-start.38) | collective-permute-done | bytes 233504 | tf_op jit(solution)/shard_map/ppermute | solution.py:28
  (321 shorter events, 147.9 us)
Async XLA Ops:
  7.2 81.2 %all-gather.4.cloned.1.call-start = ((), (), s32[]{:S(2)}) async-start(), calls=%async_computation.1 | async-start | bytes 7299072 | tf_op jit(solution)/shard_map/all_gather | solution.py:520
  10.5 166.3 %all-gather.6.cloned.1.call-start = ((), (), s32[]{:S(2)}) async-start(), calls=%async_computation.2 | async-start | bytes 5971968 | tf_op jit(solution)/shard_map/all_gather | solution.py:522
  11.5 410.9 %reduce-scatter.2.cloned.1.call-start = ((), (), s32[]{:S(2)}) async-start(), calls=%async_computation.3 | async-start | bytes 5971968 | tf_op jit(solution)/shard_map/reduce_scatter | solution.py:643
  13.9 33.0 %collective-permute-start.5 = (bf16[2,256,1152]{2,1,0:T(8,128)(2,1)S(1)}, bf16[2,256,1152]{2,1,0:T(8,128)(2,1)S(1)}, u32[]{:S(2)}, u32[]{:S(2)}) collective-permute-start(bf16[2,256,1152]{2,1,0:T(8,128)(2,1)S(1)} %get-tuple-element.130), channel_id=1, source_target_pairs={{0,2},{1,3},{2,0},{3,1},{4,6},{5,7},{6,4},{7,5},{8,10},{9,11},{10,... | collective-permute-start | bytes 3538952 | tf_op jit(solution)/shard_map/ppermute | solution.py:28
  48.8 101.9 %collective-permute-start.6 = (bf16[2,2,256,1152]{3,2,1,0:T(8,128)(2,1)}, bf16[2,2,256,1152]{3,2,1,0:T(8,128)(2,1)}, u32[]{:S(2)}, u32[]{:S(2)}) collective-permute-start(bf16[2,2,256,1152]{3,2,1,0:T(8,128)(2,1)} %pad_maximum_fusion.1), channel_id=1, source_target_pairs={{0,1},{1,0},{2,3},{3,2},{4,5},{5,4},{6,7},{7,6},{8,9},{9,8},{10,11... | collective-permute-start | bytes 7077896 | tf_op jit(solution)/shard_map/ppermute | solution.py:23
  92.6 12.0 %collective-permute-start = (bf16[256,768]{1,0:T(8,128)(2,1)S(1)}, bf16[256,768]{1,0:T(8,128)(2,1)S(1)}, u32[]{:S(2)}, u32[]{:S(2)}) collective-permute-start(bf16[256,768]{1,0:T(8,128)(2,1)S(1)} %get-tuple-element.146), channel_id=1, source_target_pairs={{0,2},{1,3},{2,0},{3,1},{4,6},{5,7},{6,4},{7,5},{8,10},{9,11},{10,... | collective-permute-start | bytes 1179656 | tf_op jit(solution)/shard_map/ppermute | solution.py:28
  94.2 18.2 %collective-permute-start.7 = (bf16[256,768]{1,0:T(8,128)(2,1)S(1)}, bf16[256,768]{1,0:T(8,128)(2,1)S(1)}, u32[]{:S(2)}, u32[]{:S(2)}) collective-permute-start(bf16[256,768]{1,0:T(8,128)(2,1)S(1)} %get-tuple-element.147), channel_id=1, source_target_pairs={{0,2},{1,3},{2,0},{3,1},{4,6},{5,7},{6,4},{7,5},{8,10},{9,11},{10,... | collective-permute-start | bytes 1179656 | tf_op jit(solution)/shard_map/ppermute | solution.py:28
  95.9 23.1 %collective-permute-start.1 = (bf16[256,768]{1,0:T(8,128)(2,1)S(1)}, bf16[256,768]{1,0:T(8,128)(2,1)S(1)}, u32[]{:S(2)}, u32[]{:S(2)}) collective-permute-start(bf16[256,768]{1,0:T(8,128)(2,1)S(1)} %get-tuple-element.146), channel_id=1, source_target_pairs={{0,1},{1,0},{2,3},{3,2},{4,5},{5,4},{6,7},{7,6},{8,9},{9,8},{10,11... | collective-permute-start | bytes 1179656 | tf_op jit(solution)/shard_map/ppermute | solution.py:23
  96.0 41.8 %collective-permute-start.8 = (bf16[256,768]{1,0:T(8,128)(2,1)S(1)}, bf16[256,768]{1,0:T(8,128)(2,1)S(1)}, u32[]{:S(2)}, u32[]{:S(2)}) collective-permute-start(bf16[256,768]{1,0:T(8,128)(2,1)S(1)} %get-tuple-element.147), channel_id=1, source_target_pairs={{0,1},{1,0},{2,3},{3,2},{4,5},{5,4},{6,7},{7,6},{8,9},{9,8},{10,11... | collective-permute-start | bytes 1179656 | tf_op jit(solution)/shard_map/ppermute | solution.py:23
  104.7 14.4 %collective-permute-start.2 = (bf16[256,768]{1,0:T(8,128)(2,1)S(1)}, bf16[256,768]{1,0:T(8,128)(2,1)S(1)}, u32[]{:S(2)}, u32[]{:S(2)}) collective-permute-start(bf16[256,768]{1,0:T(8,128)(2,1)S(1)} %collective-permute-done.p1), channel_id=1, source_target_pairs={{0,1},{1,0},{2,3},{3,2},{4,5},{5,4},{6,7},{7,6},{8,9},{9,8},{10,11... | collective-permute-start | bytes 1179656 | tf_op jit(solution)/shard_map/ppermute | solution.py:23
  112.4 25.3 %collective-permute-start.9 = (bf16[256,768]{1,0:T(8,128)(2,1)S(1)}, bf16[256,768]{1,0:T(8,128)(2,1)S(1)}, u32[]{:S(2)}, u32[]{:S(2)}) collective-permute-start(bf16[256,768]{1,0:T(8,128)(2,1)S(1)} %collective-permute-done.7.p1), channel_id=1, source_target_pairs={{0,1},{1,0},{2,3},{3,2},{4,5},{5,4},{6,7},{7,6},{8,9},{9,8},{10,11... | collective-permute-start | bytes 1179656 | tf_op jit(solution)/shard_map/ppermute | solution.py:23
  136.2 22.5 %collective-permute-start.3 = (bf16[256,1152]{1,0:T(8,128)(2,1)S(1)}, bf16[256,1152]{1,0:T(8,128)(2,1)S(1)}, u32[]{:S(2)}, u32[]{:S(2)}) collective-permute-start(bf16[256,1152]{1,0:T(8,128)(2,1)S(1)} %get-tuple-element.40), channel_id=1, source_target_pairs={{0,2},{1,3},{2,0},{3,1},{4,6},{5,7},{6,4},{7,5},{8,10},{9,11},{10,... | collective-permute-start | bytes 1769480 | tf_op jit(solution)/shard_map/ppermute | solution.py:28
  157.1 15.5 %collective-permute-start.10 = (bf16[256,1152]{1,0:T(8,128)(2,1)S(1)}, bf16[256,1152]{1,0:T(8,128)(2,1)S(1)}, u32[]{:S(2)}, u32[]{:S(2)}) collective-permute-start(bf16[256,1152]{1,0:T(8,128)(2,1)S(1)} %get-tuple-element.41), channel_id=1, source_target_pairs={{0,2},{1,3},{2,0},{3,1},{4,6},{5,7},{6,4},{7,5},{8,10},{9,11},{10,... | collective-permute-start | bytes 1769480 | tf_op jit(solution)/shard_map/ppermute | solution.py:28
  158.8 51.3 %collective-permute-start.4 = (bf16[512,1152]{1,0:T(8,128)(2,1)S(1)}, bf16[512,1152]{1,0:T(8,128)(2,1)}, u32[]{:S(2)}, u32[]{:S(2)}) collective-permute-start(bf16[512,1152]{1,0:T(8,128)(2,1)S(1)} %pad_maximum_fusion.5), channel_id=1, source_target_pairs={{0,1},{1,0},{2,3},{3,2},{4,5},{5,4},{6,7},{7,6},{8,9},{9,8},{10,11... | collective-permute-start | bytes 3538952 | tf_op jit(solution)/shard_map/ppermute | solution.py:23
  173.8 11.5 %collective-permute-start.11 = (bf16[512,1152]{1,0:T(8,128)(2,1)}, bf16[512,1152]{1,0:T(8,128)(2,1)}, u32[]{:S(2)}, u32[]{:S(2)}) collective-permute-start(bf16[512,1152]{1,0:T(8,128)(2,1)} %pad_maximum_fusion.7), channel_id=1, source_target_pairs={{0,1},{1,0},{2,3},{3,2},{4,5},{5,4},{6,7},{7,6},{8,9},{9,8},{10,11... | collective-permute-start | bytes 3538952 | tf_op jit(solution)/shard_map/ppermute | solution.py:23
  200.0 88.1 %collective-permute-start.14 = (bf16[512,1152]{1,0:T(8,128)(2,1)}, bf16[512,1152]{1,0:T(8,128)(2,1)}, u32[]{:S(2)}, u32[]{:S(2)}) collective-permute-start(bf16[512,1152]{1,0:T(8,128)(2,1)} %slice.629), channel_id=1, source_target_pairs={{0,1},{1,0},{2,3},{3,2},{4,5},{5,4},{6,7},{7,6},{8,9},{9,8},{10,11... | collective-permute-start | bytes 3538952 | tf_op jit(solution)/shard_map/ppermute | solution.py:23
  232.0 14.0 %collective-permute-start.18 = (bf16[512,1152]{1,0:T(8,128)(2,1)}, bf16[512,1152]{1,0:T(8,128)(2,1)S(1)}, u32[]{:S(2)}, u32[]{:S(2)}) collective-permute-start(bf16[512,1152]{1,0:T(8,128)(2,1)} %slice.627), channel_id=1, source_target_pairs={{0,1},{1,0},{2,3},{3,2},{4,5},{5,4},{6,7},{7,6},{8,9},{9,8},{10,11... | collective-permute-start | bytes 3538952 | tf_op jit(solution)/shard_map/ppermute | solution.py:23
  238.1 21.4 %collective-permute-start.16 = (bf16[512,1152]{1,0:T(8,128)(2,1)}, bf16[512,1152]{1,0:T(8,128)(2,1)}, u32[]{:S(2)}, u32[]{:S(2)}) collective-permute-start(bf16[512,1152]{1,0:T(8,128)(2,1)} %slice.628), channel_id=1, source_target_pairs={{0,1},{1,0},{2,3},{3,2},{4,5},{5,4},{6,7},{7,6},{8,9},{9,8},{10,11... | collective-permute-start | bytes 3538952 | tf_op jit(solution)/shard_map/ppermute | solution.py:23
  249.2 15.5 %collective-permute-start.19 = (bf16[256,1152]{1,0:T(8,128)(2,1)}, bf16[256,1152]{1,0:T(8,128)(2,1)S(1)}, u32[]{:S(2)}, u32[]{:S(2)}) collective-permute-start(bf16[256,1152]{1,0:T(8,128)(2,1)} %fusion.6), channel_id=1, source_target_pairs={{0,2},{1,3},{2,0},{3,1},{4,6},{5,7},{6,4},{7,5},{8,10},{9,11},{10,... | collective-permute-start | bytes 1769480 | tf_op jit(solution)/shard_map/ppermute | solution.py:28
  259.5 92.9 %collective-permute-start.12 = (bf16[512,1152]{1,0:T(8,128)(2,1)}, bf16[512,1152]{1,0:T(8,128)(2,1)}, u32[]{:S(2)}, u32[]{:S(2)}) collective-permute-start(bf16[512,1152]{1,0:T(8,128)(2,1)} %slice.630), channel_id=1, source_target_pairs={{0,1},{1,0},{2,3},{3,2},{4,5},{5,4},{6,7},{7,6},{8,9},{9,8},{10,11... | collective-permute-start | bytes 3538952 | tf_op jit(solution)/shard_map/ppermute | solution.py:23
  261.8 28.0 %collective-permute-start.17 = (bf16[256,1152]{1,0:T(8,128)(2,1)}, bf16[256,1152]{1,0:T(8,128)(2,1)S(1)}, u32[]{:S(2)}, u32[]{:S(2)}) collective-permute-start(bf16[256,1152]{1,0:T(8,128)(2,1)} %fusion.7), channel_id=1, source_target_pairs={{0,2},{1,3},{2,0},{3,1},{4,6},{5,7},{6,4},{7,5},{8,10},{9,11},{10,... | collective-permute-start | bytes 1769480 | tf_op jit(solution)/shard_map/ppermute | solution.py:28
  288.1 30.9 %collective-permute-start.22 = (bf16[512,768]{1,0:T(8,128)(2,1)}, bf16[512,768]{1,0:T(8,128)(2,1)S(1)}, u32[]{:S(2)}, u32[]{:S(2)}) collective-permute-start(bf16[512,768]{1,0:T(8,128)(2,1)} %get-tuple-element.54), channel_id=1, source_target_pairs={{0,1},{1,0},{2,3},{3,2},{4,5},{5,4},{6,7},{7,6},{8,9},{9,8},{10,11... | collective-permute-start | bytes 2359304 | tf_op jit(solution)/shard_map/ppermute | solution.py:23
  318.6 23.3 %collective-permute-start.31 = (bf16[1152,384]{1,0:T(8,128)(2,1)S(1)}, bf16[1152,384]{1,0:T(8,128)(2,1)}, u32[]{:S(2)}, u32[]{:S(2)}) collective-permute-start(bf16[1152,384]{1,0:T(8,128)(2,1)S(1)} %convolution_convert_fusion.1), channel_id=1, source_target_pairs={{0,1},{1,0},{2,3},{3,2},{4,5},{5,4},{6,7},{7,6},{8,9},{9,8},{10,11... | collective-permute-start | bytes 2654216 | tf_op jit(solution)/shard_map/ppermute | solution.py:23
  319.2 12.0 %collective-permute-start.23 = (bf16[256,768]{1,0:T(8,128)(2,1)S(1)}, bf16[256,768]{1,0:T(8,128)(2,1)S(1)}, u32[]{:S(2)}, u32[]{:S(2)}) collective-permute-start(bf16[256,768]{1,0:T(8,128)(2,1)S(1)} %add_convert_fusion), channel_id=1, source_target_pairs={{0,2},{1,3},{2,0},{3,1},{4,6},{5,7},{6,4},{7,5},{8,10},{9,11},{10,... | collective-permute-start | bytes 1179656 | tf_op jit(solution)/shard_map/ppermute | solution.py:28
  321.2 18.4 %collective-permute-start.21 = (bf16[256,768]{1,0:T(8,128)(2,1)S(1)}, bf16[256,768]{1,0:T(8,128)(2,1)S(1)}, u32[]{:S(2)}, u32[]{:S(2)}) collective-permute-start(bf16[256,768]{1,0:T(8,128)(2,1)S(1)} %add_convert_fusion.1), channel_id=1, source_target_pairs={{0,2},{1,3},{2,0},{3,1},{4,6},{5,7},{6,4},{7,5},{8,10},{9,11},{10,... | collective-permute-start | bytes 1179656 | tf_op jit(solution)/shard_map/ppermute | solution.py:28
  323.2 24.2 %collective-permute-start.24 = (bf16[1152,384]{1,0:T(8,128)(2,1)}, bf16[1152,384]{1,0:T(8,128)(2,1)S(1)}, u32[]{:S(2)}, u32[]{:S(2)}) collective-permute-start(bf16[1152,384]{1,0:T(8,128)(2,1)} %convolution_convert_fusion.3), channel_id=1, source_target_pairs={{0,1},{1,0},{2,3},{3,2},{4,5},{5,4},{6,7},{7,6},{8,9},{9,8},{10,11... | collective-permute-start | bytes 2654216 | tf_op jit(solution)/shard_map/ppermute | solution.py:23
  331.2 44.8 %collective-permute-start.15 = (bf16[256,1152]{1,0:T(8,128)(2,1)S(1)}, bf16[256,1152]{1,0:T(8,128)(2,1)}, u32[]{:S(2)}, u32[]{:S(2)}) collective-permute-start(bf16[256,1152]{1,0:T(8,128)(2,1)S(1)} %slice.631), channel_id=1, source_target_pairs={{0,2},{1,3},{2,0},{3,1},{4,6},{5,7},{6,4},{7,5},{8,10},{9,11},{10,... | collective-permute-start | bytes 1769480 | tf_op jit(solution)/shard_map/ppermute | solution.py:28
  346.8 21.8 %collective-permute-start.33 = (bf16[2,4,144,384]{3,2,1,0:T(8,128)(2,1)}, bf16[2,4,144,384]{3,2,1,0:T(8,128)(2,1)}, u32[]{:S(2)}, u32[]{:S(2)}) collective-permute-start(bf16[2,4,144,384]{3,2,1,0:T(8,128)(2,1)} %fusion.43), channel_id=1, source_target_pairs={{0,4},{4,0},{8,12},{12,8},{16,20},{20,16},{24,28},{28,24},{1,5},{5... | collective-permute-start | bytes 2654216 | tf_op jit(solution)/shard_map/ppermute | solution.py:464
  350.6 25.0 %collective-permute-start.26 = (bf16[1152,384]{1,0:T(8,128)(2,1)}, bf16[1152,384]{1,0:T(8,128)(2,1)S(1)}, u32[]{:S(2)}, u32[]{:S(2)}) collective-permute-start(bf16[1152,384]{1,0:T(8,128)(2,1)} %get-tuple-element.172), channel_id=1, source_target_pairs={{0,2},{1,3},{2,0},{3,1},{4,6},{5,7},{6,4},{7,5},{8,10},{9,11},{10,... | collective-permute-start | bytes 2654216 | tf_op jit(solution)/shard_map/ppermute | solution.py:28
  356.3 52.7 %collective-permute-start.13 = (bf16[256,1152]{1,0:T(8,128)(2,1)}, bf16[256,1152]{1,0:T(8,128)(2,1)}, u32[]{:S(2)}, u32[]{:S(2)}) collective-permute-start(bf16[256,1152]{1,0:T(8,128)(2,1)} %slice.632), channel_id=1, source_target_pairs={{0,2},{1,3},{2,0},{3,1},{4,6},{5,7},{6,4},{7,5},{8,10},{9,11},{10,... | collective-permute-start | bytes 1769480 | tf_op jit(solution)/shard_map/ppermute | solution.py:28
  375.6 18.2 %collective-permute-start.35 = (bf16[2,144,384]{2,1,0:T(8,128)(2,1)S(1)}, bf16[2,144,384]{2,1,0:T(8,128)(2,1)S(1)}, u32[]{:S(2)}, u32[]{:S(2)}) collective-permute-start(bf16[2,144,384]{2,1,0:T(8,128)(2,1)S(1)} %get-tuple-element.145), channel_id=1, source_target_pairs={{0,16},{4,20},{8,24},{12,28},{16,0},{20,4},{24,8},{28,12},{1,17},{... | collective-permute-start | bytes 663560 | tf_op jit(solution)/shard_map/ppermute | solution.py:473
  375.9 19.6 %collective-permute-start.27 = (bf16[4,160,384]{2,1,0:T(8,128)(2,1)S(1)}, bf16[4,160,384]{2,1,0:T(8,128)(2,1)S(1)}, u32[]{:S(2)}, u32[]{:S(2)}) collective-permute-start(bf16[4,160,384]{2,1,0:T(8,128)(2,1)S(1)} %fusion.46), channel_id=1, source_target_pairs={{0,4},{4,0},{8,12},{12,8},{16,20},{20,16},{24,28},{28,24},{1,5},{5... | collective-permute-start | bytes 1474568 | tf_op jit(solution)/shard_map/ppermute | solution.py:464
  (80 other events, 671.2 us)
Sparse Core Ops, SparseCore 0:
  11.6 76.7 all-gather.3
  91.2 85.5 all-gather.5
  256.6 101.4 reduce-scatter.1

commit v4 on v3

--- a/solution.py
+++ b/solution.py
@@ -26,13 +26,6 @@
 def far(value):
     count = lax.axis_size("tensor")
     return lax.ppermute(value, "tensor", [(i, i ^ 2) for i in range(count)])
-
-
-def scatter_rows(partial):
-    half = partial.shape[0] // 2
-    quarter = half // 2
-    kept = partial[:half].astype(F32) + near(partial[half:].astype(BF16)).astype(F32)
-    return kept[:quarter] + far(kept[quarter:].astype(BF16)).astype(F32)
 
 
 def dot(left_side, right_side):
@@ -101,7 +94,7 @@
         ),
         out_shape=outs,
         input_output_aliases=aliases or {},
-        compiler_params=pltpu.CompilerParams(vmem_limit_bytes=52 << 20),
+        compiler_params=pltpu.CompilerParams(vmem_limit_bytes=VMEM_MIB[name] << 20),
         cost_estimate=pl.CostEstimate(flops=1, transcendentals=0, bytes_accessed=1),
         name=name,
     )(*scalars, *arrays)
@@ -120,6 +113,17 @@
 
 
 ANY = pl.BlockSpec(memory_space=pl.ANY)
+VMEM_MIB = {
+    "project_pairs": 24,
+    "project_queries": 24,
+    "attend": 28,
+    "leave": 20,
+    "feed": 40,
+    "enter": 24,
+    "attend_back": 36,
+    "pairs_back": 12,
+    "finish": 28,
+}
 
 
 def project_pairs_kernel(x_ref, gain_ref, cosine_ref, sine_ref, wk, wv, pair_ref, normed_ref):
@@ -311,6 +315,78 @@
     )
 
 
+def feed_kernel(steps, low_ref, high_ref, grad_ref, weight_ref, *rest):
+    rows_ref, act_ref, inner_ref, out_low, out_high, back_low, back_high = rest[-7:]
+    step = pl.program_id(0)
+    share = weight_ref.shape[1] // 3
+    gate, up, down_t = (slice(i * share, (i + 1) * share) for i in range(3))
+
+    @pl.when(step < steps // 2)
+    def _():
+        rows_ref[...] = low_ref[...]
+
+    @pl.when(step >= steps // 2)
+    def _():
+        rows_ref[...] = high_ref[...]
+
+    rows = rows_ref[...]
+    gate_proj = dot_nn(rows, weight_ref[:, gate])
+    up_proj = dot_nn(rows, weight_ref[:, up])
+    grad_act = dot_nn(grad_ref[...], weight_ref[:, down_t])
+    sigma = 1.0 / (1.0 + jnp.exp(-gate_proj))
+    silu = gate_proj * sigma
+    act = (silu * up_proj).astype(BF16)
+    act_ref[...] = act
+    grad_gate = (grad_act * up_proj * sigma * (1.0 + gate_proj * (1.0 - sigma))).astype(BF16)
+    grad_up = (grad_act * silu).astype(BF16)
+    inner_ref[:, gate] = grad_gate
+    inner_ref[:, up] = grad_up
+    back = dot_nt(grad_gate, weight_ref[:, gate]) + dot_nt(grad_up, weight_ref[:, up])
+    out = dot_nt(act, weight_ref[:, down_t])
+
+    @pl.when(step < steps // 2)
+    def _():
+        out_low[...] = out.astype(BF16)
+        back_low[...] = back.astype(BF16)
+
+    @pl.when(step >= steps // 2)
+    def _():
+        out_high[...] = out.astype(BF16)
+        back_high[...] = back.astype(BF16)
+
+
+def feed(b, low, high, grads, weights, earlier):
+    half, width = low.shape
+    share = weights.shape[1] // 3
+    steps = 4
+    rows = 2 * half // steps
+    first = pl.BlockSpec((rows, width), lambda i: (jnp.minimum(i, steps // 2 - 1), 0))
+    second = pl.BlockSpec((rows, width), lambda i: (jnp.maximum(i - steps // 2, 0), 0))
+
+    def here(columns):
+        return pl.BlockSpec((rows, columns), lambda i: (b * steps + i, 0))
+
+    more = [] if earlier is None else list(earlier)
+    return call(
+        functools.partial(feed_kernel, steps),
+        "feed",
+        (low, high, grads, weights, *more),
+        [
+            first,
+            second,
+            here(width),
+            pl.BlockSpec(weights.shape, lambda i: (0, 0), pipeline_mode=pl.Buffered(1)),
+        ]
+        + [ANY] * len(more),
+        [array((4 * half, width)), array((4 * half, share)), array((4 * half, 2 * share))]
+        + [array((half, width))] * 4,
+        [here(width), here(share), here(2 * share), first, second, first, second],
+        24 * half * width * share,
+        aliases={4: 0, 5: 1, 6: 2} if more else None,
+        grid=(steps,),
+    )
+
+
 def enter_kernel(
     count, part_ref, near_ref, far_ref, middle_ref, cot_ref, gain_ref, w0, w1, w2, *rest
 ):
@@ -318,7 +394,9 @@
     rows, width = middle_ref.shape
     third = width // 3
     middle = middle_ref[...]
-    grad_normed = part_ref[...] + near_ref[...].astype(F32) + far_ref[...].astype(F32)
+    grad_normed = (
+        part_ref[...].astype(F32) + near_ref[...].astype(F32) + far_ref[...].astype(F32)
+    )
     scale = row_scale_of(middle)
     row = lax.broadcasted_iota(jnp.int32, (rows, width), 0)
     grad_row = jnp.where(row < count[0], cot_ref[...].astype(F32), 0.0)
@@ -434,11 +512,15 @@
     return with_layout_constraint(value, Layout(major_to_minor=tuple(range(value.ndim))))
 
 
+def added(first, second):
+    return (first.astype(F32) + second.astype(F32)).astype(BF16)
+
+
 def pick(flag, first, second):
     return jnp.where(flag, first, second)
 
 
-def sum_over_data(part_a, part_b, extra):
+def sum_over_data(part_a, part_b, extra, earlier):
     data_count = lax.axis_size("dp")
     data_index = lax.axis_index("dp")
     columns = part_a[0].shape[1]
@@ -452,7 +534,7 @@
         rows = jnp.concatenate([split(total), split(other), extra], axis=1).astype(BF16)
         rows = lax.psum_scatter(rows, "dp", scatter_dimension=0, tiled=True)[0].astype(F32)
         share = total.shape[0] // data_count
-        return rows[:share], rows[share : 2 * share], rows[2 * share :]
+        return rows[:share], rows[share : 2 * share], rows[2 * share :], earlier
 
     groups = data_count // 2
     odd = (data_index & 1) == 1
@@ -477,12 +559,12 @@
     second = beside(second.reshape(2, groups, 2, -1, columns))
     first = split(part_a[0] + far(part_a[1].astype(BF16)).astype(F32))
     first = jnp.concatenate([first, extra], axis=1).reshape(groups, 2, -1, columns)
-    first = beside(first)
+    first, earlier = lax.optimization_barrier((beside(first), earlier))
     second = along(jnp.moveaxis(second, 1, 0))
     first = along(first)
     second = second[0] + far(second[1].astype(BF16)).astype(F32)
     share = second.shape[0]
-    return first[:share], second, first[share:]
+    return first[:share], second, first[share:], earlier
 
 
 def shards(
@@ -553,10 +635,10 @@
     )
     grad_far = far(grad_own)
     grad_near = near(jnp.stack([grad_own, grad_far]))
-    grad_ffn = [
-        jnp.concatenate([grad_own[b], grad_far[b], grad_near[0, b], grad_near[1, b]], axis=0)
-        for b in range(micro)
-    ]
+    grad_ffn = jnp.concatenate(
+        [p[b] for b in range(micro) for p in (grad_own, grad_far, grad_near[0], grad_near[1])],
+        axis=0,
+    )
 
     x_rows = inputs[:, 0].reshape(micro * row_share, width)
     cot_rows = cotangent[:, 0].reshape(micro * row_share, width)
@@ -568,49 +650,34 @@
     attended = None
     for b in range(micro):
         own = pairs_own[b * row_share : (b + 1) * row_share]
+        if b > 0:
+            own, queries = lax.optimization_barrier((own, queries))
         across = far(own)
+        if b == 0:
+            across, queries = lax.optimization_barrier((across, queries))
         others = [across, near(own), near(across)]
         attended = attend(b, counts[b], queries, pairs_own, others, attended)
         middle, hidden_own = leave(b, x_rows, attended, gain_two, attn_w)
         across = far(hidden_own)
-        half = jnp.concatenate([hidden_own, across], axis=0)
-        hidden = jnp.concatenate([half, near(half)], axis=0)
-        kept.append(dict(others=others, middle=middle, hidden=hidden))
+        low = jnp.concatenate([hidden_own, across], axis=0)
+        kept.append(dict(others=others, middle=middle, low=low, high=near(low)))
         if b == micro - 1:
             mlp_full, _ = lax.optimization_barrier((mlp_full, across))
 
-    full_gate = mlp_full[:, :hidden_share]
-    full_up = mlp_full[:, hidden_share : 2 * hidden_share]
-    full_down_t = mlp_full[:, 2 * hidden_share :]
+    shared = None
     for b in range(micro):
         k = kept[b]
-        gate_proj = dot(k["hidden"], full_gate)
-        up_proj = dot(k["hidden"], full_up)
-        grad_act = dot(grad_ffn[b], full_down_t)
-        sigmoid_gate = jax.nn.sigmoid(gate_proj)
-        k["activated"] = (gate_proj * sigmoid_gate * up_proj).astype(BF16)
-        k["grad_gate"] = (
-            grad_act * up_proj * sigmoid_gate * (1.0 + gate_proj * (1.0 - sigmoid_gate))
-        ).astype(BF16)
-        k["grad_up"] = (grad_act * gate_proj * sigmoid_gate).astype(BF16)
-        k["part"] = contract_last(k["grad_gate"], full_gate) + contract_last(k["grad_up"], full_up)
-        k["near_part"] = near(k["part"][2 * row_share :].astype(BF16))
-        k["far_part"] = far(
-            (
-                k["part"][row_share : 2 * row_share] + k["near_part"][row_share:].astype(F32)
-            ).astype(BF16)
+        *shared, k["out_low"], k["out_high"], k["part"], back_high = feed(
+            b, k["low"], k["high"], grad_ffn, mlp_full, shared
         )
-
-    def total(left_side, right_side):
-        parts = [contract_rows(left_side(b), right_side(b)) for b in range(micro)]
-        return row_major(sum(parts[1:], parts[0]).astype(BF16))
-
+        k["near_part"] = near(back_high)
+        k["far_part"] = far(added(k["part"][row_share:], k["near_part"][row_share:]))
+    hidden_rows, activated, inner_grads = shared
     grad_mlp_w = row_major(
         jnp.concatenate(
             [
-                total(lambda b: kept[b]["hidden"], lambda b: kept[b]["grad_gate"]),
-                total(lambda b: kept[b]["hidden"], lambda b: kept[b]["grad_up"]),
-                total(lambda b: grad_ffn[b], lambda b: kept[b]["activated"]),
+                row_major(contract_rows(hidden_rows, inner_grads).astype(BF16)),
+                row_major(contract_rows(grad_ffn, activated).astype(BF16)),
             ],
             axis=1,
         )
@@ -620,7 +687,8 @@
     gain_two_grads = []
     branch = query_grads = pair_grads = None
 
-    def backward(b, branch, query_grads):
+    grad_mlp_w = lax.psum_scatter(grad_mlp_w, "dp", scatter_dimension=0, tiled=True)
+    for b in range(micro):
         k = kept[b]
         k["grad_middle"], branch, grad_att, gain_two_grad = enter(
             b,
@@ -635,23 +703,19 @@
             branch,
         )
         gain_two_grads.append(gain_two_grad[0:1])
-        query_grads, k["pair_kept"], k["pair_sent"] = attend_back(
+        if b > 0:
+            near_pair, grad_att = lax.optimization_barrier((kept[b - 1]["near_pair"], grad_att))
+            kept[b - 1]["near_pair"] = near_pair
+        query_grads, k["pair_kept"], pair_sent = attend_back(
             b, counts[b], queries, grad_att, cosine_t, sine_t, pairs_own, k["others"], query_grads
         )
-        return branch, query_grads
-
-    grad_mlp_w = lax.psum_scatter(grad_mlp_w, "dp", scatter_dimension=0, tiled=True)
-    for b in range(micro):
-        branch, query_grads = backward(b, branch, query_grads)
+        k["near_pair"] = near(pair_sent)
     for b in range(micro):
         k = kept[b]
-        near_pair = near(k["pair_sent"])
-        far_pair = far(
-            (k["pair_kept"][row_share:].astype(F32) + near_pair[row_share:].astype(F32)).astype(
-                BF16
-            )
+        far_pair = far(added(k["pair_kept"][row_share:], k["near_pair"][row_share:]))
+        pair_grads = pairs_back(
+            b, k["pair_kept"], k["near_pair"], far_pair, cosine, sine, pair_grads
         )
-        pair_grads = pairs_back(b, k["pair_kept"], near_pair, far_pair, cosine, sine, pair_grads)
 
     outputs, input_grads, gain_one_grads = [], [], []
     for b in range(micro):
@@ -661,7 +725,13 @@
         )
         gain_one_grads.append(gain_one_grad[0:1])
         input_grads.append(input_grad)
-        ffn_out = scatter_rows(contract_last(k["activated"], full_down_t))
+        out_near = near(k["out_high"])
+        out_far = far(added(k["out_low"][row_share:], out_near[row_share:]))
+        ffn_out = (
+            k["out_low"][:row_share].astype(F32)
+            + out_near[:row_share].astype(F32)
+            + out_far.astype(F32)
+        )
         outputs.append(jnp.where(valids[b], k["middle"] + ffn_out, 0.0).astype(BF16))
 
     odd = (tensor_index & 1) == 1
@@ -687,10 +757,11 @@
     gain_part = jnp.moveaxis(gain_part.reshape(2, data_count, -1), 1, 0)
     gain_share = gain_part.shape[2]
     gain_part = jnp.pad(gain_part, ((0, 0), (0, 14), (0, third - gain_share)))
-    first, second, gain_rows = sum_over_data(
+    first, second, gain_rows, grad_mlp_w = sum_over_data(
         (pick(high, pair_high, pair_low), pick(high, pair_low, pair_high)),
         (pick(high, query_high, query_low), pick(high, query_low, query_high)),
         gain_part,
+        grad_mlp_w,
     )
     quarter = jnp.concatenate([first, second, gain_rows], axis=0).astype(BF16)
     other = far(quarter)

time: 439 us -> 432 us (0.984)
  matrix products: 72.3 us -> 24.1 us
  waiting for transfers between devices: 117 us -> 148 us
  Pallas kernels: 101 us -> 112 us
    dot_general x12 -> x0, matrix products: 42 us -> none  [the longest x6 24.7 us: dot(): return jnp.dot(left_side, right_side, preferred_element_type=F32)]
    ppermute x14, waiting for transfers between devices: 57.2 us -> 70.7 us  [far(): return lax.ppermute(value, 'tensor', [(i, i ^ 2) for i in range(count)])]
    all_gather x1, waiting for transfers between devices: 0.69 us -> 11 us  [shards(): mlp_full = lax.all_gather(mlp_local, 'dp', axis=0, tiled=True)]
    pallas_call x14 -> x16, Pallas kernels: 101 us -> 112 us  [call(): pl.pallas_call(kernel, grid_spec=pltpu.PrefetchScalarGridSpec(num_scalar_...]
    unnamed x143 -> x164, local copies, waits for them, and re-layouts: 16 us -> 26.1 us
    slice x8 -> x2, local copies, waits for them, and re-layouts: 7.62 us -> 0.02 us  [sum_over_data(): return (first[:share], second, first[share:], earlier)]
    dot_general x14 -> x10, matrix products: 30.3 us -> 24.1 us  [contract_rows(): lax.dot_general(left_side, right_side, (((0,), (0,)), ((), ())), preferre...]
  transfers between devices with their start and end apart: 43 -> 43, of which waited for: 16 -> 19; matrix products, arithmetic and copies ran while one was open for 28% -> 12% of each run, Pallas kernels for 23% -> 22%
where the time goes in v4:
time: 432 us; the launch traced here: 426 us
  waiting for transfers between devices  148 us (34%)
  Pallas kernels  112 us (26%)
  local copies, waits for them, and re-layouts  35.3 us (8%)
  other arithmetic  34.3 us (8%)
  starting transfers between devices  31.5 us (7%)
  matrix products  24.1 us (6%)
  blocking collectives  20.8 us (5%)
  between operations  20.7 us (5%)
    pallas_call x16, Pallas kernels, call(): pl.pallas_call(kernel, grid_spec=pltpu.PrefetchScalarGridSpec(num_scalar_...  112 us
    ppermute x14, waiting for transfers between devices, far(): return lax.ppermute(value, 'tensor', [(i, i ^ 2) for i in range(count)])  70.7 us
    all_gather x1, waiting for transfers between devices, shards(): attn_w = lax.all_gather(attn_quarter, ('tensor', 'dp'), axis=0, tiled=True)  37.3 us
    unnamed x164, local copies, waits for them, and re-layouts  26.1 us
    dot_general x10, matrix products, contract_rows(): lax.dot_general(left_side, right_side, (((0,), (0,)), ((), ())), preferre...  24.1 us
    ppermute x6, waiting for transfers between devices, along(): total = total + lax.ppermute(sent, 'dp', moves).astype(F32)  23.5 us
    all_gather x1, blocking collectives, shards(): lax.all_gather(jnp.stack([gain_attn, gain_mlp]), 'dp', axis=1, tiled=True)  20.8 us
    ppermute x14, starting transfers between devices, far(): return lax.ppermute(value, 'tensor', [(i, i ^ 2) for i in range(count)])  19.6 us
  transfers between devices with their start and end apart: 43, of which 19 were waited for; matrix products, arithmetic and copies ran while one was open for 12% of the time, Pallas kernels for 22%

profile of v4, /device:TPU:0, one launch (start us, length us, event | category | flops | bytes accessed | tf_op | source)
XLA Modules:
  0.0 426.0 jit_solution(11242579898569513288)
XLA Ops:
  14.1 3.0 collective-permute-start.8
  21.1 20.8 %all-gather = bf16[8,144,2]{1,2,0:T(2,128)(2,1)S(1)} all-gather(bf16[1,144,2]{1,2,0:T(2,128)(2,1)S(1)} %maximum_bitcast_fusion.3), channel_id=1, replica_groups=mesh['dp'=8,'tensor'=4] {'dp'}, dimensions={0}, use_global_device_ids=true | all-gather | bytes 5184 | tf_op jit(solution)/shard_map/all_gather | solution.py:605
  42.6 4.8 %collective-permute-done.8 = bf16[2,256,1152]{2,1,0:T(8,128)(2,1)S(1)} collective-permute-done((bf16[2,256,1152]{2,1,0:T(8,128)(2,1)}, bf16[2,256,1152]{2,1,0:T(8,128)(2,1)S(1)}, u32[]{:S(2)}, u32[]{:S(2)}) %collective-permute-start.8) | collective-permute-done | bytes 1179680 | tf_op jit(solution)/shard_map/ppermute | solution.py:28
  51.5 37.3 %all-gather.4.cloned.1.call-done.wk.wv.w0.w1.w2 = bf16[4608,768]{1,0:T(8,128)(2,1)} async-done(((bf16[144,768]{1,0:T(8,128)(2,1)}), bf16[4608,768]{1,0:T(8,128)(2,1)}) %all-gather.4.cloned.1.call-update) | async-done | bytes 7077904 | tf_op jit(solution)/shard_map/all_gather | solution.py:602
  88.8 3.0 copy-done
  99.3 5.8 %collective-permute-done.p1 = bf16[256,768]{1,0:T(8,128)(2,1)S(1)} collective-permute-done((bf16[256,768]{1,0:T(8,128)(2,1)S(1)}, bf16[256,768]{1,0:T(8,128)(2,1)S(1)}, u32[]{:S(2)}, u32[]{:S(2)}) %collective-permute-start) | collective-permute-done | bytes 393248 | tf_op jit(solution)/shard_map/ppermute | solution.py:28
  109.0 6.6 %collective-permute-done.1.p1 = bf16[256,768]{1,0:T(8,128)(2,1)S(1)} collective-permute-done((bf16[256,768]{1,0:T(8,128)(2,1)S(1)}, bf16[256,768]{1,0:T(8,128)(2,1)S(1)}, u32[]{:S(2)}, u32[]{:S(2)}) %collective-permute-start.1) | collective-permute-done | bytes 393248 | tf_op jit(solution)/shard_map/ppermute | solution.py:28
  117.6 11.4 %attend.2.rest_0_.o_ref = bf16[512,1152]{1,0:T(8,128)(2,1)S(1)} custom-call(s32[4]{0:T(128)S(1)} %get-tuple-element.210.counts, bf16[512,1152]{1,0:T(8,128)(2,1)S(1)} %project_queries.1.q_ref, bf16[512,768]{1,0:T(8,128)(2,1)S(1)} %get-tuple-element.60.p0, bf16[256,768]{1,0:T(8,128)(2,1)S(1)} %collective-permute-done.p1, ...), custom_call_target="tpu_custom_call" | custom-call | flops 1 | bytes 1 | tf_op jit(solution)/shard_map/attend/pallas_call | solution.py:86
  131.9 11.2 %attend.3.o_ref = bf16[512,1152]{1,0:T(8,128)(2,1)S(1)} custom-call(s32[4]{0:T(128)S(1)} %get-tuple-element.209.counts, bf16[512,1152]{1,0:T(8,128)(2,1)S(1)} %project_queries.1.q_ref, bf16[512,768]{1,0:T(8,128)(2,1)S(1)} %get-tuple-element.60.p0, bf16[256,768]{1,0:T(8,128)(2,1)S(1)} %collective-permute-done.1.p1, ...), custom_call_target="tpu_custom_call", output_to_operand_aliasing={{}: (6, {})} | custom-call | flops 1 | bytes 1 | tf_op jit(solution)/shard_map/attend/pallas_call | solution.py:86
  147.1 14.2 %collective-permute-done.6 = bf16[256,1152]{1,0:T(8,128)(2,1)S(1)} collective-permute-done((bf16[256,1152]{1,0:T(8,128)(2,1)S(1)}, bf16[256,1152]{1,0:T(8,128)(2,1)S(1)}, u32[]{:S(2)}, u32[]{:S(2)}) %collective-permute-start.6) | collective-permute-done | bytes 589856 | tf_op jit(solution)/shard_map/ppermute | solution.py:28
  166.2 11.0 %all-gather.6.cloned.1.call-done.weight_ref = bf16[1152,2304]{1,0:T(8,128)(2,1)} async-done(((bf16[144,2304]{1,0:T(8,128)(2,1)}), bf16[1152,2304]{1,0:T(8,128)(2,1)}) %all-gather.6.cloned.1.call-update) | async-done | bytes 5308432 | tf_op jit(solution)/shard_map/all_gather | solution.py:604
  177.2 18.9 %feed.2 = (bf16[2048,1152]{1,0:T(8,128)(2,1)}, bf16[2048,768]{1,0:T(8,128)(2,1)S(1)}, bf16[2048,1536]{1,0:T(8,128)(2,1)}, bf16[512,1152]{1,0:T(8,128)(2,1)S(1)},...) custom-call(bf16[512,1152]{1,0:T(8,128)(2,1)S(1)} %constant_dynamic-update-slice_fusion.2.low_re, ...), custom_call_target="tpu_custom_call" | custom-call | flops 1 | bytes 1 | tf_op jit(solution)/shard_map/feed/pallas_call | solution.py:86
  198.2 18.6 %feed.3 = (bf16[2048,1152]{1,0:T(8,128)(2,1)}, bf16[2048,768]{1,0:T(8,128)(2,1)S(1)}, bf16[2048,1536]{1,0:T(8,128)(2,1)}, bf16[512,1152]{1,0:T(8,128)(2,1)S(1)},...) custom-call(bf16[512,1152]{1,0:T(8,128)(2,1)S(1)} %constant_dynamic-, ...), custom_call_target="tpu_custom_call", output_to_operand_aliasing={{0}: (4, {}), {1}: (5, {}), {2}: (6, {})} | custom-call | flops 1 | bytes 1 | tf_op jit(solution)/shard_map/feed/pallas_call | solution.py:86
  216.8 7.5 %convolution_convert_fusion.1 = bf16[1152,768]{1,0:T(8,128)(2,1)S(1)} fusion(bf16[2048,1152]{1,0:T(8,128)(2,1)} %fusion.13.grad_ref, bf16[2048,768]{1,0:T(8,128)(2,1)S(1)} %get-tuple-element.74), kind=kOutput, calls=%fused_computation.4 | convolution fusion | flops 3624763392 | bytes 9633792 | tf_op jit(solution)/shard_map/dot_general | solution.py:36
  224.4 8.5 %convolution_convert_fusion = bf16[1152,1536]{1,0:T(8,128)(2,1)S(1)} fusion(bf16[2048,1152]{1,0:T(8,128)(2,1)S(1)} %copy-done.55, bf16[2048,1536]{1,0:T(8,128)(2,1)S(1)} %copy-done.54), kind=kOutput, calls=%fused_computation | convolution fusion | flops 7249526784 | bytes 14548992 | tf_op jit(solution)/shard_map/dot_general | solution.py:36
  232.9 2.7 pad_maximum_fusion
  248.4 8.2 %collective-permute-done.17.far_ref = bf16[256,1152]{1,0:T(8,128)(2,1)S(1)} collective-permute-done((bf16[256,1152]{1,0:T(8,128)(2,1)S(1)}, bf16[256,1152]{1,0:T(8,128)(2,1)S(1)}, u32[]{:S(2)}, u32[]{:S(2)}) %collective-permute-start.17) | collective-permute-done | bytes 589856 | tf_op jit(solution)/shard_map/ppermute | solution.py:28
  256.5 3.1 copy-done.2
  260.9 3.1 enter.2
  264.1 17.2 %attend_back.2 = (bf16[512,1152]{1,0:T(8,128)(2,1)S(1)}, bf16[512,768]{1,0:T(8,128)(2,1)S(1)}, bf16[512,768]{1,0:T(8,128)(2,1)S(1)}) custom-call(s32[4]{0:T(128)S(1)} %get-tuple-element.210.counts, bf16[512,1152]{1,0:T(8,128)(2,1)S(1)} %copy-done.9, bf16[256,1152]{1,0:T(8,128)(2,1)S(1)} %get-tuple-element.84.g_ref, ...), custom_call_target="tpu_custom_call" | custom-call | flops 1 | bytes 1 | tf_op jit(solution)/shard_map/attend_back/pallas_call | solution.py:86
  285.5 11.9 %collective-permute-done.20.far_ref = bf16[256,1152]{1,0:T(8,128)(2,1)S(1)} collective-permute-done((bf16[256,1152]{1,0:T(8,128)(2,1)S(1)}, bf16[256,1152]{1,0:T(8,128)(2,1)S(1)}, u32[]{:S(2)}, u32[]{:S(2)}) %collective-permute-start.20) | collective-permute-done | bytes 589856 | tf_op jit(solution)/shard_map/ppermute | solution.py:28
  300.4 17.3 %attend_back.3 = (bf16[512,1152]{1,0:T(8,128)(2,1)S(1)}, bf16[512,768]{1,0:T(8,128)(2,1)S(1)}, bf16[512,768]{1,0:T(8,128)(2,1)S(1)}) custom-call(s32[4]{0:T(128)S(1)} %get-tuple-element.209.counts, bf16[512,1152]{1,0:T(8,128)(2,1)S(1)} %copy-done.9, bf16[256,1152]{1,0:T(8,128)(2,1)S(1)} %get-tuple-element.90.g_ref, ...), custom_call_target="tpu_custom_call", output_to_operand_aliasing={{0}: (9, {})} | custom-call | flops 1 | bytes 1 | tf_op jit(solution)/shard_map/attend_back/pallas_call | solution.py:86
  323.7 7.6 %collective-permute-done.23.far_ref = bf16[256,768]{1,0:T(8,128)(2,1)S(1)} collective-permute-done((bf16[256,768]{1,0:T(8,128)(2,1)S(1)}, bf16[256,768]{1,0:T(8,128)(2,1)S(1)}, u32[]{:S(2)}, u32[]{:S(2)}) %collective-permute-start.23) | collective-permute-done | bytes 393248 | tf_op jit(solution)/shard_map/ppermute | solution.py:28
  332.5 6.4 %collective-permute-done.22.far_ref = bf16[256,768]{1,0:T(8,128)(2,1)S(1)} collective-permute-done((bf16[256,768]{1,0:T(8,128)(2,1)S(1)}, bf16[256,768]{1,0:T(8,128)(2,1)S(1)}, u32[]{:S(2)}, u32[]{:S(2)}) %collective-permute-start.22) | collective-permute-done | bytes 393248 | tf_op jit(solution)/shard_map/ppermute | solution.py:28
  350.2 3.0 copy-done.3
  360.7 4.9 %collective-permute-done.33 = bf16[2,4,144,384]{3,2,1,0:T(8,128)(2,1)} collective-permute-done((bf16[2,4,144,384]{3,2,1,0:T(8,128)(2,1)}, bf16[2,4,144,384]{3,2,1,0:T(8,128)(2,1)}, u32[]{:S(2)}, u32[]{:S(2)}) %collective-permute-start.33) | collective-permute-done | bytes 884768 | tf_op jit(solution)/shard_map/ppermute | solution.py:546
  369.1 3.5 collective-permute-start.36
  380.6 10.6 %collective-permute-done.35 = bf16[2,144,384]{2,1,0:T(8,128)(2,1)S(1)} collective-permute-done((bf16[2,144,384]{2,1,0:T(8,128)(2,1)S(1)}, bf16[2,144,384]{2,1,0:T(8,128)(2,1)S(1)}, u32[]{:S(2)}, u32[]{:S(2)}) %collective-permute-start.35) | collective-permute-done | bytes 221216 | tf_op jit(solution)/shard_map/ppermute | solution.py:555
  393.2 3.8 collective-permute-start.30
  397.1 4.3 %collective-permute-done.28 = bf16[160,384]{1,0:T(8,128)(2,1)S(1)} collective-permute-done((bf16[160,384]{1,0:T(8,128)(2,1)S(1)}, bf16[160,384]{1,0:T(8,128)(2,1)S(1)}, u32[]{:S(2)}, u32[]{:S(2)}) %collective-permute-start.28) | collective-permute-done | bytes 122912 | tf_op jit(solution)/shard_map/ppermute | solution.py:555
  401.4 4.3 %collective-permute-done.29 = bf16[160,384]{1,0:T(8,128)(2,1)S(1)} collective-permute-done((bf16[160,384]{1,0:T(8,128)(2,1)S(1)}, bf16[160,384]{1,0:T(8,128)(2,1)S(1)}, u32[]{:S(2)}, u32[]{:S(2)}) %collective-permute-start.29) | collective-permute-done | bytes 122912 | tf_op jit(solution)/shard_map/ppermute | solution.py:555
  407.8 5.4 %collective-permute-done.38 = bf16[304,384]{1,0:T(8,128)(2,1)S(1)} collective-permute-done((bf16[304,384]{1,0:T(8,128)(2,1)S(1)}, bf16[304,384]{1,0:T(8,128)(2,1)S(1)}, u32[]{:S(2)}, u32[]{:S(2)}) %collective-permute-start.38) | collective-permute-done | bytes 233504 | tf_op jit(solution)/shard_map/ppermute | solution.py:28
  (320 shorter events, 105.5 us)
Async XLA Ops:
  7.2 81.6 %all-gather.4.cloned.1.call-start = ((), (), s32[]{:S(2)}) async-start(), calls=%async_computation.1 | async-start | bytes 7299072 | tf_op jit(solution)/shard_map/all_gather | solution.py:602
  9.5 167.7 %all-gather.6.cloned.1.call-start = ((), (), s32[]{:S(2)}) async-start(), calls=%async_computation.2 | async-start | bytes 5971968 | tf_op jit(solution)/shard_map/all_gather | solution.py:604
  10.5 382.6 %reduce-scatter.2.cloned.1.call-start = ((), (), s32[]{:S(2)}) async-start(), calls=%async_computation.3 | async-start | bytes 5971968 | tf_op jit(solution)/shard_map/reduce_scatter | solution.py:690
  14.1 33.2 %collective-permute-start.8 = (bf16[2,256,1152]{2,1,0:T(8,128)(2,1)}, bf16[2,256,1152]{2,1,0:T(8,128)(2,1)S(1)}, u32[]{:S(2)}, u32[]{:S(2)}) collective-permute-start(bf16[2,256,1152]{2,1,0:T(8,128)(2,1)} %get-tuple-element.158), channel_id=1, source_target_pairs={{0,2},{1,3},{2,0},{3,1},{4,6},{5,7},{6,4},{7,5},{8,10},{9,11},{10,... | collective-permute-start | bytes 3538952 | tf_op jit(solution)/shard_map/ppermute | solution.py:28
  49.3 57.3 %collective-permute-start.9 = (bf16[2,2,256,1152]{3,2,1,0:T(8,128)(2,1)}, bf16[2,2,256,1152]{3,2,1,0:T(8,128)(2,1)}, u32[]{:S(2)}, u32[]{:S(2)}) collective-permute-start(bf16[2,2,256,1152]{3,2,1,0:T(8,128)(2,1)} %pad_maximum_fusion.1), channel_id=1, source_target_pairs={{0,1},{1,0},{2,3},{3,2},{4,5},{5,4},{6,7},{7,6},{8,9},{9,8},{10,11... | collective-permute-start | bytes 7077896 | tf_op jit(solution)/shard_map/ppermute | solution.py:23
  93.7 11.3 %collective-permute-start = (bf16[256,768]{1,0:T(8,128)(2,1)S(1)}, bf16[256,768]{1,0:T(8,128)(2,1)S(1)}, u32[]{:S(2)}, u32[]{:S(2)}) collective-permute-start(bf16[256,768]{1,0:T(8,128)(2,1)S(1)} %get-tuple-element.174), channel_id=1, source_target_pairs={{0,2},{1,3},{2,0},{3,1},{4,6},{5,7},{6,4},{7,5},{8,10},{9,11},{10,... | collective-permute-start | bytes 1179656 | tf_op jit(solution)/shard_map/ppermute | solution.py:28
  105.1 10.6 %collective-permute-start.1 = (bf16[256,768]{1,0:T(8,128)(2,1)S(1)}, bf16[256,768]{1,0:T(8,128)(2,1)S(1)}, u32[]{:S(2)}, u32[]{:S(2)}) collective-permute-start(bf16[256,768]{1,0:T(8,128)(2,1)S(1)} %get-tuple-element.64), channel_id=1, source_target_pairs={{0,2},{1,3},{2,0},{3,1},{4,6},{5,7},{6,4},{7,5},{8,10},{9,11},{10,... | collective-permute-start | bytes 1179656 | tf_op jit(solution)/shard_map/ppermute | solution.py:28
  108.5 9.1 %collective-permute-start.4 = (bf16[256,768]{1,0:T(8,128)(2,1)S(1)}, bf16[256,768]{1,0:T(8,128)(2,1)S(1)}, u32[]{:S(2)}, u32[]{:S(2)}) collective-permute-start(bf16[256,768]{1,0:T(8,128)(2,1)S(1)} %get-tuple-element.174), channel_id=1, source_target_pairs={{0,1},{1,0},{2,3},{3,2},{4,5},{5,4},{6,7},{7,6},{8,9},{9,8},{10,11... | collective-permute-start | bytes 1179656 | tf_op jit(solution)/shard_map/ppermute | solution.py:23
  108.5 23.4 %collective-permute-start.2 = (bf16[256,768]{1,0:T(8,128)(2,1)S(1)}, bf16[256,768]{1,0:T(8,128)(2,1)S(1)}, u32[]{:S(2)}, u32[]{:S(2)}) collective-permute-start(bf16[256,768]{1,0:T(8,128)(2,1)S(1)} %get-tuple-element.64), channel_id=1, source_target_pairs={{0,1},{1,0},{2,3},{3,2},{4,5},{5,4},{6,7},{7,6},{8,9},{9,8},{10,11... | collective-permute-start | bytes 1179656 | tf_op jit(solution)/shard_map/ppermute | solution.py:23
  115.6 16.3 %collective-permute-start.3 = (bf16[256,768]{1,0:T(8,128)(2,1)S(1)}, bf16[256,768]{1,0:T(8,128)(2,1)S(1)}, u32[]{:S(2)}, u32[]{:S(2)}) collective-permute-start(bf16[256,768]{1,0:T(8,128)(2,1)S(1)} %collective-permute-done.1.p1), channel_id=1, source_target_pairs={{0,1},{1,0},{2,3},{3,2},{4,5},{5,4},{6,7},{7,6},{8,9},{9,8},{10,11... | collective-permute-start | bytes 1179656 | tf_op jit(solution)/shard_map/ppermute | solution.py:23
  130.3 16.4 %collective-permute-start.10 = (bf16[256,1152]{1,0:T(8,128)(2,1)S(1)}, bf16[256,1152]{1,0:T(8,128)(2,1)S(1)}, u32[]{:S(2)}, u32[]{:S(2)}) collective-permute-start(bf16[256,1152]{1,0:T(8,128)(2,1)S(1)} %get-tuple-element.68), channel_id=1, source_target_pairs={{0,2},{1,3},{2,0},{3,1},{4,6},{5,7},{6,4},{7,5},{8,10},{9,11},{10,... | collective-permute-start | bytes 1769480 | tf_op jit(solution)/shard_map/ppermute | solution.py:28
  145.7 15.5 %collective-permute-start.6 = (bf16[256,1152]{1,0:T(8,128)(2,1)S(1)}, bf16[256,1152]{1,0:T(8,128)(2,1)S(1)}, u32[]{:S(2)}, u32[]{:S(2)}) collective-permute-start(bf16[256,1152]{1,0:T(8,128)(2,1)S(1)} %get-tuple-element.66), channel_id=1, source_target_pairs={{0,2},{1,3},{2,0},{3,1},{4,6},{5,7},{6,4},{7,5},{8,10},{9,11},{10,... | collective-permute-start | bytes 1769480 | tf_op jit(solution)/shard_map/ppermute | solution.py:28
  146.8 30.4 %collective-permute-start.11 = (bf16[512,1152]{1,0:T(8,128)(2,1)S(1)}, bf16[512,1152]{1,0:T(8,128)(2,1)}, u32[]{:S(2)}, u32[]{:S(2)}) collective-permute-start(bf16[512,1152]{1,0:T(8,128)(2,1)S(1)} %constant_dynamic-update-slice_fusion.2.low_ref), channel_id=1, source_target_pairs={{0,1},{1,0},{2,3},{3,2},{4,5},{5,4},{6,7},{7,6},{8,9},{9,8},{10,11... | collective-permute-start | bytes 3538952 | tf_op jit(solution)/shard_map/ppermute | solution.py:23
  161.3 36.9 %collective-permute-start.7 = (bf16[512,1152]{1,0:T(8,128)(2,1)S(1)}, bf16[512,1152]{1,0:T(8,128)(2,1)}, u32[]{:S(2)}, u32[]{:S(2)}) collective-permute-start(bf16[512,1152]{1,0:T(8,128)(2,1)S(1)} %constant_dynamic-update-slice_fusion.low_ref), channel_id=1, source_target_pairs={{0,1},{1,0},{2,3},{3,2},{4,5},{5,4},{6,7},{7,6},{8,9},{9,8},{10,11... | collective-permute-start | bytes 3538952 | tf_op jit(solution)/shard_map/ppermute | solution.py:23
  238.2 43.2 %collective-permute-start.19 = (bf16[512,1152]{1,0:T(8,128)(2,1)}, bf16[512,1152]{1,0:T(8,128)(2,1)S(1)}, u32[]{:S(2)}, u32[]{:S(2)}) collective-permute-start(bf16[512,1152]{1,0:T(8,128)(2,1)} %copy-done.48), channel_id=1, source_target_pairs={{0,1},{1,0},{2,3},{3,2},{4,5},{5,4},{6,7},{7,6},{8,9},{9,8},{10,11... | collective-permute-start | bytes 3538952 | tf_op jit(solution)/shard_map/ppermute | solution.py:23
  240.3 16.2 %collective-permute-start.17 = (bf16[256,1152]{1,0:T(8,128)(2,1)S(1)}, bf16[256,1152]{1,0:T(8,128)(2,1)S(1)}, u32[]{:S(2)}, u32[]{:S(2)}) collective-permute-start(bf16[256,1152]{1,0:T(8,128)(2,1)S(1)} %add_convert_fusion.1), channel_id=1, source_target_pairs={{0,2},{1,3},{2,0},{3,1},{4,6},{5,7},{6,4},{7,5},{8,10},{9,11},{10,... | collective-permute-start | bytes 1769480 | tf_op jit(solution)/shard_map/ppermute | solution.py:28
  244.1 39.0 %collective-permute-start.13 = (bf16[256,1152]{1,0:T(8,128)(2,1)}, bf16[256,1152]{1,0:T(8,128)(2,1)}, u32[]{:S(2)}, u32[]{:S(2)}) collective-permute-start(bf16[256,1152]{1,0:T(8,128)(2,1)} %add_convert_fusion.3), channel_id=1, source_target_pairs={{0,2},{1,3},{2,0},{3,1},{4,6},{5,7},{6,4},{7,5},{8,10},{9,11},{10,... | collective-permute-start | bytes 1769480 | tf_op jit(solution)/shard_map/ppermute | solution.py:28
  247.1 100.6 %collective-permute-start.15 = (bf16[256,1152]{1,0:T(8,128)(2,1)}, bf16[256,1152]{1,0:T(8,128)(2,1)}, u32[]{:S(2)}, u32[]{:S(2)}) collective-permute-start(bf16[256,1152]{1,0:T(8,128)(2,1)} %add_convert_fusion.2), channel_id=1, source_target_pairs={{0,2},{1,3},{2,0},{3,1},{4,6},{5,7},{6,4},{7,5},{8,10},{9,11},{10,... | collective-permute-start | bytes 1769480 | tf_op jit(solution)/shard_map/ppermute | solution.py:28
  281.4 19.0 %collective-permute-start.18 = (bf16[512,768]{1,0:T(8,128)(2,1)S(1)}, bf16[512,768]{1,0:T(8,128)(2,1)S(1)}, u32[]{:S(2)}, u32[]{:S(2)}) collective-permute-start(bf16[512,768]{1,0:T(8,128)(2,1)S(1)} %get-tuple-element.85), channel_id=1, source_target_pairs={{0,1},{1,0},{2,3},{3,2},{4,5},{5,4},{6,7},{7,6},{8,9},{9,8},{10,11... | collective-permute-start | bytes 2359304 | tf_op jit(solution)/shard_map/ppermute | solution.py:23
  281.6 15.8 %collective-permute-start.20 = (bf16[256,1152]{1,0:T(8,128)(2,1)S(1)}, bf16[256,1152]{1,0:T(8,128)(2,1)S(1)}, u32[]{:S(2)}, u32[]{:S(2)}) collective-permute-start(bf16[256,1152]{1,0:T(8,128)(2,1)S(1)} %add_convert_fusion), channel_id=1, source_target_pairs={{0,2},{1,3},{2,0},{3,1},{4,6},{5,7},{6,4},{7,5},{8,10},{9,11},{10,... | collective-permute-start | bytes 1769480 | tf_op jit(solution)/shard_map/ppermute | solution.py:28
  318.6 13.0 %collective-permute-start.24 = (bf16[1152,384]{1,0:T(8,128)(2,1)S(1)}, bf16[1152,384]{1,0:T(8,128)(2,1)S(1)}, u32[]{:S(2)}, u32[]{:S(2)}) collective-permute-start(bf16[1152,384]{1,0:T(8,128)(2,1)S(1)} %convolution_convert_fusion.5), channel_id=1, source_target_pairs={{0,1},{1,0},{2,3},{3,2},{4,5},{5,4},{6,7},{7,6},{8,9},{9,8},{10,11... | collective-permute-start | bytes 2654216 | tf_op jit(solution)/shard_map/ppermute | solution.py:23
  319.3 12.0 %collective-permute-start.23 = (bf16[256,768]{1,0:T(8,128)(2,1)S(1)}, bf16[256,768]{1,0:T(8,128)(2,1)S(1)}, u32[]{:S(2)}, u32[]{:S(2)}) collective-permute-start(bf16[256,768]{1,0:T(8,128)(2,1)S(1)} %add_convert_fusion.4), channel_id=1, source_target_pairs={{0,2},{1,3},{2,0},{3,1},{4,6},{5,7},{6,4},{7,5},{8,10},{9,11},{10,... | collective-permute-start | bytes 1179656 | tf_op jit(solution)/shard_map/ppermute | solution.py:28
  321.6 18.4 %collective-permute-start.32 = (bf16[1152,384]{1,0:T(8,128)(2,1)S(1)}, bf16[1152,384]{1,0:T(8,128)(2,1)S(1)}, u32[]{:S(2)}, u32[]{:S(2)}) collective-permute-start(bf16[1152,384]{1,0:T(8,128)(2,1)S(1)} %convolution_convert_fusion.2), channel_id=1, source_target_pairs={{0,1},{1,0},{2,3},{3,2},{4,5},{5,4},{6,7},{7,6},{8,9},{9,8},{10,11... | collective-permute-start | bytes 2654216 | tf_op jit(solution)/shard_map/ppermute | solution.py:23
  321.8 17.0 %collective-permute-start.22 = (bf16[256,768]{1,0:T(8,128)(2,1)S(1)}, bf16[256,768]{1,0:T(8,128)(2,1)S(1)}, u32[]{:S(2)}, u32[]{:S(2)}) collective-permute-start(bf16[256,768]{1,0:T(8,128)(2,1)S(1)} %add_convert_fusion.5), channel_id=1, source_target_pairs={{0,2},{1,3},{2,0},{3,1},{4,6},{5,7},{6,4},{7,5},{8,10},{9,11},{10,... | collective-permute-start | bytes 1179656 | tf_op jit(solution)/shard_map/ppermute | solution.py:28
  331.3 9.5 %collective-permute-start.31 = (bf16[1152,384]{1,0:T(8,128)(2,1)S(1)}, bf16[1152,384]{1,0:T(8,128)(2,1)S(1)}, u32[]{:S(2)}, u32[]{:S(2)}) collective-permute-start(bf16[1152,384]{1,0:T(8,128)(2,1)S(1)} %convolution_convert_fusion.3), channel_id=1, source_target_pairs={{0,1},{1,0},{2,3},{3,2},{4,5},{5,4},{6,7},{7,6},{8,9},{9,8},{10,11... | collective-permute-start | bytes 2654216 | tf_op jit(solution)/shard_map/ppermute | solution.py:23
  343.2 22.4 %collective-permute-start.33 = (bf16[2,4,144,384]{3,2,1,0:T(8,128)(2,1)}, bf16[2,4,144,384]{3,2,1,0:T(8,128)(2,1)}, u32[]{:S(2)}, u32[]{:S(2)}) collective-permute-start(bf16[2,4,144,384]{3,2,1,0:T(8,128)(2,1)} %fusion.10), channel_id=1, source_target_pairs={{0,4},{4,0},{8,12},{12,8},{16,20},{20,16},{24,28},{28,24},{1,5},{5... | collective-permute-start | bytes 2654216 | tf_op jit(solution)/shard_map/ppermute | solution.py:546
  346.2 26.4 %collective-permute-start.26 = (bf16[1152,384]{1,0:T(8,128)(2,1)}, bf16[1152,384]{1,0:T(8,128)(2,1)}, u32[]{:S(2)}, u32[]{:S(2)}) collective-permute-start(bf16[1152,384]{1,0:T(8,128)(2,1)} %get-tuple-element.200), channel_id=1, source_target_pairs={{0,2},{1,3},{2,0},{3,1},{4,6},{5,7},{6,4},{7,5},{8,10},{9,11},{10,... | collective-permute-start | bytes 2654216 | tf_op jit(solution)/shard_map/ppermute | solution.py:28
  368.7 10.2 %collective-permute-start.34 = (bf16[2,144,384]{2,1,0:T(8,128)(2,1)S(1)}, bf16[2,144,384]{2,1,0:T(8,128)(2,1)S(1)}, u32[]{:S(2)}, u32[]{:S(2)}) collective-permute-start(bf16[2,144,384]{2,1,0:T(8,128)(2,1)S(1)} %get-tuple-element.171), channel_id=1, source_target_pairs={{0,8},{4,12},{8,16},{12,20},{16,24},{20,28},{24,0},{28,4},{1,9},{5... | collective-permute-start | bytes 663560 | tf_op jit(solution)/shard_map/ppermute | solution.py:555
  369.1 11.5 %collective-permute-start.36 = (bf16[2,144,384]{2,1,0:T(8,128)(2,1)S(1)}, bf16[2,144,384]{2,1,0:T(8,128)(2,1)S(1)}, u32[]{:S(2)}, u32[]{:S(2)}) collective-permute-start(bf16[2,144,384]{2,1,0:T(8,128)(2,1)S(1)} %get-tuple-element.172), channel_id=1, source_target_pairs={{0,24},{4,28},{8,0},{12,4},{16,8},{20,12},{24,16},{28,20},{1,25},{... | collective-permute-start | bytes 663560 | tf_op jit(solution)/shard_map/ppermute | solution.py:555
  372.5 18.7 %collective-permute-start.35 = (bf16[2,144,384]{2,1,0:T(8,128)(2,1)S(1)}, bf16[2,144,384]{2,1,0:T(8,128)(2,1)S(1)}, u32[]{:S(2)}, u32[]{:S(2)}) collective-permute-start(bf16[2,144,384]{2,1,0:T(8,128)(2,1)S(1)} %get-tuple-element.173), channel_id=1, source_target_pairs={{0,16},{4,20},{8,24},{12,28},{16,0},{20,4},{24,8},{28,12},{1,17},{... | collective-permute-start | bytes 663560 | tf_op jit(solution)/shard_map/ppermute | solution.py:555
  374.1 18.7 %collective-permute-start.27 = (bf16[4,160,384]{2,1,0:T(8,128)(2,1)S(1)}, bf16[4,160,384]{2,1,0:T(8,128)(2,1)S(1)}, u32[]{:S(2)}, u32[]{:S(2)}) collective-permute-start(bf16[4,160,384]{2,1,0:T(8,128)(2,1)S(1)} %fusion.21), channel_id=1, source_target_pairs={{0,4},{4,0},{8,12},{12,8},{16,20},{20,16},{24,28},{28,24},{1,5},{5... | collective-permute-start | bytes 1474568 | tf_op jit(solution)/shard_map/ppermute | solution.py:546
  397.1 8.7 %collective-permute-start.29 = (bf16[160,384]{1,0:T(8,128)(2,1)S(1)}, bf16[160,384]{1,0:T(8,128)(2,1)S(1)}, u32[]{:S(2)}, u32[]{:S(2)}) collective-permute-start(bf16[160,384]{1,0:T(8,128)(2,1)S(1)} %get-tuple-element.180), channel_id=1, source_target_pairs={{0,16},{4,20},{8,24},{12,28},{16,0},{20,4},{24,8},{28,12},{1,17},{... | collective-permute-start | bytes 368648 | tf_op jit(solution)/shard_map/ppermute | solution.py:555
  (89 other events, 769.9 us)
Sparse Core Ops, SparseCore 0:
  11.6 77.1 all-gather.3
  91.6 85.5 all-gather.5
  235.8 102.3 reduce-scatter.1

commit v5 on v4

--- a/solution.py
+++ b/solution.py
@@ -35,12 +35,6 @@
 def contract_rows(left_side, right_side):
     return lax.dot_general(
         left_side, right_side, (((0,), (0,)), ((), ())), preferred_element_type=F32
-    )
-
-
-def contract_last(left_side, right_side):
-    return lax.dot_general(
-        left_side, right_side, (((1,), (1,)), ((), ())), preferred_element_type=F32
     )
 
 
@@ -655,6 +649,8 @@
         across = far(own)
         if b == 0:
             across, queries = lax.optimization_barrier((across, queries))
+        else:
+            across, _ = lax.optimization_barrier((across, attended))
         others = [across, near(own), near(across)]
         attended = attend(b, counts[b], queries, pairs_own, others, attended)
         middle, hidden_own = leave(b, x_rows, attended, gain_two, attn_w)
@@ -667,11 +663,16 @@
     shared = None
     for b in range(micro):
         k = kept[b]
+        if b > 0:
+            k["low"], kept[b - 1]["far_sent"] = lax.optimization_barrier(
+                (k["low"], kept[b - 1]["far_sent"])
+            )
         *shared, k["out_low"], k["out_high"], k["part"], back_high = feed(
             b, k["low"], k["high"], grad_ffn, mlp_full, shared
         )
         k["near_part"] = near(back_high)
-        k["far_part"] = far(added(k["part"][row_share:], k["near_part"][row_share:]))
+        k["far_sent"] = added(k["part"][row_share:], k["near_part"][row_share:])
+    shared[0], kept[-1]["far_sent"] = lax.optimization_barrier((shared[0], kept[-1]["far_sent"]))
     hidden_rows, activated, inner_grads = shared
     grad_mlp_w = row_major(
         jnp.concatenate(
@@ -695,7 +696,7 @@
             valid_rows[b][None],
             k["part"],
             k["near_part"],
-            k["far_part"],
+            far(k["far_sent"]),
             k["middle"],
             cot_rows,
             gain_two,
@@ -703,18 +704,20 @@
             branch,
         )
         gain_two_grads.append(gain_two_grad[0:1])
+        k["out_high"], grad_att = lax.optimization_barrier((k["out_high"], grad_att))
         if b > 0:
-            near_pair, grad_att = lax.optimization_barrier((kept[b - 1]["near_pair"], grad_att))
-            kept[b - 1]["near_pair"] = near_pair
+            kept[b - 1]["pair_far"], grad_att = lax.optimization_barrier(
+                (kept[b - 1]["pair_far"], grad_att)
+            )
         query_grads, k["pair_kept"], pair_sent = attend_back(
             b, counts[b], queries, grad_att, cosine_t, sine_t, pairs_own, k["others"], query_grads
         )
         k["near_pair"] = near(pair_sent)
+        k["pair_far"] = added(k["pair_kept"][row_share:], k["near_pair"][row_share:])
     for b in range(micro):
         k = kept[b]
-        far_pair = far(added(k["pair_kept"][row_share:], k["near_pair"][row_share:]))
         pair_grads = pairs_back(
-            b, k["pair_kept"], k["near_pair"], far_pair, cosine, sine, pair_grads
+            b, k["pair_kept"], k["near_pair"], far(k["pair_far"]), cosine, sine, pair_grads
         )
 
     outputs, input_grads, gain_one_grads = [], [], []

time: 432 us -> 454 us (1.051)
  local copies, waits for them, and re-layouts: 35.3 us -> 57.8 us
    unnamed x164 -> x236, local copies, waits for them, and re-layouts: 26.1 us -> 45.7 us
    all_gather x1, waiting for transfers between devices: 11 us -> 30.1 us  [shards(): mlp_full = lax.all_gather(mlp_local, 'dp', axis=0, tiled=True)]
    ppermute x6, waiting for transfers between devices: 23.5 us -> 9.68 us  [along(): total = total + lax.ppermute(sent, 'dp', moves).astype(F32)]
    ppermute x14, waiting for transfers between devices: 70.7 us -> 60.8 us  [far(): return lax.ppermute(value, 'tensor', [(i, i ^ 2) for i in range(count)])]
  transfers between devices with their start and end apart: 43 -> 43, of which waited for: 19 -> 15; matrix products, arithmetic and copies ran while one was open for 12% -> 14% of each run, Pallas kernels for 22% -> 17%
where the time goes in v5:
time: 454 us; the launch traced here: 447 us
  waiting for transfers between devices  146 us (32%)
  Pallas kernels  114 us (25%)
  local copies, waits for them, and re-layouts  57.8 us (13%)
  other arithmetic  34.3 us (8%)
  starting transfers between devices  27.8 us (6%)
  matrix products  24.6 us (5%)
  between operations  21 us (5%)
  blocking collectives  20.8 us (5%)
    pallas_call x16, Pallas kernels, call(): pl.pallas_call(kernel, grid_spec=pltpu.PrefetchScalarGridSpec(num_scalar_...  114 us
    ppermute x14, waiting for transfers between devices, far(): return lax.ppermute(value, 'tensor', [(i, i ^ 2) for i in range(count)])  60.8 us
    unnamed x236, local copies, waits for them, and re-layouts  45.7 us
    all_gather x1, waiting for transfers between devices, shards(): attn_w = lax.all_gather(attn_quarter, ('tensor', 'dp'), axis=0, tiled=True)  35.3 us
    all_gather x1, waiting for transfers between devices, shards(): mlp_full = lax.all_gather(mlp_local, 'dp', axis=0, tiled=True)  30.1 us
    dot_general x10, matrix products, contract_rows(): lax.dot_general(left_side, right_side, (((0,), (0,)), ((), ())), preferre...  24.6 us
    all_gather x1, blocking collectives, shards(): lax.all_gather(jnp.stack([gain_attn, gain_mlp]), 'dp', axis=1, tiled=True)  20.8 us
    ppermute x14, starting transfers between devices, far(): return lax.ppermute(value, 'tensor', [(i, i ^ 2) for i in range(count)])  15.6 us
  transfers between devices with their start and end apart: 43, of which 15 were waited for; matrix products, arithmetic and copies ran while one was open for 14% of the time, Pallas kernels for 17%

profile of v5, /device:TPU:0, one launch (start us, length us, event | category | flops | bytes accessed | tf_op | source)
XLA Modules:
  0.0 446.8 jit_solution(8938421981641831317)
XLA Ops:
  14.1 3.0 collective-permute-start.9
  21.1 20.8 %all-gather = bf16[8,144,2]{1,2,0:T(2,128)(2,1)S(1)} all-gather(bf16[1,144,2]{1,2,0:T(2,128)(2,1)S(1)} %maximum_bitcast_fusion.3), channel_id=1, replica_groups=mesh['dp'=8,'tensor'=4] {'dp'}, dimensions={0}, use_global_device_ids=true | all-gather | bytes 5184 | tf_op jit(solution)/shard_map/all_gather | solution.py:599
  43.9 3.5 collective-permute-done.9
  53.5 35.3 %all-gather.4.cloned.1.call-done.wk.wv.w0.w1.w2 = bf16[4608,768]{1,0:T(8,128)(2,1)} async-done(((bf16[144,768]{1,0:T(8,128)(2,1)}), bf16[4608,768]{1,0:T(8,128)(2,1)}) %all-gather.4.cloned.1.call-update) | async-done | bytes 7077904 | tf_op jit(solution)/shard_map/all_gather | solution.py:596
  88.8 3.0 copy-done
  97.2 2.6 project_queries.1.q_ref
  99.9 5.2 %collective-permute-done.p1 = bf16[256,768]{1,0:T(8,128)(2,1)S(1)} collective-permute-done((bf16[256,768]{1,0:T(8,128)(2,1)S(1)}, bf16[256,768]{1,0:T(8,128)(2,1)S(1)}, u32[]{:S(2)}, u32[]{:S(2)}) %collective-permute-start) | collective-permute-done | bytes 393248 | tf_op jit(solution)/shard_map/ppermute | solution.py:28
  109.0 11.4 %attend.2.rest_0_.o_ref = bf16[512,1152]{1,0:T(8,128)(2,1)S(1)} custom-call(s32[4]{0:T(128)S(1)} %copy-done.70, bf16[512,1152]{1,0:T(8,128)(2,1)S(1)} %project_queries.1.q_ref, bf16[512,768]{1,0:T(8,128)(2,1)S(1)} %get-tuple-element.69.p0, bf16[256,768]{1,0:T(8,128)(2,1)S(1)} %collective-permute-done.p1, bf16[256,768]{1,0:T(8,128)(2,1)S(1)} %collective-permute-done.2.p2, ...), custom_call_target="tpu_custom_call" | custom-call | flops 1 | bytes 1 | tf_op jit(solution)/shard_map/attend/pallas_call | solution.py:80
  124.5 11.2 %attend.3.o_ref = bf16[512,1152]{1,0:T(8,128)(2,1)S(1)} custom-call(s32[4]{0:T(128)S(1)} %copy-done.68, bf16[512,1152]{1,0:T(8,128)(2,1)S(1)} %project_queries.1.q_ref, bf16[512,768]{1,0:T(8,128)(2,1)S(1)} %get-tuple-element.69.p0, bf16[256,768]{1,0:T(8,128)(2,1)S(1)} %collective-permute-done.1.p1, ...), custom_call_target="tpu_custom_call", output_to_operand_aliasing={{}: (6, {})} | custom-call | flops 1 | bytes 1 | tf_op jit(solution)/shard_map/attend/pallas_call | solution.py:80
  147.1 30.1 %all-gather.6.cloned.1.call-done.weight_ref = bf16[1152,2304]{1,0:T(8,128)(2,1)} async-done(((bf16[144,2304]{1,0:T(8,128)(2,1)}), bf16[1152,2304]{1,0:T(8,128)(2,1)}) %all-gather.6.cloned.1.call-update) | async-done | bytes 5308432 | tf_op jit(solution)/shard_map/all_gather | solution.py:598
  177.2 19.0 %feed.2 = (bf16[2048,1152]{1,0:T(8,128)(2,1)}, bf16[2048,768]{1,0:T(8,128)(2,1)S(1)}, bf16[2048,1536]{1,0:T(8,128)(2,1)}, bf16[512,1152]{1,0:T(8,128)(2,1)S(1)},...) custom-call(bf16[512,1152]{1,0:T(8,128)(2,1)} %constant_dynamic-update-slice_fusion.2.lo, ...), custom_call_target="tpu_custom_call" | custom-call | flops 1 | bytes 1 | tf_op jit(solution)/shard_map/feed/pallas_call | solution.py:80
  202.9 18.1 %feed.3 = (bf16[2048,1152]{1,0:T(8,128)(2,1)}, bf16[2048,768]{1,0:T(8,128)(2,1)S(1)}, bf16[2048,1536]{1,0:T(8,128)(2,1)}, bf16[512,1152]{1,0:T(8,128)(2,1)S(1)},...) custom-call(bf16[512,1152]{1,0:T(8,128)(2,1)S(1)} %constant_dynamic-, ...), custom_call_target="tpu_custom_call", output_to_operand_aliasing={{0}: (4, {}), {1}: (5, {}), {2}: (6, {})} | custom-call | flops 1 | bytes 1 | tf_op jit(solution)/shard_map/feed/pallas_call | solution.py:80
  222.2 7.0 %convolution_convert_fusion.1 = bf16[1152,768]{1,0:T(8,128)(2,1)S(1)} fusion(bf16[2048,1152]{1,0:T(8,128)(2,1)} %fusion.13.grad_ref, bf16[2048,768]{1,0:T(8,128)(2,1)S(1)} %get-tuple-element.90), kind=kOutput, calls=%fused_computation.4 | convolution fusion | flops 3624763392 | bytes 9633792 | tf_op jit(solution)/shard_map/dot_general | solution.py:36
  230.4 8.2 %convolution_convert_fusion = bf16[1152,1536]{1,0:T(8,128)(2,1)S(1)} fusion(bf16[2048,1152]{1,0:T(8,128)(2,1)S(1)} %bitcast.212, bf16[2048,1536]{1,0:T(8,128)(2,1)S(1)} %bitcast.210), kind=kOutput, calls=%fused_computation | convolution fusion | flops 7249526784 | bytes 14548992 | tf_op jit(solution)/shard_map/dot_general | solution.py:36
  238.6 2.7 pad_maximum_fusion
  244.4 13.5 %collective-permute-done.14.far_ref = bf16[256,1152]{1,0:T(8,128)(2,1)S(1)} collective-permute-done((bf16[256,1152]{1,0:T(8,128)(2,1)}, bf16[256,1152]{1,0:T(8,128)(2,1)S(1)}, u32[]{:S(2)}, u32[]{:S(2)}) %collective-permute-start.14) | collective-permute-done | bytes 589856 | tf_op jit(solution)/shard_map/ppermute | solution.py:28
  257.8 3.1 copy-done.2
  270.7 18.0 %attend_back.2 = (bf16[512,1152]{1,0:T(8,128)(2,1)S(1)}, bf16[512,768]{1,0:T(8,128)(2,1)S(1)}, bf16[512,768]{1,0:T(8,128)(2,1)}) custom-call(s32[4]{0:T(128)S(1)} %copy-done.71, bf16[512,1152]{1,0:T(8,128)(2,1)S(1)} %project_queries.1.q_ref, bf16[256,1152]{1,0:T(8,128)(2,1)S(1)} %get-tuple-element.105.g_ref, f32[32,256]{1,0:T(8,128)S(1)} %get-tuple-element.212.cos_ref, ...), custom_call_target="tpu_custom_call" | custom-call | flops 1 | bytes 1 | tf_op jit(solution)/shard_map/attend_back/pallas_call | solution.py:80
  290.7 2.3 pad_maximum_fusion.10
  293.5 3.0 copy-done.3
  302.9 3.0 enter.3
  315.9 17.3 %attend_back.3 = (bf16[512,1152]{1,0:T(8,128)(2,1)S(1)}, bf16[512,768]{1,0:T(8,128)(2,1)S(1)}, bf16[512,768]{1,0:T(8,128)(2,1)S(1)}) custom-call(s32[4]{0:T(128)S(1)} %copy-done.69, bf16[512,1152]{1,0:T(8,128)(2,1)S(1)} %project_queries.1.q_ref, bf16[256,1152]{1,0:T(8,128)(2,1)S(1)} %copy-done.63, ...), custom_call_target="tpu_custom_call", output_to_operand_aliasing={{0}: (9, {})} | custom-call | flops 1 | bytes 1 | tf_op jit(solution)/shard_map/attend_back/pallas_call | solution.py:80
  346.2 16.7 %collective-permute-done.22.far_ref = bf16[256,768]{1,0:T(8,128)(2,1)S(1)} collective-permute-done((bf16[256,768]{1,0:T(8,128)(2,1)S(1)}, bf16[256,768]{1,0:T(8,128)(2,1)S(1)}, u32[]{:S(2)}, u32[]{:S(2)}) %collective-permute-start.22) | collective-permute-done | bytes 393248 | tf_op jit(solution)/shard_map/ppermute | solution.py:28
  373.2 2.4 select_convert_fusion.1
  378.4 2.2 fusion.66
  381.1 3.7 collective-permute-start.36
  384.8 15.2 %collective-permute-done.26 = bf16[1152,384]{1,0:T(8,128)(2,1)S(1)} collective-permute-done((bf16[1152,384]{1,0:T(8,128)(2,1)}, bf16[1152,384]{1,0:T(8,128)(2,1)S(1)}, u32[]{:S(2)}, u32[]{:S(2)}) %collective-permute-start.26) | collective-permute-done | bytes 884768 | tf_op jit(solution)/shard_map/ppermute | solution.py:28
  404.7 8.7 %collective-permute-done.27 = bf16[4,160,384]{2,1,0:T(8,128)(2,1)S(1)} collective-permute-done((bf16[4,160,384]{2,1,0:T(8,128)(2,1)S(1)}, bf16[4,160,384]{2,1,0:T(8,128)(2,1)S(1)}, u32[]{:S(2)}, u32[]{:S(2)}) %collective-permute-start.27) | collective-permute-done | bytes 491552 | tf_op jit(solution)/shard_map/ppermute | solution.py:540
  414.1 3.4 collective-permute-start.30
  417.6 4.3 collective-permute-done.28
  421.9 5.0 %collective-permute-done.29 = bf16[160,384]{1,0:T(8,128)(2,1)S(1)} collective-permute-done((bf16[160,384]{1,0:T(8,128)(2,1)S(1)}, bf16[160,384]{1,0:T(8,128)(2,1)S(1)}, u32[]{:S(2)}, u32[]{:S(2)}) %collective-permute-start.29) | collective-permute-done | bytes 122912 | tf_op jit(solution)/shard_map/ppermute | solution.py:549
  428.9 4.8 %collective-permute-done.38 = bf16[304,384]{1,0:T(8,128)(2,1)S(1)} collective-permute-done((bf16[304,384]{1,0:T(8,128)(2,1)S(1)}, bf16[304,384]{1,0:T(8,128)(2,1)S(1)}, u32[]{:S(2)}, u32[]{:S(2)}) %collective-permute-start.38) | collective-permute-done | bytes 233504 | tf_op jit(solution)/shard_map/ppermute | solution.py:28
  (395 shorter events, 118.0 us)
Async XLA Ops:
  7.2 81.6 %all-gather.4.cloned.1.call-start = ((), (), s32[]{:S(2)}) async-start(), calls=%async_computation.1 | async-start | bytes 7299072 | tf_op jit(solution)/shard_map/all_gather | solution.py:596
  9.5 167.7 %all-gather.6.cloned.1.call-start = ((), (), s32[]{:S(2)}) async-start(), calls=%async_computation.2 | async-start | bytes 5971968 | tf_op jit(solution)/shard_map/all_gather | solution.py:598
  10.5 403.0 %reduce-scatter.2.cloned.1.call-start = ((), (), s32[]{:S(2)}) async-start(), calls=%async_computation.3 | async-start | bytes 5971968 | tf_op jit(solution)/shard_map/reduce_scatter | solution.py:691
  14.1 33.2 %collective-permute-start.9 = (bf16[2,256,1152]{2,1,0:T(8,128)(2,1)}, bf16[2,256,1152]{2,1,0:T(8,128)(2,1)S(1)}, u32[]{:S(2)}, u32[]{:S(2)}) collective-permute-start(bf16[2,256,1152]{2,1,0:T(8,128)(2,1)} %get-tuple-element.176), channel_id=1, source_target_pairs={{0,2},{1,3},{2,0},{3,1},{4,6},{5,7},{6,4},{7,5},{8,10},{9,11},{10,... | collective-permute-start | bytes 3538952 | tf_op jit(solution)/shard_map/ppermute | solution.py:28
  49.3 46.0 %collective-permute-start.10 = (bf16[2,2,256,1152]{3,2,1,0:T(8,128)(2,1)}, bf16[2,2,256,1152]{3,2,1,0:T(8,128)(2,1)}, u32[]{:S(2)}, u32[]{:S(2)}) collective-permute-start(bf16[2,2,256,1152]{3,2,1,0:T(8,128)(2,1)} %pad_maximum_fusion.1), channel_id=1, source_target_pairs={{0,1},{1,0},{2,3},{3,2},{4,5},{5,4},{6,7},{7,6},{8,9},{9,8},{10,11... | collective-permute-start | bytes 7077896 | tf_op jit(solution)/shard_map/ppermute | solution.py:23
  93.7 11.3 %collective-permute-start = (bf16[256,768]{1,0:T(8,128)(2,1)S(1)}, bf16[256,768]{1,0:T(8,128)(2,1)S(1)}, u32[]{:S(2)}, u32[]{:S(2)}) collective-permute-start(bf16[256,768]{1,0:T(8,128)(2,1)S(1)} %get-tuple-element.192), channel_id=1, source_target_pairs={{0,2},{1,3},{2,0},{3,1},{4,6},{5,7},{6,4},{7,5},{8,10},{9,11},{10,... | collective-permute-start | bytes 1179656 | tf_op jit(solution)/shard_map/ppermute | solution.py:28
  97.2 11.8 %collective-permute-start.2 = (bf16[256,768]{1,0:T(8,128)(2,1)S(1)}, bf16[256,768]{1,0:T(8,128)(2,1)S(1)}, u32[]{:S(2)}, u32[]{:S(2)}) collective-permute-start(bf16[256,768]{1,0:T(8,128)(2,1)S(1)} %get-tuple-element.192), channel_id=1, source_target_pairs={{0,1},{1,0},{2,3},{3,2},{4,5},{5,4},{6,7},{7,6},{8,9},{9,8},{10,11... | collective-permute-start | bytes 1179656 | tf_op jit(solution)/shard_map/ppermute | solution.py:23
  105.1 15.4 %collective-permute-start.1 = (bf16[256,768]{1,0:T(8,128)(2,1)S(1)}, bf16[256,768]{1,0:T(8,128)(2,1)S(1)}, u32[]{:S(2)}, u32[]{:S(2)}) collective-permute-start(bf16[256,768]{1,0:T(8,128)(2,1)S(1)} %get-tuple-element.73), channel_id=1, source_target_pairs={{0,2},{1,3},{2,0},{3,1},{4,6},{5,7},{6,4},{7,5},{8,10},{9,11},{10,... | collective-permute-start | bytes 1179656 | tf_op jit(solution)/shard_map/ppermute | solution.py:28
  108.5 16.0 %collective-permute-start.4 = (bf16[256,768]{1,0:T(8,128)(2,1)S(1)}, bf16[256,768]{1,0:T(8,128)(2,1)S(1)}, u32[]{:S(2)}, u32[]{:S(2)}) collective-permute-start(bf16[256,768]{1,0:T(8,128)(2,1)S(1)} %get-tuple-element.73), channel_id=1, source_target_pairs={{0,1},{1,0},{2,3},{3,2},{4,5},{5,4},{6,7},{7,6},{8,9},{9,8},{10,11... | collective-permute-start | bytes 1179656 | tf_op jit(solution)/shard_map/ppermute | solution.py:23
  122.0 15.8 %collective-permute-start.7 = (bf16[256,1152]{1,0:T(8,128)(2,1)S(1)}, bf16[256,1152]{1,0:T(8,128)(2,1)S(1)}, u32[]{:S(2)}, u32[]{:S(2)}) collective-permute-start(bf16[256,1152]{1,0:T(8,128)(2,1)S(1)} %get-tuple-element.77), channel_id=1, source_target_pairs={{0,2},{1,3},{2,0},{3,1},{4,6},{5,7},{6,4},{7,5},{8,10},{9,11},{10,... | collective-permute-start | bytes 1769480 | tf_op jit(solution)/shard_map/ppermute | solution.py:28
  138.6 38.6 %collective-permute-start.8 = (bf16[512,1152]{1,0:T(8,128)(2,1)}, bf16[512,1152]{1,0:T(8,128)(2,1)}, u32[]{:S(2)}, u32[]{:S(2)}) collective-permute-start(bf16[512,1152]{1,0:T(8,128)(2,1)} %constant_dynamic-update-slice_fusion.2.low_ref), channel_id=1, source_target_pairs={{0,1},{1,0},{2,3},{3,2},{4,5},{5,4},{6,7},{7,6},{8,9},{9,8},{10,11... | collective-permute-start | bytes 3538952 | tf_op jit(solution)/shard_map/ppermute | solution.py:23
  142.7 34.5 %collective-permute-start.6 = (bf16[256,1152]{1,0:T(8,128)(2,1)}, bf16[256,1152]{1,0:T(8,128)(2,1)}, u32[]{:S(2)}, u32[]{:S(2)}) collective-permute-start(bf16[256,1152]{1,0:T(8,128)(2,1)} %get-tuple-element.76), channel_id=1, source_target_pairs={{0,2},{1,3},{2,0},{3,1},{4,6},{5,7},{6,4},{7,5},{8,10},{9,11},{10,... | collective-permute-start | bytes 1769480 | tf_op jit(solution)/shard_map/ppermute | solution.py:28
  241.4 16.5 %collective-permute-start.14 = (bf16[256,1152]{1,0:T(8,128)(2,1)}, bf16[256,1152]{1,0:T(8,128)(2,1)S(1)}, u32[]{:S(2)}, u32[]{:S(2)}) collective-permute-start(bf16[256,1152]{1,0:T(8,128)(2,1)} %add_convert_fusion.3), channel_id=1, source_target_pairs={{0,2},{1,3},{2,0},{3,1},{4,6},{5,7},{6,4},{7,5},{8,10},{9,11},{10,... | collective-permute-start | bytes 1769480 | tf_op jit(solution)/shard_map/ppermute | solution.py:28
  242.9 50.5 %collective-permute-start.17 = (bf16[256,1152]{1,0:T(8,128)(2,1)}, bf16[256,1152]{1,0:T(8,128)(2,1)}, u32[]{:S(2)}, u32[]{:S(2)}) collective-permute-start(bf16[256,1152]{1,0:T(8,128)(2,1)} %add_convert_fusion.2), channel_id=1, source_target_pairs={{0,2},{1,3},{2,0},{3,1},{4,6},{5,7},{6,4},{7,5},{8,10},{9,11},{10,... | collective-permute-start | bytes 1769480 | tf_op jit(solution)/shard_map/ppermute | solution.py:28
  290.7 22.4 %collective-permute-start.20 = (bf16[512,768]{1,0:T(8,128)(2,1)}, bf16[512,768]{1,0:T(8,128)(2,1)}, u32[]{:S(2)}, u32[]{:S(2)}) collective-permute-start(bf16[512,768]{1,0:T(8,128)(2,1)} %get-tuple-element.107), channel_id=1, source_target_pairs={{0,1},{1,0},{2,3},{3,2},{4,5},{5,4},{6,7},{7,6},{8,9},{9,8},{10,11... | collective-permute-start | bytes 2359304 | tf_op jit(solution)/shard_map/ppermute | solution.py:23
  293.0 44.4 %collective-permute-start.15 = (bf16[512,1152]{1,0:T(8,128)(2,1)}, bf16[512,1152]{1,0:T(8,128)(2,1)}, u32[]{:S(2)}, u32[]{:S(2)}) collective-permute-start(bf16[512,1152]{1,0:T(8,128)(2,1)} %copy-done.74), channel_id=1, source_target_pairs={{0,1},{1,0},{2,3},{3,2},{4,5},{5,4},{6,7},{7,6},{8,9},{9,8},{10,11... | collective-permute-start | bytes 3538952 | tf_op jit(solution)/shard_map/ppermute | solution.py:23
  312.5 26.2 %collective-permute-start.24 = (bf16[1152,384]{1,0:T(8,128)(2,1)S(1)}, bf16[1152,384]{1,0:T(8,128)(2,1)S(1)}, u32[]{:S(2)}, u32[]{:S(2)}) collective-permute-start(bf16[1152,384]{1,0:T(8,128)(2,1)S(1)} %convolution_convert_fusion.5), channel_id=1, source_target_pairs={{0,1},{1,0},{2,3},{3,2},{4,5},{5,4},{6,7},{7,6},{8,9},{9,8},{10,11... | collective-permute-start | bytes 2654216 | tf_op jit(solution)/shard_map/ppermute | solution.py:23
  312.6 51.5 %collective-permute-start.18 = (bf16[512,1152]{1,0:T(8,128)(2,1)}, bf16[512,1152]{1,0:T(8,128)(2,1)S(1)}, u32[]{:S(2)}, u32[]{:S(2)}) collective-permute-start(bf16[512,1152]{1,0:T(8,128)(2,1)} %copy-done.73), channel_id=1, source_target_pairs={{0,1},{1,0},{2,3},{3,2},{4,5},{5,4},{6,7},{7,6},{8,9},{9,8},{10,11... | collective-permute-start | bytes 3538952 | tf_op jit(solution)/shard_map/ppermute | solution.py:23
  314.2 21.2 %collective-permute-start.23 = (bf16[256,768]{1,0:T(8,128)(2,1)S(1)}, bf16[256,768]{1,0:T(8,128)(2,1)S(1)}, u32[]{:S(2)}, u32[]{:S(2)}) collective-permute-start(bf16[256,768]{1,0:T(8,128)(2,1)S(1)} %add_convert_fusion.5), channel_id=1, source_target_pairs={{0,2},{1,3},{2,0},{3,1},{4,6},{5,7},{6,4},{7,5},{8,10},{9,11},{10,... | collective-permute-start | bytes 1179656 | tf_op jit(solution)/shard_map/ppermute | solution.py:28
  338.7 26.9 %collective-permute-start.16 = (bf16[256,1152]{1,0:T(8,128)(2,1)S(1)}, bf16[256,1152]{1,0:T(8,128)(2,1)S(1)}, u32[]{:S(2)}, u32[]{:S(2)}) collective-permute-start(bf16[256,1152]{1,0:T(8,128)(2,1)S(1)} %add_convert_fusion.1), channel_id=1, source_target_pairs={{0,2},{1,3},{2,0},{3,1},{4,6},{5,7},{6,4},{7,5},{8,10},{9,11},{10,... | collective-permute-start | bytes 1769480 | tf_op jit(solution)/shard_map/ppermute | solution.py:28
  340.2 22.7 %collective-permute-start.22 = (bf16[256,768]{1,0:T(8,128)(2,1)S(1)}, bf16[256,768]{1,0:T(8,128)(2,1)S(1)}, u32[]{:S(2)}, u32[]{:S(2)}) collective-permute-start(bf16[256,768]{1,0:T(8,128)(2,1)S(1)} %add_convert_fusion.4), channel_id=1, source_target_pairs={{0,2},{1,3},{2,0},{3,1},{4,6},{5,7},{6,4},{7,5},{8,10},{9,11},{10,... | collective-permute-start | bytes 1179656 | tf_op jit(solution)/shard_map/ppermute | solution.py:28
  345.6 32.0 %collective-permute-start.33 = (bf16[2,4,144,384]{3,2,1,0:T(8,128)(2,1)}, bf16[2,4,144,384]{3,2,1,0:T(8,128)(2,1)}, u32[]{:S(2)}, u32[]{:S(2)}) collective-permute-start(bf16[2,4,144,384]{3,2,1,0:T(8,128)(2,1)} %fusion.10), channel_id=1, source_target_pairs={{0,4},{4,0},{8,12},{12,8},{16,20},{20,16},{24,28},{28,24},{1,5},{5... | collective-permute-start | bytes 2654216 | tf_op jit(solution)/shard_map/ppermute | solution.py:540
  364.1 9.1 %collective-permute-start.25 = (bf16[1152,384]{1,0:T(8,128)(2,1)S(1)}, bf16[1152,384]{1,0:T(8,128)(2,1)S(1)}, u32[]{:S(2)}, u32[]{:S(2)}) collective-permute-start(bf16[1152,384]{1,0:T(8,128)(2,1)S(1)} %convolution_convert_fusion.4), channel_id=1, source_target_pairs={{0,1},{1,0},{2,3},{3,2},{4,5},{5,4},{6,7},{7,6},{8,9},{9,8},{10,11... | collective-permute-start | bytes 2654216 | tf_op jit(solution)/shard_map/ppermute | solution.py:23
  365.2 36.0 %collective-permute-start.19 = (bf16[256,1152]{1,0:T(8,128)(2,1)}, bf16[256,1152]{1,0:T(8,128)(2,1)}, u32[]{:S(2)}, u32[]{:S(2)}) collective-permute-start(bf16[256,1152]{1,0:T(8,128)(2,1)} %add_convert_fusion), channel_id=1, source_target_pairs={{0,2},{1,3},{2,0},{3,1},{4,6},{5,7},{6,4},{7,5},{8,10},{9,11},{10,... | collective-permute-start | bytes 1769480 | tf_op jit(solution)/shard_map/ppermute | solution.py:28
  375.6 24.5 %collective-permute-start.26 = (bf16[1152,384]{1,0:T(8,128)(2,1)}, bf16[1152,384]{1,0:T(8,128)(2,1)S(1)}, u32[]{:S(2)}, u32[]{:S(2)}) collective-permute-start(bf16[1152,384]{1,0:T(8,128)(2,1)} %get-tuple-element.218), channel_id=1, source_target_pairs={{0,2},{1,3},{2,0},{3,1},{4,6},{5,7},{6,4},{7,5},{8,10},{9,11},{10,... | collective-permute-start | bytes 2654216 | tf_op jit(solution)/shard_map/ppermute | solution.py:28
  380.7 22.7 %collective-permute-start.34 = (bf16[2,144,384]{2,1,0:T(8,128)(2,1)S(1)}, bf16[2,144,384]{2,1,0:T(8,128)(2,1)S(1)}, u32[]{:S(2)}, u32[]{:S(2)}) collective-permute-start(bf16[2,144,384]{2,1,0:T(8,128)(2,1)S(1)} %get-tuple-element.189), channel_id=1, source_target_pairs={{0,8},{4,12},{8,16},{12,20},{16,24},{20,28},{24,0},{28,4},{1,9},{5... | collective-permute-start | bytes 663560 | tf_op jit(solution)/shard_map/ppermute | solution.py:549
  381.1 22.3 %collective-permute-start.36 = (bf16[2,144,384]{2,1,0:T(8,128)(2,1)S(1)}, bf16[2,144,384]{2,1,0:T(8,128)(2,1)S(1)}, u32[]{:S(2)}, u32[]{:S(2)}) collective-permute-start(bf16[2,144,384]{2,1,0:T(8,128)(2,1)S(1)} %get-tuple-element.190), channel_id=1, source_target_pairs={{0,24},{4,28},{8,0},{12,4},{16,8},{20,12},{24,16},{28,20},{1,25},{... | collective-permute-start | bytes 663560 | tf_op jit(solution)/shard_map/ppermute | solution.py:549
  384.8 18.9 %collective-permute-start.35 = (bf16[2,144,384]{2,1,0:T(8,128)(2,1)S(1)}, bf16[2,144,384]{2,1,0:T(8,128)(2,1)S(1)}, u32[]{:S(2)}, u32[]{:S(2)}) collective-permute-start(bf16[2,144,384]{2,1,0:T(8,128)(2,1)S(1)} %get-tuple-element.191), channel_id=1, source_target_pairs={{0,16},{4,20},{8,24},{12,28},{16,0},{20,4},{24,8},{28,12},{1,17},{... | collective-permute-start | bytes 663560 | tf_op jit(solution)/shard_map/ppermute | solution.py:549
  400.5 12.9 %collective-permute-start.27 = (bf16[4,160,384]{2,1,0:T(8,128)(2,1)S(1)}, bf16[4,160,384]{2,1,0:T(8,128)(2,1)S(1)}, u32[]{:S(2)}, u32[]{:S(2)}) collective-permute-start(bf16[4,160,384]{2,1,0:T(8,128)(2,1)S(1)} %fusion.21), channel_id=1, source_target_pairs={{0,4},{4,0},{8,12},{12,8},{16,20},{20,16},{24,28},{28,24},{1,5},{5... | collective-permute-start | bytes 1474568 | tf_op jit(solution)/shard_map/ppermute | solution.py:540
  403.9 13.7 %collective-permute-start.37 = (bf16[144,384]{1,0:T(8,128)(2,1)S(1)}, bf16[144,384]{1,0:T(8,128)(2,1)S(1)}, u32[]{:S(2)}, u32[]{:S(2)}) collective-permute-start(bf16[144,384]{1,0:T(8,128)(2,1)S(1)} %fusion.62), channel_id=1, source_target_pairs={{0,2},{1,3},{2,0},{3,1},{4,6},{5,7},{6,4},{7,5},{8,10},{9,11},{10,... | collective-permute-start | bytes 331784 | tf_op jit(solution)/shard_map/ppermute | solution.py:28
  413.7 8.2 %collective-permute-start.28 = (bf16[160,384]{1,0:T(8,128)(2,1)S(1)}, bf16[160,384]{1,0:T(8,128)(2,1)S(1)}, u32[]{:S(2)}, u32[]{:S(2)}) collective-permute-start(bf16[160,384]{1,0:T(8,128)(2,1)S(1)} %get-tuple-element.196), channel_id=1, source_target_pairs={{0,8},{4,12},{8,16},{12,20},{16,24},{20,28},{24,0},{28,4},{1,9},{5... | collective-permute-start | bytes 368648 | tf_op jit(solution)/shard_map/ppermute | solution.py:549
  417.5 9.4 %collective-permute-start.29 = (bf16[160,384]{1,0:T(8,128)(2,1)S(1)}, bf16[160,384]{1,0:T(8,128)(2,1)S(1)}, u32[]{:S(2)}, u32[]{:S(2)}) collective-permute-start(bf16[160,384]{1,0:T(8,128)(2,1)S(1)} %get-tuple-element.198), channel_id=1, source_target_pairs={{0,16},{4,20},{8,24},{12,28},{16,0},{20,4},{24,8},{28,12},{1,17},{... | collective-permute-start | bytes 368648 | tf_op jit(solution)/shard_map/ppermute | solution.py:549
  (125 other events, 779.6 us)
Sparse Core Ops, SparseCore 0:
  11.6 77.1 all-gather.3
  91.6 85.5 all-gather.5
  241.5 102.3 reduce-scatter.1

commit v6 on v5

--- a/solution.py
+++ b/solution.py
@@ -75,8 +75,7 @@
 OUT_CHUNKS = ((3, 1), (2, 0), (3, 0))
 
 
-def call(kernel, name, arrays, specs, outs, out_specs, flops=0, scalars=(), aliases=None, **more):
-    moved = sum(x.size * x.dtype.itemsize for x in (*arrays, *jax.tree.leaves(outs)))
+def call(kernel, name, arrays, specs, outs, out_specs, scalars=(), aliases=None, **more):
     return pl.pallas_call(
         kernel,
         grid_spec=pltpu.PrefetchScalarGridSpec(
@@ -88,8 +87,10 @@
         ),
         out_shape=outs,
         input_output_aliases=aliases or {},
-        compiler_params=pltpu.CompilerParams(vmem_limit_bytes=VMEM_MIB[name] << 20),
-        cost_estimate=pl.CostEstimate(flops=1, transcendentals=0, bytes_accessed=1),
+        compiler_params=pltpu.CompilerParams(vmem_limit_bytes=KERNELS[name][0] << 20),
+        cost_estimate=pl.CostEstimate(
+            flops=int(KERNELS[name][1] * FLOPS_PER_MICROSECOND), transcendentals=0, bytes_accessed=1
+        ),
         name=name,
     )(*scalars, *arrays)
 
@@ -107,17 +108,19 @@
 
 
 ANY = pl.BlockSpec(memory_space=pl.ANY)
-VMEM_MIB = {
-    "project_pairs": 24,
-    "project_queries": 24,
-    "attend": 28,
-    "leave": 20,
-    "feed": 40,
-    "enter": 24,
-    "attend_back": 36,
-    "pairs_back": 12,
-    "finish": 28,
+KERNELS = {
+    "project_pairs": (24, 1.8),
+    "project_queries": (24, 2.6),
+    "attend": (28, 11.3),
+    "leave": (20, 1.4),
+    "feed": (40, 18.5),
+    "feed_grads": (32, 17.0),
+    "enter": (24, 2.5),
+    "attend_back": (36, 17.3),
+    "pairs_back": (12, 0.8),
+    "finish": (28, 2.2),
 }
+FLOPS_PER_MICROSECOND = 1.15e9
 
 
 def project_pairs_kernel(x_ref, gain_ref, cosine_ref, sine_ref, wk, wv, pair_ref, normed_ref):
@@ -141,7 +144,6 @@
         [block(x.shape) for x in (x_rows, gain, cosine, sine)] + chunk_specs(width, PAIR_CHUNKS),
         [array((rows, pair_width)), array((rows, width))],
         [block((rows, pair_width)), block((rows, width))],
-        2 * rows * width * pair_width,
     )
 
 
@@ -161,7 +163,6 @@
         [block(x.shape) for x in (normed, cosine, sine)] + chunk_specs(width, QUERY_CHUNKS),
         array((rows, width)),
         block((rows, width)),
-        2 * rows * width * width,
     )
 
 
@@ -213,7 +214,6 @@
         [query_spec, own_spec] + [pair_spec] * 3 + [ANY] * len(more),
         array(queries.shape),
         query_spec,
-        16 * rows * rows * width,
         (counts,),
         {6: 0} if more else None,
         grid=(steps,),
@@ -279,7 +279,6 @@
         + [ANY] * len(more),
         [array(queries.shape)] + [array((2 * rows, pairs_own.shape[1]))] * 2,
         [query_spec, half_spec, half_spec],
-        40 * rows * rows * width,
         (counts,),
         {9: 0} if more else None,
         grid=(steps,),
@@ -305,12 +304,11 @@
         [here, here, block(gain.shape)] + chunk_specs(width, OUT_CHUNKS),
         [array((rows, width), F32), array((rows, width))],
         [block((rows, width))] * 2,
-        2 * rows * width * width,
-    )
-
-
-def feed_kernel(steps, low_ref, high_ref, grad_ref, weight_ref, *rest):
-    rows_ref, act_ref, inner_ref, out_low, out_high, back_low, back_high = rest[-7:]
+    )
+
+
+def feed_kernel(steps, places, low_ref, high_ref, grad_ref, weight_ref, *rest):
+    rows_ref, act_ref, inner_ref, out_ref, back_low, back_high = rest[-6:]
     step = pl.program_id(0)
     share = weight_ref.shape[1] // 3
     gate, up, down_t = (slice(i * share, (i + 1) * share) for i in range(3))
@@ -336,29 +334,27 @@
     inner_ref[:, gate] = grad_gate
     inner_ref[:, up] = grad_up
     back = dot_nt(grad_gate, weight_ref[:, gate]) + dot_nt(grad_up, weight_ref[:, up])
-    out = dot_nt(act, weight_ref[:, down_t])
+    out_ref[...] = dot_nt(act, weight_ref[:, down_t]).astype(BF16)
 
     @pl.when(step < steps // 2)
     def _():
-        out_low[...] = out.astype(BF16)
         back_low[...] = back.astype(BF16)
 
     @pl.when(step >= steps // 2)
     def _():
-        out_high[...] = out.astype(BF16)
         back_high[...] = back.astype(BF16)
 
 
-def feed(b, low, high, grads, weights, earlier):
+def feed(b, places, low, high, grads, weights, earlier):
     half, width = low.shape
     share = weights.shape[1] // 3
     steps = 4
     rows = 2 * half // steps
-    first = pl.BlockSpec((rows, width), lambda i: (jnp.minimum(i, steps // 2 - 1), 0))
-    second = pl.BlockSpec((rows, width), lambda i: (jnp.maximum(i - steps // 2, 0), 0))
+    first = pl.BlockSpec((rows, width), lambda i, p: (jnp.minimum(i, steps // 2 - 1), 0))
+    second = pl.BlockSpec((rows, width), lambda i, p: (jnp.maximum(i - steps // 2, 0), 0))
 
     def here(columns):
-        return pl.BlockSpec((rows, columns), lambda i: (b * steps + i, 0))
+        return pl.BlockSpec((rows, columns), lambda i, p: (b * steps + i, 0))
 
     more = [] if earlier is None else list(earlier)
     return call(
@@ -369,14 +365,42 @@
             first,
             second,
             here(width),
-            pl.BlockSpec(weights.shape, lambda i: (0, 0), pipeline_mode=pl.Buffered(1)),
+            pl.BlockSpec(weights.shape, lambda i, p: (0, 0), pipeline_mode=pl.Buffered(1)),
         ]
         + [ANY] * len(more),
         [array((4 * half, width)), array((4 * half, share)), array((4 * half, 2 * share))]
-        + [array((half, width))] * 4,
-        [here(width), here(share), here(2 * share), first, second, first, second],
-        24 * half * width * share,
-        aliases={4: 0, 5: 1, 6: 2} if more else None,
+        + [array((2 * half, width))]
+        + [array((half, width))] * 2,
+        [here(width), here(share), here(2 * share)]
+        + [pl.BlockSpec((rows, width), lambda i, p: (p[i], 0)), first, second],
+        (places,),
+        aliases={5: 0, 6: 1, 7: 2} if more else None,
+        grid=(steps,),
+    )
+
+
+def feed_grads_kernel(rows_ref, grad_ref, inner_ref, act_ref, out_ref):
+    share = act_ref.shape[1]
+    out_ref[:, : 2 * share] = dot_nn(rows_ref[...].T, inner_ref[...]).astype(BF16)
+    out_ref[:, 2 * share :] = dot_nn(grad_ref[...].T, act_ref[...]).astype(BF16)
+
+
+def feed_grads(rows, grads, inner_grads, activated):
+    count, width = rows.shape
+    share = activated.shape[1]
+    steps = 3
+    left = pl.BlockSpec((count, width // steps), lambda i: (0, i))
+
+    def held(columns):
+        return pl.BlockSpec((count, columns), lambda i: (0, 0), pipeline_mode=pl.Buffered(1))
+
+    return call(
+        feed_grads_kernel,
+        "feed_grads",
+        (rows, grads, inner_grads, activated),
+        [left, left, held(2 * share), held(share)],
+        array((width, 3 * share)),
+        pl.BlockSpec((width // steps, 3 * share), lambda i: (i, 0)),
         grid=(steps,),
     )
 
@@ -428,7 +452,6 @@
             array((8, width), F32),
         ],
         [full, here, full, block((8, width))],
-        2 * rows * width * width,
         (count,),
         {10: 1} if more else None,
     )
@@ -498,7 +521,6 @@
         + chunk_specs(width, PAIR_CHUNKS + QUERY_CHUNKS),
         [array((rows, width)), array((8, width), F32)],
         [block((rows, width)), block((8, width))],
-        10 * rows * width * width // 3,
     )
 
 
@@ -532,7 +554,7 @@
 
     groups = data_count // 2
     odd = (data_index & 1) == 1
-    group = data_index // 2
+    group = lax.shift_right_logical(data_index, 1)
 
     def beside(value):
         even_rows, odd_rows = value[..., 0, :, :], value[..., 1, :, :]
@@ -542,9 +564,13 @@
 
     def along(value):
         low = value.astype(BF16)
-        total = lax.dynamic_index_in_dim(value, group, 0, keepdims=False)
+        total = lax.dynamic_index_in_dim(
+            value, group, 0, keepdims=False, allow_negative_indices=False
+        )
         for step in range(1, groups):
-            sent = lax.dynamic_index_in_dim(low, (group + step) % groups, 0, keepdims=False)
+            sent = lax.dynamic_index_in_dim(
+                low, (group + step) & (groups - 1), 0, keepdims=False, allow_negative_indices=False
+            )
             moves = [(i, (i + 2 * step) % data_count) for i in range(data_count)]
             total = total + lax.ppermute(sent, "dp", moves).astype(F32)
         return total
@@ -660,35 +686,37 @@
         if b == micro - 1:
             mlp_full, _ = lax.optimization_barrier((mlp_full, across))
 
+    places = jnp.stack([tensor_index ^ x for x in BLOCK_XOR]).astype(jnp.int32)
     shared = None
     for b in range(micro):
         k = kept[b]
+        *shared, k["out"], k["part"], back_high = feed(
+            b, places, k["low"], k["high"], grad_ffn, mlp_full, shared
+        )
         if b > 0:
-            k["low"], kept[b - 1]["far_sent"] = lax.optimization_barrier(
-                (k["low"], kept[b - 1]["far_sent"])
+            back_high, kept[b - 1]["far_part"] = lax.optimization_barrier(
+                (back_high, far(kept[b - 1]["far_part"]))
             )
-        *shared, k["out_low"], k["out_high"], k["part"], back_high = feed(
-            b, k["low"], k["high"], grad_ffn, mlp_full, shared
-        )
         k["near_part"] = near(back_high)
-        k["far_sent"] = added(k["part"][row_share:], k["near_part"][row_share:])
-    shared[0], kept[-1]["far_sent"] = lax.optimization_barrier((shared[0], kept[-1]["far_sent"]))
+        k["far_part"] = added(k["part"][row_share:], k["near_part"][row_share:])
     hidden_rows, activated, inner_grads = shared
-    grad_mlp_w = row_major(
-        jnp.concatenate(
-            [
-                row_major(contract_rows(hidden_rows, inner_grads).astype(BF16)),
-                row_major(contract_rows(grad_ffn, activated).astype(BF16)),
-            ],
-            axis=1,
-        )
-    )
-    grad_mlp_w, kept[0]["middle"] = lax.optimization_barrier((grad_mlp_w, kept[0]["middle"]))
+    hidden_rows, kept[-1]["far_part"] = lax.optimization_barrier(
+        (hidden_rows, kept[-1]["far_part"])
+    )
+    kept[-1]["far_part"] = far(kept[-1]["far_part"])
+    grad_mlp_w = feed_grads(hidden_rows, grad_ffn, inner_grads, activated)
+    grad_mlp_w, kept[0]["middle"], kept[-1]["far_part"] = lax.optimization_barrier(
+        (grad_mlp_w, kept[0]["middle"], kept[-1]["far_part"])
+    )
 
     gain_two_grads = []
     branch = query_grads = pair_grads = None
 
     grad_mlp_w = lax.psum_scatter(grad_mlp_w, "dp", scatter_dimension=0, tiled=True)
+    def summed_out(b):
+        return lax.psum_scatter(kept[b]["out"], "tensor", scatter_dimension=0, tiled=True)
+
+    kept[0]["out"] = summed_out(0)
     for b in range(micro):
         k = kept[b]
         k["grad_middle"], branch, grad_att, gain_two_grad = enter(
@@ -696,7 +724,7 @@
             valid_rows[b][None],
             k["part"],
             k["near_part"],
-            far(k["far_sent"]),
+            k["far_part"],
             k["middle"],
             cot_rows,
             gain_two,
@@ -704,8 +732,9 @@
             branch,
         )
         gain_two_grads.append(gain_two_grad[0:1])
-        k["out_high"], grad_att = lax.optimization_barrier((k["out_high"], grad_att))
         if b > 0:
+            k["out"], grad_att = lax.optimization_barrier((k["out"], grad_att))
+            k["out"] = summed_out(b)
             kept[b - 1]["pair_far"], grad_att = lax.optimization_barrier(
                 (kept[b - 1]["pair_far"], grad_att)
             )
@@ -720,7 +749,7 @@
             b, k["pair_kept"], k["near_pair"], far(k["pair_far"]), cosine, sine, pair_grads
         )
 
-    outputs, input_grads, gain_one_grads = [], [], []
+    input_grads, gain_one_grads = [], []
     for b in range(micro):
         k = kept[b]
         input_grad, gain_one_grad = finish(
@@ -728,14 +757,6 @@
         )
         gain_one_grads.append(gain_one_grad[0:1])
         input_grads.append(input_grad)
-        out_near = near(k["out_high"])
-        out_far = far(added(k["out_low"][row_share:], out_near[row_share:]))
-        ffn_out = (
-            k["out_low"][:row_share].astype(F32)
-            + out_near[:row_share].astype(F32)
-            + out_far.astype(F32)
-        )
-        outputs.append(jnp.where(valids[b], k["middle"] + ffn_out, 0.0).astype(BF16))
 
     odd = (tensor_index & 1) == 1
     high = (tensor_index & 2) == 2
@@ -766,6 +787,11 @@
         gain_part,
         grad_mlp_w,
     )
+    outputs = []
+    for b in range(micro):
+        k = kept[b]
+        ffn_out = k["out"].astype(F32)
+        outputs.append(jnp.where(valids[b], k["middle"] + ffn_out, 0.0).astype(BF16))
     quarter = jnp.concatenate([first, second, gain_rows], axis=0).astype(BF16)
     other = far(quarter)
     pair = jnp.stack([pick(high, other, quarter), pick(high, quarter, other)])

time: 454 us -> 450 us (level)
  waiting for transfers between devices: 146 us -> 127 us
  Pallas kernels: 114 us -> 132 us
  local copies, waits for them, and re-layouts: 57.8 us -> 69.9 us
  matrix products: 24.6 us -> 15 us
    ppermute x14 -> x12, waiting for transfers between devices: 60.8 us -> 39.5 us  [far(): return lax.ppermute(value, 'tensor', [(i, i ^ 2) for i in range(count)])]
    pallas_call x16 -> x17, Pallas kernels: 114 us -> 132 us  [call(): pl.pallas_call(kernel, grid_spec=pltpu.PrefetchScalarGridSpec(num_scalar_...]
    ppermute x6, waiting for transfers between devices: 9.68 us -> 25.8 us  [along(): total = total + lax.ppermute(sent, 'dp', moves).astype(F32)]
    unnamed x236, local copies, waits for them, and re-layouts: 45.7 us -> 58.3 us
    dot_general x10 -> x8, matrix products: 24.6 us -> 15 us  [contract_rows(): lax.dot_general(left_side, right_side, (((0,), (0,)), ((), ())), preferre...]
    all_gather x1, waiting for transfers between devices: 30.1 us -> 21.6 us  [shards(): mlp_full = lax.all_gather(mlp_local, 'dp', axis=0, tiled=True)]
    all_gather x1, waiting for transfers between devices: 35.3 us -> 30.5 us  [shards(): attn_w = lax.all_gather(attn_quarter, ('tensor', 'dp'), axis=0, tiled=True)]
    ppermute x14 -> x12, starting transfers between devices: 15.6 us -> 15.8 us  [far(): return lax.ppermute(value, 'tensor', [(i, i ^ 2) for i in range(count)])]
  transfers between devices with their start and end apart: 43 -> 41, of which waited for: 15 -> 17; matrix products, arithmetic and copies ran while one was open for 14% -> 14% of each run, Pallas kernels for 17% -> 25%
where the time goes in v6:
time: 450 us; the launch traced here: 443 us
  Pallas kernels  132 us (29%)
  waiting for transfers between devices  127 us (28%)
  local copies, waits for them, and re-layouts  69.9 us (16%)
  other arithmetic  30.1 us (7%)
  starting transfers between devices  27.2 us (6%)
  blocking collectives  20.8 us (5%)
  between operations  20.8 us (5%)
  matrix products  15 us (3%)
    pallas_call x17, Pallas kernels, call(): pl.pallas_call(kernel, grid_spec=pltpu.PrefetchScalarGridSpec(num_scalar_...  132 us
    unnamed x236, local copies, waits for them, and re-layouts  58.3 us
    ppermute x12, waiting for transfers between devices, far(): return lax.ppermute(value, 'tensor', [(i, i ^ 2) for i in range(count)])  39.5 us
    all_gather x1, waiting for transfers between devices, shards(): attn_w = lax.all_gather(attn_quarter, ('tensor', 'dp'), axis=0, tiled=True)  30.5 us
    ppermute x6, waiting for transfers between devices, along(): total = total + lax.ppermute(sent, 'dp', moves).astype(F32)  25.8 us
    all_gather x1, waiting for transfers between devices, shards(): mlp_full = lax.all_gather(mlp_local, 'dp', axis=0, tiled=True)  21.6 us
    all_gather x1, blocking collectives, shards(): lax.all_gather(jnp.stack([gain_attn, gain_mlp]), 'dp', axis=1, tiled=True)  20.8 us
    ppermute x12, starting transfers between devices, far(): return lax.ppermute(value, 'tensor', [(i, i ^ 2) for i in range(count)])  15.8 us
  transfers between devices with their start and end apart: 41, of which 17 were waited for; matrix products, arithmetic and copies ran while one was open for 14% of the time, Pallas kernels for 25%

profile of v6, /device:TPU:0, one launch (start us, length us, event | category | flops | bytes accessed | tf_op | source)
XLA Modules:
  0.0 442.8 jit_solution(10965157514476094038)
XLA Ops:
  13.2 3.0 collective-permute-start.8
  17.2 20.8 %all-gather = bf16[8,144,2]{1,2,0:T(2,128)(2,1)S(1)} all-gather(bf16[1,144,2]{1,2,0:T(2,128)(2,1)S(1)} %maximum_bitcast_fusion.3), channel_id=1, replica_groups=mesh['dp'=8,'tensor'=4] {'dp'}, dimensions={0}, use_global_device_ids=true | all-gather | bytes 5184 | tf_op jit(solution)/shard_map/all_gather | solution.py:625
  38.0 8.0 %collective-permute-done.8 = bf16[2,256,1152]{2,1,0:T(8,128)(2,1)S(1)} collective-permute-done((bf16[2,256,1152]{2,1,0:T(8,128)(2,1)}, bf16[2,256,1152]{2,1,0:T(8,128)(2,1)S(1)}, u32[]{:S(2)}, u32[]{:S(2)}) %collective-permute-start.8) | collective-permute-done | bytes 1179680 | tf_op jit(solution)/shard_map/ppermute | solution.py:28
  57.7 30.5 %all-gather.4.cloned.1.call-done.wk.wv.w0.w1.w2 = bf16[4608,768]{1,0:T(8,128)(2,1)} async-done(((bf16[144,768]{1,0:T(8,128)(2,1)}), bf16[4608,768]{1,0:T(8,128)(2,1)}) %all-gather.4.cloned.1.call-update) | async-done | bytes 7077904 | tf_op jit(solution)/shard_map/all_gather | solution.py:622
  88.2 3.0 copy-done
  99.1 5.3 %collective-permute-done.p1 = bf16[256,768]{1,0:T(8,128)(2,1)S(1)} collective-permute-done((bf16[256,768]{1,0:T(8,128)(2,1)S(1)}, bf16[256,768]{1,0:T(8,128)(2,1)S(1)}, u32[]{:S(2)}, u32[]{:S(2)}) %collective-permute-start) | collective-permute-done | bytes 393248 | tf_op jit(solution)/shard_map/ppermute | solution.py:28
  106.9 11.4 %attend.2.rest_0_.o_ref = bf16[512,1152]{1,0:T(8,128)(2,1)S(1)} custom-call(s32[4]{0:T(128)S(1)} %pad_add_fusion.2.counts, bf16[512,1152]{1,0:T(8,128)(2,1)S(1)} %project_queries.1.q_ref, bf16[512,768]{1,0:T(8,128)(2,1)S(1)} %get-tuple-element.66.p0, bf16[256,768]{1,0:T(8,128)(2,1)S(1)} %collective-permute-done.p1, ...), custom_call_target="tpu_custom_call" | custom-call | flops 12995000320 | bytes 1 | tf_op jit(solution)/shard_map/attend/pallas_call | solution.py:79
  122.8 12.5 %collective-permute-done.10 = bf16[256,1152]{1,0:T(8,128)(2,1)S(1)} collective-permute-done((bf16[256,1152]{1,0:T(8,128)(2,1)S(1)}, bf16[256,1152]{1,0:T(8,128)(2,1)S(1)}, u32[]{:S(2)}, u32[]{:S(2)}) %collective-permute-start.10) | collective-permute-done | bytes 589856 | tf_op jit(solution)/shard_map/ppermute | solution.py:28
  136.2 11.2 %attend.3.o_ref = bf16[512,1152]{1,0:T(8,128)(2,1)S(1)} custom-call(s32[4]{0:T(128)S(1)} %pad_add_fusion.1.counts, bf16[512,1152]{1,0:T(8,128)(2,1)S(1)} %project_queries.1.q_ref, bf16[512,768]{1,0:T(8,128)(2,1)S(1)} %get-tuple-element.66.p0, bf16[256,768]{1,0:T(8,128)(2,1)S(1)} %collective-permute-done.1.p1, ...), custom_call_target="tpu_custom_call", output_to_operand_aliasing={{}: (6, {})} | custom-call | flops 12995000320 | bytes 1 | tf_op jit(solution)/shard_map/attend/pallas_call | solution.py:79
  155.0 21.6 %all-gather.6.cloned.1.call-done.weight_ref = bf16[1152,2304]{1,0:T(8,128)(2,1)} async-done(((bf16[144,2304]{1,0:T(8,128)(2,1)}), bf16[1152,2304]{1,0:T(8,128)(2,1)}) %all-gather.6.cloned.1.call-update) | async-done | bytes 5308432 | tf_op jit(solution)/shard_map/all_gather | solution.py:624
  177.2 19.6 %feed.2 = (bf16[2048,1152]{1,0:T(8,128)(2,1)}, bf16[2048,768]{1,0:T(8,128)(2,1)S(1)}, bf16[2048,1536]{1,0:T(8,128)(2,1)}, bf16[1024,1152]{1,0:T(8,128)(2,1)S(1)}...) custom-call(s32[4]{0:T(128)S(1)} %copy-done.57, ...), custom_call_target="tpu_custom_call" | custom-call | flops 21275000832 | bytes 1 | tf_op jit(solution)/shard_map/feed/pallas_call | solution.py:79
  209.4 19.3 %feed.3 = (bf16[2048,1152]{1,0:T(8,128)(2,1)}, bf16[2048,768]{1,0:T(8,128)(2,1)S(1)}, bf16[2048,1536]{1,0:T(8,128)(2,1)}, bf16[1024,1152]{1,0:T(8,128)(2,1)S(1)}...) custom-call(s32[4]{0:T(128)S(1)} %copy-done.58, ...), custom_call_target="tpu_custom_call", output_to_operand_aliasing={{0}: (5, {}), {1}: (6, {}), {2}: (7, {})} | custom-call | flops 21275000832 | bytes 1 | tf_op jit(solution)/shard_map/feed/pallas_call | solution.py:79
  242.5 15.2 %feed_grads.1 = bf16[1152,2304]{1,0:T(8,128)(2,1)S(1)} custom-call(bf16[2048,1152]{1,0:T(8,128)(2,1)S(1)} %copy-done.73, bf16[2048,1152]{1,0:T(8,128)(2,1)} %fusion.13.grad_ref, bf16[2048,1536]{1,0:T(8,128)(2,1)} %get-tuple-element.86.inner_ref, bf16[2048,768]{1,0:T(8,128)(2,1)S(1)} %copy-done.77), custom_call_target="tpu_custom_call" | custom-call | flops 19549999104 | bytes 1 | tf_op jit(solution)/shard_map/feed_grads/pallas_call | solution.py:79
  261.4 3.0 copy-done.2
  268.1 3.1 enter.2
  272.3 17.8 %attend_back.2 = (bf16[512,1152]{1,0:T(8,128)(2,1)S(1)}, bf16[512,768]{1,0:T(8,128)(2,1)S(1)}, bf16[512,768]{1,0:T(8,128)(2,1)}) custom-call(s32[4]{0:T(128)S(1)} %pad_add_fusion.2.counts, bf16[512,1152]{1,0:T(8,128)(2,1)S(1)} %copy-done.31, bf16[256,1152]{1,0:T(8,128)(2,1)S(1)} %get-tuple-element.99.g_ref, f32[32,256]{1,0:T(8,128)S(1)} %get-tuple-element.206.cos_ref, ...), custom_call_target="tpu_custom_call" | custom-call | flops 19894999040 | bytes 1 | tf_op jit(solution)/shard_map/attend_back/pallas_call | solution.py:79
  291.4 2.9 enter.3
  298.0 2.8 convolution_convert_fusion.3
  311.6 17.3 %attend_back.3 = (bf16[512,1152]{1,0:T(8,128)(2,1)S(1)}, bf16[512,768]{1,0:T(8,128)(2,1)S(1)}, bf16[512,768]{1,0:T(8,128)(2,1)S(1)}) custom-call(s32[4]{0:T(128)S(1)} %pad_add_fusion.1.counts, bf16[512,1152]{1,0:T(8,128)(2,1)S(1)} %copy-done.32, bf16[256,1152]{1,0:T(8,128)(2,1)S(1)} %copy-done.60, ...), custom_call_target="tpu_custom_call", output_to_operand_aliasing={{0}: (9, {})} | custom-call | flops 19894999040 | bytes 1 | tf_op jit(solution)/shard_map/attend_back/pallas_call | solution.py:79
  331.7 3.3 convolution_add_fusion.3
  342.4 5.4 %collective-permute-done.18.far_ref = bf16[256,768]{1,0:T(8,128)(2,1)S(1)} collective-permute-done((bf16[256,768]{1,0:T(8,128)(2,1)S(1)}, bf16[256,768]{1,0:T(8,128)(2,1)S(1)}, u32[]{:S(2)}, u32[]{:S(2)}) %collective-permute-start.18) | collective-permute-done | bytes 393248 | tf_op jit(solution)/shard_map/ppermute | solution.py:28
  352.6 3.0 copy-done.3
  362.2 3.7 select_convert_fusion.1
  370.7 3.8 collective-permute-start.32
  374.6 5.9 %collective-permute-done.30 = bf16[2,144,384]{2,1,0:T(8,128)(2,1)S(1)} collective-permute-done((bf16[2,144,384]{2,1,0:T(8,128)(2,1)S(1)}, bf16[2,144,384]{2,1,0:T(8,128)(2,1)S(1)}, u32[]{:S(2)}, u32[]{:S(2)}) %collective-permute-start.30) | collective-permute-done | bytes 221216 | tf_op jit(solution)/shard_map/ppermute | solution.py:575
  383.0 10.5 %collective-permute-done.31 = bf16[2,144,384]{2,1,0:T(8,128)(2,1)S(1)} collective-permute-done((bf16[2,144,384]{2,1,0:T(8,128)(2,1)S(1)}, bf16[2,144,384]{2,1,0:T(8,128)(2,1)S(1)}, u32[]{:S(2)}, u32[]{:S(2)}) %collective-permute-start.31) | collective-permute-done | bytes 221216 | tf_op jit(solution)/shard_map/ppermute | solution.py:575
  399.5 3.0 collective-permute-done.33
  402.6 7.2 %collective-permute-done.23 = bf16[4,160,384]{2,1,0:T(8,128)(2,1)S(1)} collective-permute-done((bf16[4,160,384]{2,1,0:T(8,128)(2,1)S(1)}, bf16[4,160,384]{2,1,0:T(8,128)(2,1)S(1)}, u32[]{:S(2)}, u32[]{:S(2)}) %collective-permute-start.23) | collective-permute-done | bytes 491552 | tf_op jit(solution)/shard_map/ppermute | solution.py:562
  410.1 3.8 collective-permute-start.26
  415.2 3.0 collective-permute-done.24
  418.3 3.8 collective-permute-done.25
  424.5 5.3 %collective-permute-done.34 = bf16[304,384]{1,0:T(8,128)(2,1)S(1)} collective-permute-done((bf16[304,384]{1,0:T(8,128)(2,1)S(1)}, bf16[304,384]{1,0:T(8,128)(2,1)S(1)}, u32[]{:S(2)}, u32[]{:S(2)}) %collective-permute-start.34) | collective-permute-done | bytes 233504 | tf_op jit(solution)/shard_map/ppermute | solution.py:28
  (388 shorter events, 131.9 us)
Async XLA Ops:
  7.2 81.0 %all-gather.4.cloned.1.call-start = ((), (), s32[]{:S(2)}) async-start(), calls=%async_computation.3 | async-start | bytes 7299072 | tf_op jit(solution)/shard_map/all_gather | solution.py:622
  9.5 167.1 %all-gather.6.cloned.1.call-start = ((), (), s32[]{:S(2)}) async-start(), calls=%async_computation.4 | async-start | bytes 5971968 | tf_op jit(solution)/shard_map/all_gather | solution.py:624
  13.2 32.8 %collective-permute-start.8 = (bf16[2,256,1152]{2,1,0:T(8,128)(2,1)}, bf16[2,256,1152]{2,1,0:T(8,128)(2,1)S(1)}, u32[]{:S(2)}, u32[]{:S(2)}) collective-permute-start(bf16[2,256,1152]{2,1,0:T(8,128)(2,1)} %get-tuple-element.170), channel_id=1, source_target_pairs={{0,2},{1,3},{2,0},{3,1},{4,6},{5,7},{6,4},{7,5},{8,10},{9,11},{10,... | collective-permute-start | bytes 3538952 | tf_op jit(solution)/shard_map/ppermute | solution.py:28
  17.1 332.9 %reduce-scatter.4.cloned.1.call-start = ((), (), s32[]{:S(2)}) async-start(), calls=%async_computation.5 | async-start | bytes 2949120 | tf_op jit(solution)/shard_map/reduce_scatter | solution.py:717
  47.9 7.9 %collective-permute-start.9 = (bf16[2,2,256,1152]{3,2,1,0:T(8,128)(2,1)}, bf16[2,2,256,1152]{3,2,1,0:T(8,128)(2,1)}, u32[]{:S(2)}, u32[]{:S(2)}) collective-permute-start(bf16[2,2,256,1152]{3,2,1,0:T(8,128)(2,1)} %pad_maximum_fusion), channel_id=1, source_target_pairs={{0,1},{1,0},{2,3},{3,2},{4,5},{5,4},{6,7},{7,6},{8,9},{9,8},{10,11... | collective-permute-start | bytes 7077896 | tf_op jit(solution)/shard_map/ppermute | solution.py:23
  93.1 11.3 %collective-permute-start = (bf16[256,768]{1,0:T(8,128)(2,1)S(1)}, bf16[256,768]{1,0:T(8,128)(2,1)S(1)}, u32[]{:S(2)}, u32[]{:S(2)}) collective-permute-start(bf16[256,768]{1,0:T(8,128)(2,1)S(1)} %get-tuple-element.186), channel_id=1, source_target_pairs={{0,2},{1,3},{2,0},{3,1},{4,6},{5,7},{6,4},{7,5},{8,10},{9,11},{10,... | collective-permute-start | bytes 1179656 | tf_op jit(solution)/shard_map/ppermute | solution.py:28
  96.5 10.4 %collective-permute-start.2 = (bf16[256,768]{1,0:T(8,128)(2,1)S(1)}, bf16[256,768]{1,0:T(8,128)(2,1)S(1)}, u32[]{:S(2)}, u32[]{:S(2)}) collective-permute-start(bf16[256,768]{1,0:T(8,128)(2,1)S(1)} %get-tuple-element.186), channel_id=1, source_target_pairs={{0,1},{1,0},{2,3},{3,2},{4,5},{5,4},{6,7},{7,6},{8,9},{9,8},{10,11... | collective-permute-start | bytes 1179656 | tf_op jit(solution)/shard_map/ppermute | solution.py:23
  105.4 16.0 %collective-permute-start.1 = (bf16[256,768]{1,0:T(8,128)(2,1)S(1)}, bf16[256,768]{1,0:T(8,128)(2,1)S(1)}, u32[]{:S(2)}, u32[]{:S(2)}) collective-permute-start(bf16[256,768]{1,0:T(8,128)(2,1)S(1)} %get-tuple-element.70), channel_id=1, source_target_pairs={{0,2},{1,3},{2,0},{3,1},{4,6},{5,7},{6,4},{7,5},{8,10},{9,11},{10,... | collective-permute-start | bytes 1179656 | tf_op jit(solution)/shard_map/ppermute | solution.py:28
  119.7 15.5 %collective-permute-start.10 = (bf16[256,1152]{1,0:T(8,128)(2,1)S(1)}, bf16[256,1152]{1,0:T(8,128)(2,1)S(1)}, u32[]{:S(2)}, u32[]{:S(2)}) collective-permute-start(bf16[256,1152]{1,0:T(8,128)(2,1)S(1)} %get-tuple-element.75), channel_id=1, source_target_pairs={{0,2},{1,3},{2,0},{3,1},{4,6},{5,7},{6,4},{7,5},{8,10},{9,11},{10,... | collective-permute-start | bytes 1769480 | tf_op jit(solution)/shard_map/ppermute | solution.py:28
  121.4 14.7 %collective-permute-start.4 = (bf16[256,768]{1,0:T(8,128)(2,1)S(1)}, bf16[256,768]{1,0:T(8,128)(2,1)S(1)}, u32[]{:S(2)}, u32[]{:S(2)}) collective-permute-start(bf16[256,768]{1,0:T(8,128)(2,1)S(1)} %get-tuple-element.70), channel_id=1, source_target_pairs={{0,1},{1,0},{2,3},{3,2},{4,5},{5,4},{6,7},{7,6},{8,9},{9,8},{10,11... | collective-permute-start | bytes 1179656 | tf_op jit(solution)/shard_map/ppermute | solution.py:23
  121.4 14.7 %collective-permute-start.5 = (bf16[256,768]{1,0:T(8,128)(2,1)S(1)}, bf16[256,768]{1,0:T(8,128)(2,1)S(1)}, u32[]{:S(2)}, u32[]{:S(2)}) collective-permute-start(bf16[256,768]{1,0:T(8,128)(2,1)S(1)} %collective-permute-done.1.p1), channel_id=1, source_target_pairs={{0,1},{1,0},{2,3},{3,2},{4,5},{5,4},{6,7},{7,6},{8,9},{9,8},{10,11... | collective-permute-start | bytes 1179656 | tf_op jit(solution)/shard_map/ppermute | solution.py:23
  136.1 40.5 %collective-permute-start.11 = (bf16[512,1152]{1,0:T(8,128)(2,1)}, bf16[512,1152]{1,0:T(8,128)(2,1)}, u32[]{:S(2)}, u32[]{:S(2)}) collective-permute-start(bf16[512,1152]{1,0:T(8,128)(2,1)} %constant_dynamic-update-slice_fusion.2.low_ref), channel_id=1, source_target_pairs={{0,1},{1,0},{2,3},{3,2},{4,5},{5,4},{6,7},{7,6},{8,9},{9,8},{10,11... | collective-permute-start | bytes 3538952 | tf_op jit(solution)/shard_map/ppermute | solution.py:23
  150.5 26.1 %collective-permute-start.6 = (bf16[256,1152]{1,0:T(8,128)(2,1)}, bf16[256,1152]{1,0:T(8,128)(2,1)}, u32[]{:S(2)}, u32[]{:S(2)}) collective-permute-start(bf16[256,1152]{1,0:T(8,128)(2,1)} %get-tuple-element.73), channel_id=1, source_target_pairs={{0,2},{1,3},{2,0},{3,1},{4,6},{5,7},{6,4},{7,5},{8,10},{9,11},{10,... | collective-permute-start | bytes 1769480 | tf_op jit(solution)/shard_map/ppermute | solution.py:28
  204.2 205.7 %reduce-scatter.8.cloned.1.call-start = ((), (), s32[]{:S(2)}) async-start(), calls=%async_computation.7 | async-start | bytes 5971968 | tf_op jit(solution)/shard_map/reduce_scatter | solution.py:715
  205.7 26.1 %collective-permute-start.13 = (bf16[256,1152]{1,0:T(8,128)(2,1)S(1)}, bf16[256,1152]{1,0:T(8,128)(2,1)S(1)}, u32[]{:S(2)}, u32[]{:S(2)}) collective-permute-start(bf16[256,1152]{1,0:T(8,128)(2,1)S(1)} %add_convert_fusion.1), channel_id=1, source_target_pairs={{0,2},{1,3},{2,0},{3,1},{4,6},{5,7},{6,4},{7,5},{8,10},{9,11},{10,... | collective-permute-start | bytes 1769480 | tf_op jit(solution)/shard_map/ppermute | solution.py:28
  236.6 23.6 %collective-permute-start.15 = (bf16[256,1152]{1,0:T(8,128)(2,1)}, bf16[256,1152]{1,0:T(8,128)(2,1)}, u32[]{:S(2)}, u32[]{:S(2)}) collective-permute-start(bf16[256,1152]{1,0:T(8,128)(2,1)} %add_convert_fusion), channel_id=1, source_target_pairs={{0,2},{1,3},{2,0},{3,1},{4,6},{5,7},{6,4},{7,5},{8,10},{9,11},{10,... | collective-permute-start | bytes 1769480 | tf_op jit(solution)/shard_map/ppermute | solution.py:28
  260.2 153.8 %reduce-scatter.6.cloned.1.call-start = ((), (), s32[]{:S(2)}) async-start(), calls=%async_computation.6 | async-start | bytes 2949120 | tf_op jit(solution)/shard_map/reduce_scatter | solution.py:717
  290.1 11.0 %collective-permute-start.16 = (bf16[512,768]{1,0:T(8,128)(2,1)}, bf16[512,768]{1,0:T(8,128)(2,1)}, u32[]{:S(2)}, u32[]{:S(2)}) collective-permute-start(bf16[512,768]{1,0:T(8,128)(2,1)} %get-tuple-element.101), channel_id=1, source_target_pairs={{0,1},{1,0},{2,3},{3,2},{4,5},{5,4},{6,7},{7,6},{8,9},{9,8},{10,11... | collective-permute-start | bytes 2359304 | tf_op jit(solution)/shard_map/ppermute | solution.py:23
  300.9 30.9 %collective-permute-start.20 = (bf16[1152,384]{1,0:T(8,128)(2,1)}, bf16[1152,384]{1,0:T(8,128)(2,1)}, u32[]{:S(2)}, u32[]{:S(2)}) collective-permute-start(bf16[1152,384]{1,0:T(8,128)(2,1)} %convolution_convert_fusion.3), channel_id=1, source_target_pairs={{0,1},{1,0},{2,3},{3,2},{4,5},{5,4},{6,7},{7,6},{8,9},{9,8},{10,11... | collective-permute-start | bytes 2654216 | tf_op jit(solution)/shard_map/ppermute | solution.py:23
  303.1 31.9 %collective-permute-start.19 = (bf16[256,768]{1,0:T(8,128)(2,1)S(1)}, bf16[256,768]{1,0:T(8,128)(2,1)S(1)}, u32[]{:S(2)}, u32[]{:S(2)}) collective-permute-start(bf16[256,768]{1,0:T(8,128)(2,1)S(1)} %add_convert_fusion.3), channel_id=1, source_target_pairs={{0,2},{1,3},{2,0},{3,1},{4,6},{5,7},{6,4},{7,5},{8,10},{9,11},{10,... | collective-permute-start | bytes 1179656 | tf_op jit(solution)/shard_map/ppermute | solution.py:28
  329.8 8.3 %collective-permute-start.28 = (bf16[1152,384]{1,0:T(8,128)(2,1)S(1)}, bf16[1152,384]{1,0:T(8,128)(2,1)S(1)}, u32[]{:S(2)}, u32[]{:S(2)}) collective-permute-start(bf16[1152,384]{1,0:T(8,128)(2,1)S(1)} %convolution_convert_fusion), channel_id=1, source_target_pairs={{0,1},{1,0},{2,3},{3,2},{4,5},{5,4},{6,7},{7,6},{8,9},{9,8},{10,11... | collective-permute-start | bytes 2654216 | tf_op jit(solution)/shard_map/ppermute | solution.py:23
  336.5 11.3 %collective-permute-start.18 = (bf16[256,768]{1,0:T(8,128)(2,1)S(1)}, bf16[256,768]{1,0:T(8,128)(2,1)S(1)}, u32[]{:S(2)}, u32[]{:S(2)}) collective-permute-start(bf16[256,768]{1,0:T(8,128)(2,1)S(1)} %add_convert_fusion.2), channel_id=1, source_target_pairs={{0,2},{1,3},{2,0},{3,1},{4,6},{5,7},{6,4},{7,5},{8,10},{9,11},{10,... | collective-permute-start | bytes 1179656 | tf_op jit(solution)/shard_map/ppermute | solution.py:28
  341.9 25.5 %collective-permute-start.29 = (bf16[2,4,144,384]{3,2,1,0:T(8,128)(2,1)}, bf16[2,4,144,384]{3,2,1,0:T(8,128)(2,1)}, u32[]{:S(2)}, u32[]{:S(2)}) collective-permute-start(bf16[2,4,144,384]{3,2,1,0:T(8,128)(2,1)} %fusion.10), channel_id=1, source_target_pairs={{0,4},{4,0},{8,12},{12,8},{16,20},{20,16},{24,28},{28,24},{1,5},{5... | collective-permute-start | bytes 2654216 | tf_op jit(solution)/shard_map/ppermute | solution.py:562
  349.9 12.2 %collective-permute-start.21 = (bf16[1152,384]{1,0:T(8,128)(2,1)}, bf16[1152,384]{1,0:T(8,128)(2,1)}, u32[]{:S(2)}, u32[]{:S(2)}) collective-permute-start(bf16[1152,384]{1,0:T(8,128)(2,1)} %convolution_convert_fusion.2), channel_id=1, source_target_pairs={{0,1},{1,0},{2,3},{3,2},{4,5},{5,4},{6,7},{7,6},{8,9},{9,8},{10,11... | collective-permute-start | bytes 2654216 | tf_op jit(solution)/shard_map/ppermute | solution.py:23
  365.9 29.3 %collective-permute-start.22 = (bf16[1152,384]{1,0:T(8,128)(2,1)}, bf16[1152,384]{1,0:T(8,128)(2,1)}, u32[]{:S(2)}, u32[]{:S(2)}) collective-permute-start(bf16[1152,384]{1,0:T(8,128)(2,1)} %get-tuple-element.212), channel_id=1, source_target_pairs={{0,2},{1,3},{2,0},{3,1},{4,6},{5,7},{6,4},{7,5},{8,10},{9,11},{10,... | collective-permute-start | bytes 2654216 | tf_op jit(solution)/shard_map/ppermute | solution.py:28
  370.3 10.2 %collective-permute-start.30 = (bf16[2,144,384]{2,1,0:T(8,128)(2,1)S(1)}, bf16[2,144,384]{2,1,0:T(8,128)(2,1)S(1)}, u32[]{:S(2)}, u32[]{:S(2)}) collective-permute-start(bf16[2,144,384]{2,1,0:T(8,128)(2,1)S(1)} %get-tuple-element.183), channel_id=1, source_target_pairs={{0,8},{4,12},{8,16},{12,20},{16,24},{20,28},{24,0},{28,4},{1,9},{5... | collective-permute-start | bytes 663560 | tf_op jit(solution)/shard_map/ppermute | solution.py:575
  370.7 12.3 %collective-permute-start.32 = (bf16[2,144,384]{2,1,0:T(8,128)(2,1)S(1)}, bf16[2,144,384]{2,1,0:T(8,128)(2,1)S(1)}, u32[]{:S(2)}, u32[]{:S(2)}) collective-permute-start(bf16[2,144,384]{2,1,0:T(8,128)(2,1)S(1)} %get-tuple-element.184), channel_id=1, source_target_pairs={{0,24},{4,28},{8,0},{12,4},{16,8},{20,12},{24,16},{28,20},{1,25},{... | collective-permute-start | bytes 663560 | tf_op jit(solution)/shard_map/ppermute | solution.py:575
  374.4 19.1 %collective-permute-start.31 = (bf16[2,144,384]{2,1,0:T(8,128)(2,1)S(1)}, bf16[2,144,384]{2,1,0:T(8,128)(2,1)S(1)}, u32[]{:S(2)}, u32[]{:S(2)}) collective-permute-start(bf16[2,144,384]{2,1,0:T(8,128)(2,1)S(1)} %get-tuple-element.185), channel_id=1, source_target_pairs={{0,16},{4,20},{8,24},{12,28},{16,0},{20,4},{24,8},{28,12},{1,17},{... | collective-permute-start | bytes 663560 | tf_op jit(solution)/shard_map/ppermute | solution.py:575
  397.3 12.5 %collective-permute-start.23 = (bf16[4,160,384]{2,1,0:T(8,128)(2,1)S(1)}, bf16[4,160,384]{2,1,0:T(8,128)(2,1)S(1)}, u32[]{:S(2)}, u32[]{:S(2)}) collective-permute-start(bf16[4,160,384]{2,1,0:T(8,128)(2,1)S(1)} %fusion.21), channel_id=1, source_target_pairs={{0,4},{4,0},{8,12},{12,8},{16,20},{20,16},{24,28},{28,24},{1,5},{5... | collective-permute-start | bytes 1474568 | tf_op jit(solution)/shard_map/ppermute | solution.py:562
  410.1 8.2 %collective-permute-start.24 = (bf16[160,384]{1,0:T(8,128)(2,1)S(1)}, bf16[160,384]{1,0:T(8,128)(2,1)S(1)}, u32[]{:S(2)}, u32[]{:S(2)}) collective-permute-start(bf16[160,384]{1,0:T(8,128)(2,1)S(1)} %get-tuple-element.190), channel_id=1, source_target_pairs={{0,8},{4,12},{8,16},{12,20},{16,24},{20,28},{24,0},{28,4},{1,9},{5... | collective-permute-start | bytes 368648 | tf_op jit(solution)/shard_map/ppermute | solution.py:575
  410.1 8.1 %collective-permute-start.26 = (bf16[160,384]{1,0:T(8,128)(2,1)S(1)}, bf16[160,384]{1,0:T(8,128)(2,1)S(1)}, u32[]{:S(2)}, u32[]{:S(2)}) collective-permute-start(bf16[160,384]{1,0:T(8,128)(2,1)S(1)} %get-tuple-element.191), channel_id=1, source_target_pairs={{0,24},{4,28},{8,0},{12,4},{16,8},{20,12},{24,16},{28,20},{1,25},{... | collective-permute-start | bytes 368648 | tf_op jit(solution)/shard_map/ppermute | solution.py:575
  414.0 8.2 %collective-permute-start.25 = (bf16[160,384]{1,0:T(8,128)(2,1)S(1)}, bf16[160,384]{1,0:T(8,128)(2,1)S(1)}, u32[]{:S(2)}, u32[]{:S(2)}) collective-permute-start(bf16[160,384]{1,0:T(8,128)(2,1)S(1)} %get-tuple-element.192), channel_id=1, source_target_pairs={{0,16},{4,20},{8,24},{12,28},{16,0},{20,4},{24,8},{28,12},{1,17},{... | collective-permute-start | bytes 368648 | tf_op jit(solution)/shard_map/ppermute | solution.py:575
  (123 other events, 749.3 us)
Sparse Core Ops, SparseCore 0:
  11.6 76.5 all-gather.3
  91.0 85.5 all-gather.5
  204.3 31.3 reduce-scatter.3
  260.3 101.2 reduce-scatter.7
  364.0 40.1 reduce-scatter.5
